TPU v7x, 32 devices: a whole 2x2x4 slice. The times are simulated.
32 devices in a mesh: ctx: 8 (over z, x), head: 4 (over y, core).
Axes of the slice: x: 2, y: 2, z: 4, core: 2. Of those that a mesh axis runs over, the one named last changes fastest.
Arguments:
- hidden_in: bfloat16 [1024, 4096], P('ctx'), may hold values from -30 to 30
- query_weight: bfloat16 [4096, 8192], P(None, 'head'), may hold values from -0.1875 to 0.1875
- shared_weight: bfloat16 [4096, 512], P(None, 'head'), may hold values from -0.09375 to 0.09375
- out_weight: bfloat16 [8192, 4096], P('head'), may hold values from -1 to 1
- residual: bfloat16 [1024, 4096], P(('ctx', 'head')), may hold values from -20 to 20
- norm_gain: float32 [4096], replicated, may hold values from 0.25 to 1.75
Outputs:
- residual_out: bfloat16 [1024, 4096], P(('ctx', 'head'))
- normed: bfloat16 [1024, 4096], P('ctx')
All inputs are finite; a program needn't handle non-finite values.
Results may differ from a plain program's by a relative error of at most 0.0065.
The roundings to bfloat16 on the way count: a program that leaves them out, or rounds other values in their place, can miss the bound.
Values may be sent and summed in bfloat16 or wider, within the bound.
No kernel may reach another device: no remote copies, remote signals or barrier semaphores. Data moves between devices by JAX's collectives and lax.ppermute only.
A program may use at most 128 MiB of HBM per device.

v0:
```python
import jax
import jax.numpy as jnp
from jax import lax
from jax.sharding import PartitionSpec as P

HD = 128
W1 = 512
W2 = 32


def from_behind(value, axis, steps):
    count = lax.axis_size(axis)
    initial, last = (max(0, -steps), min(count, count - steps))
    return lax.ppermute(value, axis, [(source, source + steps) for source in range(initial, last)])


def window_mask(first, rows, spread, reach):
    query_pos = first + jnp.arange(rows, dtype=jnp.int32)[:, None, None]
    offset = jnp.arange(spread, dtype=jnp.int32)[None, :, None]
    column = jnp.arange(rows + reach, dtype=jnp.int32)[None, None, :]
    key_pos = first - reach + column
    allowed = (
        (key_pos <= query_pos)
        & (key_pos > query_pos - reach)
        & (key_pos >= 0)
        & (query_pos - offset >= 0)
    )
    return allowed


def attend_block(query, key_one, value_one, key_two, value_two, valid):
    rows = query.shape[0]
    width = query.shape[1]
    spread = key_two.shape[1]
    mixed = (query[:, None, :].astype(jnp.float32) * key_two.astype(jnp.float32)).astype(
        jnp.bfloat16
    )
    scores = lax.dot_general(
        mixed.reshape(rows * spread, width),
        key_one,
        (((1,), (1,)), ((), ())),
        preferred_element_type=jnp.float32,
    )
    scores = scores.reshape(rows, spread, -1) * width ** (-0.5)
    scores = jnp.where(valid, scores, -jnp.inf)
    peak = jnp.max(scores, axis=(1, 2), keepdims=True)
    weights = jnp.exp(scores - peak)
    total = jnp.sum(weights, axis=(1, 2))
    blended = jnp.dot(
        weights.astype(jnp.bfloat16).reshape(rows * spread, -1),
        value_one,
        preferred_element_type=jnp.float32,
    )
    blended = blended.reshape(rows, spread, width)
    return jnp.sum(value_two.astype(jnp.float32) * blended, axis=1) / total[:, None]


def body(hidden_in, query_weight, shared_weight, out_weight, residual, norm_gain):
    tokens = hidden_in.shape[0]
    queries = jnp.dot(hidden_in, query_weight, preferred_element_type=jnp.float32).astype(
        jnp.bfloat16
    )
    local_part = jnp.dot(hidden_in, shared_weight, preferred_element_type=jnp.float32).astype(
        jnp.bfloat16
    )
    shared = lax.all_gather(local_part, "head", axis=1, tiled=True)
    first_pair = shared[:, : 2 * HD]
    second_pair = shared[:, 2 * HD :]
    reach = (W1 + tokens - 1) // tokens
    earlier, rim = from_behind((first_pair, second_pair[tokens - W2 :]), "ctx", 1)
    pieces = [earlier]
    for distance in range(2, reach + 1):
        pieces.append(from_behind(first_pair, "ctx", distance))
    extended_one = jnp.concatenate(pieces[::-1] + [first_pair], 0)
    extended_two = jnp.concatenate([rim, second_pair], 0)
    heads = queries.shape[1] // HD
    block = min(128, tokens)
    anchor = lax.axis_index("ctx") * tokens
    heads_q = queries.reshape(tokens, heads, HD).transpose(1, 0, 2)
    key_one = extended_one[:, :HD]
    value_one = extended_one[:, HD:]
    near = jnp.stack([extended_two[W2 - offset : W2 - offset + block] for offset in range(W2)], 1)
    key_two = near[:, :, :HD]
    value_two = near[:, :, HD:]
    valid = window_mask(anchor + 0, block, W2, W1)
    results = lax.map(
        lambda head: attend_block(head, key_one, value_one, key_two, value_two, valid), heads_q
    )
    attention = results.transpose(1, 0, 2).reshape(tokens, heads * HD).astype(jnp.bfloat16)
    summed = lax.psum_scatter(
        jnp.dot(attention, out_weight, preferred_element_type=jnp.float32),
        "head",
        scatter_dimension=0,
        tiled=True,
    )
    residual_out = (residual.astype(jnp.float32) + summed).astype(jnp.bfloat16)
    values = residual_out.astype(jnp.float32)
    scale = lax.rsqrt(jnp.mean(values * values, axis=1, keepdims=True) + 1e-05)
    normed_local = (values * scale * norm_gain).astype(jnp.bfloat16)
    normed = lax.all_gather(normed_local, "head", axis=0, tiled=True)
    return (residual_out, normed)


def solution(mesh):
    in_specs = (
        P("ctx", None),
        P(None, "head"),
        P(None, "head"),
        P("head", None),
        P(("ctx", "head"), None),
        P(),
    )
    out_specs = (P(("ctx", "head"), None), P("ctx", None))
    return jax.shard_map(body, mesh=mesh, in_specs=in_specs, out_specs=out_specs, check_vma=False)
```

profile of v0, /device:TPU:11, one launch (start us, length us, event | category | flops | bytes accessed | tf_op | source)
XLA Modules:
  0.0 319.2 jit_solution(902550834542701428)
XLA Ops:
  8.4 1.6 convolution_convert_fusion.1
  10.0 6.0 %all_gather.6 = bf16[128,512]{1,0:T(8,128)(2,1)S(1)} all-gather(bf16[128,128]{1,0:T(8,128)(2,1)S(1)} %convolution_convert_fusion.1), channel_id=1, replica_groups=mesh['ctx'=8,'head'=4] {'head'}, dimensions={1}, use_global_device_ids=true | all-gather | bytes 163840 | tf_op jit(solution)/shard_map/all_gather | solution.py:66
  16.0 4.8 %collective-permute-start.1 = (bf16[128,256]{1,0:T(8,128)(2,1)S(1)}, bf16[128,256]{1,0:T(8,128)(2,1)}, u32[]{:S(2)}, u32[]{:S(2)}) collective-permute-start(bf16[128,256]{1,0:T(8,128)(2,1)S(1)} %slice.217), channel_id=1, source_target_pairs={{0,16},{4,20},{8,24},{12,28},{1,17},{5,21},{9,25},{13,29},{2,18},{... | collective-permute-start | bytes 196616 | tf_op jit(solution)/shard_map/ppermute | solution.py:14
  20.8 1.9 collective-permute-start.2
  22.8 1.9 collective-permute-start.3
  24.7 1.9 collective-permute-start.4
  26.6 1.9 collective-permute-start
  28.6 8.9 %fusion.17 = bf16[16,16,8,128]{3,2,1,0:T(8,128)(2,1)} fusion(bf16[128,4096]{1,0:T(8,128)(2,1)S(1)} %copy-done, bf16[4096,2048]{1,0:T(8,128)(2,1)} %param.9), kind=kOutput, calls=%fused_computation.21 | convolution fusion | flops 2147745792 | bytes 18350080 | tf_op jit(solution)/shard_map/dot_general | solution.py:60
  37.7 2.0 copy.16
  43.1 1.9 fusion.82
  45.1 203.8 %while.11 = (s32[]{:T(128)}, bf16[16,128,128]{1,2,0:T(8,128)(2,1)}, bf16[128,32,128]{2,0,1:T(8,128)(2,1)}, bf16[16,128,128]{2,1,0:T(8,128)(2,1)}, bf16[128,32,12...) while((s32[]{:T(128)}, bf16[16,128,128]{1,2,0:T(8,128)(2,1)}, ...), condition=%wide.region_4.5_spmd.clone, body=%wide.region_0.4_spmd.clone.sunk | while | flops 1382055680 | bytes 38796420 | solution.py:86
  45.8 3.8 %fusion.97 = (f32[128]{0:T(128)S(1)}, f32[128,32,640]{2,0,1:T(8,128)S(1)}) fusion(pred[128,32]{0,1:T(8,128)(4,1)S(1)} %get-tuple-element.183, pred[128,640]{1,0:T(8,128)(4,1)S(1)} %get-tuple-element.184, bf16[640,128]{1,0:T(8,128)(2,1)S(1)} %get-tuple-element.181, bf16[128,32,128]{2,0,1:T(8,128)(2,1)} %get-tuple-element.180, ...), kind=kOutput, calls=%fused_computation.5.clone.1 | convolution fusion | flops 683147136 | bytes 11850240 | tf_op jit(solution)/shard_map/while/body/eval_jaxpr/dot_general | solution.py:38
  49.6 3.5 %fusion.98 = f32[128]{0:T(128)S(1)} fusion(f32[128,32,640]{2,0,1:T(8,128)S(1)} %get-tuple-element.154, f32[128]{0:T(128)S(1)} %get-tuple-element.155, pred[128,32]{0,1:T(8,128)(4,1)S(1)} %get-tuple-element.183, pred[128,640]{1,0:T(8,128)(4,1)S(1)} %get-tuple-element.184), kind=kLoop, calls=%fused_computation.3.clone.1 | loop fusion | flops 13107072 | bytes 10572800 | tf_op jit(solution)/shard_map/while/body/eval_jaxpr/reduce_sum | solution.py:48
  53.2 3.8 %multiply_reduce_fusion.2 = f32[128,128]{1,0:T(8,128)S(1)} fusion(bf16[128,32,128]{2,0,1:T(8,128)(2,1)S(1)} %copy-done.2, f32[128,32,640]{2,0,1:T(8,128)S(1)} %get-tuple-element.154, f32[128]{0:T(128)S(1)} %get-tuple-element.155, pred[128,32]{0,1:T(8,128)(4,1)S(1)} %get-tuple-element.183, pred[128,640]{1,0:T(8,128)(4,1)S(1)} %get-tuple-element.184, ...), kind=kOutput, calls=%fused_computation.9.clone.1 | convolution fusion | flops 685752320 | bytes 11850240 | tf_op jit(solution)/shard_map/while/body/eval_jaxpr/dot_general | solution.py:49
  58.6 3.8 %fusion.97 = (f32[128]{0:T(128)S(1)}, f32[128,32,640]{2,0,1:T(8,128)S(1)}) fusion(pred[128,32]{0,1:T(8,128)(4,1)S(1)} %get-tuple-element.183, pred[128,640]{1,0:T(8,128)(4,1)S(1)} %get-tuple-element.184, bf16[640,128]{1,0:T(8,128)(2,1)S(1)} %get-tuple-element.181, bf16[128,32,128]{2,0,1:T(8,128)(2,1)} %get-tuple-element.180, ...), kind=kOutput, calls=%fused_computation.5.clone.1 | convolution fusion | flops 683147136 | bytes 11850240 | tf_op jit(solution)/shard_map/while/body/eval_jaxpr/dot_general | solution.py:38
  62.4 3.5 %fusion.98 = f32[128]{0:T(128)S(1)} fusion(f32[128,32,640]{2,0,1:T(8,128)S(1)} %get-tuple-element.154, f32[128]{0:T(128)S(1)} %get-tuple-element.155, pred[128,32]{0,1:T(8,128)(4,1)S(1)} %get-tuple-element.183, pred[128,640]{1,0:T(8,128)(4,1)S(1)} %get-tuple-element.184), kind=kLoop, calls=%fused_computation.3.clone.1 | loop fusion | flops 13107072 | bytes 10572800 | tf_op jit(solution)/shard_map/while/body/eval_jaxpr/reduce_sum | solution.py:48
  65.9 3.8 %multiply_reduce_fusion.2 = f32[128,128]{1,0:T(8,128)S(1)} fusion(bf16[128,32,128]{2,0,1:T(8,128)(2,1)S(1)} %copy-done.2, f32[128,32,640]{2,0,1:T(8,128)S(1)} %get-tuple-element.154, f32[128]{0:T(128)S(1)} %get-tuple-element.155, pred[128,32]{0,1:T(8,128)(4,1)S(1)} %get-tuple-element.183, pred[128,640]{1,0:T(8,128)(4,1)S(1)} %get-tuple-element.184, ...), kind=kOutput, calls=%fused_computation.9.clone.1 | convolution fusion | flops 685752320 | bytes 11850240 | tf_op jit(solution)/shard_map/while/body/eval_jaxpr/dot_general | solution.py:49
  71.3 3.8 %fusion.97 = (f32[128]{0:T(128)S(1)}, f32[128,32,640]{2,0,1:T(8,128)S(1)}) fusion(pred[128,32]{0,1:T(8,128)(4,1)S(1)} %get-tuple-element.183, pred[128,640]{1,0:T(8,128)(4,1)S(1)} %get-tuple-element.184, bf16[640,128]{1,0:T(8,128)(2,1)S(1)} %get-tuple-element.181, bf16[128,32,128]{2,0,1:T(8,128)(2,1)} %get-tuple-element.180, ...), kind=kOutput, calls=%fused_computation.5.clone.1 | convolution fusion | flops 683147136 | bytes 11850240 | tf_op jit(solution)/shard_map/while/body/eval_jaxpr/dot_general | solution.py:38
  75.1 3.5 %fusion.98 = f32[128]{0:T(128)S(1)} fusion(f32[128,32,640]{2,0,1:T(8,128)S(1)} %get-tuple-element.154, f32[128]{0:T(128)S(1)} %get-tuple-element.155, pred[128,32]{0,1:T(8,128)(4,1)S(1)} %get-tuple-element.183, pred[128,640]{1,0:T(8,128)(4,1)S(1)} %get-tuple-element.184), kind=kLoop, calls=%fused_computation.3.clone.1 | loop fusion | flops 13107072 | bytes 10572800 | tf_op jit(solution)/shard_map/while/body/eval_jaxpr/reduce_sum | solution.py:48
  78.7 3.8 %multiply_reduce_fusion.2 = f32[128,128]{1,0:T(8,128)S(1)} fusion(bf16[128,32,128]{2,0,1:T(8,128)(2,1)S(1)} %copy-done.2, f32[128,32,640]{2,0,1:T(8,128)S(1)} %get-tuple-element.154, f32[128]{0:T(128)S(1)} %get-tuple-element.155, pred[128,32]{0,1:T(8,128)(4,1)S(1)} %get-tuple-element.183, pred[128,640]{1,0:T(8,128)(4,1)S(1)} %get-tuple-element.184, ...), kind=kOutput, calls=%fused_computation.9.clone.1 | convolution fusion | flops 685752320 | bytes 11850240 | tf_op jit(solution)/shard_map/while/body/eval_jaxpr/dot_general | solution.py:49
  84.0 3.8 %fusion.97 = (f32[128]{0:T(128)S(1)}, f32[128,32,640]{2,0,1:T(8,128)S(1)}) fusion(pred[128,32]{0,1:T(8,128)(4,1)S(1)} %get-tuple-element.183, pred[128,640]{1,0:T(8,128)(4,1)S(1)} %get-tuple-element.184, bf16[640,128]{1,0:T(8,128)(2,1)S(1)} %get-tuple-element.181, bf16[128,32,128]{2,0,1:T(8,128)(2,1)} %get-tuple-element.180, ...), kind=kOutput, calls=%fused_computation.5.clone.1 | convolution fusion | flops 683147136 | bytes 11850240 | tf_op jit(solution)/shard_map/while/body/eval_jaxpr/dot_general | solution.py:38
  87.9 3.5 %fusion.98 = f32[128]{0:T(128)S(1)} fusion(f32[128,32,640]{2,0,1:T(8,128)S(1)} %get-tuple-element.154, f32[128]{0:T(128)S(1)} %get-tuple-element.155, pred[128,32]{0,1:T(8,128)(4,1)S(1)} %get-tuple-element.183, pred[128,640]{1,0:T(8,128)(4,1)S(1)} %get-tuple-element.184), kind=kLoop, calls=%fused_computation.3.clone.1 | loop fusion | flops 13107072 | bytes 10572800 | tf_op jit(solution)/shard_map/while/body/eval_jaxpr/reduce_sum | solution.py:48
  91.4 3.8 %multiply_reduce_fusion.2 = f32[128,128]{1,0:T(8,128)S(1)} fusion(bf16[128,32,128]{2,0,1:T(8,128)(2,1)S(1)} %copy-done.2, f32[128,32,640]{2,0,1:T(8,128)S(1)} %get-tuple-element.154, f32[128]{0:T(128)S(1)} %get-tuple-element.155, pred[128,32]{0,1:T(8,128)(4,1)S(1)} %get-tuple-element.183, pred[128,640]{1,0:T(8,128)(4,1)S(1)} %get-tuple-element.184, ...), kind=kOutput, calls=%fused_computation.9.clone.1 | convolution fusion | flops 685752320 | bytes 11850240 | tf_op jit(solution)/shard_map/while/body/eval_jaxpr/dot_general | solution.py:49
  96.8 3.8 %fusion.97 = (f32[128]{0:T(128)S(1)}, f32[128,32,640]{2,0,1:T(8,128)S(1)}) fusion(pred[128,32]{0,1:T(8,128)(4,1)S(1)} %get-tuple-element.183, pred[128,640]{1,0:T(8,128)(4,1)S(1)} %get-tuple-element.184, bf16[640,128]{1,0:T(8,128)(2,1)S(1)} %get-tuple-element.181, bf16[128,32,128]{2,0,1:T(8,128)(2,1)} %get-tuple-element.180, ...), kind=kOutput, calls=%fused_computation.5.clone.1 | convolution fusion | flops 683147136 | bytes 11850240 | tf_op jit(solution)/shard_map/while/body/eval_jaxpr/dot_general | solution.py:38
  100.6 3.5 %fusion.98 = f32[128]{0:T(128)S(1)} fusion(f32[128,32,640]{2,0,1:T(8,128)S(1)} %get-tuple-element.154, f32[128]{0:T(128)S(1)} %get-tuple-element.155, pred[128,32]{0,1:T(8,128)(4,1)S(1)} %get-tuple-element.183, pred[128,640]{1,0:T(8,128)(4,1)S(1)} %get-tuple-element.184), kind=kLoop, calls=%fused_computation.3.clone.1 | loop fusion | flops 13107072 | bytes 10572800 | tf_op jit(solution)/shard_map/while/body/eval_jaxpr/reduce_sum | solution.py:48
  104.1 3.8 %multiply_reduce_fusion.2 = f32[128,128]{1,0:T(8,128)S(1)} fusion(bf16[128,32,128]{2,0,1:T(8,128)(2,1)S(1)} %copy-done.2, f32[128,32,640]{2,0,1:T(8,128)S(1)} %get-tuple-element.154, f32[128]{0:T(128)S(1)} %get-tuple-element.155, pred[128,32]{0,1:T(8,128)(4,1)S(1)} %get-tuple-element.183, pred[128,640]{1,0:T(8,128)(4,1)S(1)} %get-tuple-element.184, ...), kind=kOutput, calls=%fused_computation.9.clone.1 | convolution fusion | flops 685752320 | bytes 11850240 | tf_op jit(solution)/shard_map/while/body/eval_jaxpr/dot_general | solution.py:49
  109.5 3.8 %fusion.97 = (f32[128]{0:T(128)S(1)}, f32[128,32,640]{2,0,1:T(8,128)S(1)}) fusion(pred[128,32]{0,1:T(8,128)(4,1)S(1)} %get-tuple-element.183, pred[128,640]{1,0:T(8,128)(4,1)S(1)} %get-tuple-element.184, bf16[640,128]{1,0:T(8,128)(2,1)S(1)} %get-tuple-element.181, bf16[128,32,128]{2,0,1:T(8,128)(2,1)} %get-tuple-element.180, ...), kind=kOutput, calls=%fused_computation.5.clone.1 | convolution fusion | flops 683147136 | bytes 11850240 | tf_op jit(solution)/shard_map/while/body/eval_jaxpr/dot_general | solution.py:38
  113.3 3.5 %fusion.98 = f32[128]{0:T(128)S(1)} fusion(f32[128,32,640]{2,0,1:T(8,128)S(1)} %get-tuple-element.154, f32[128]{0:T(128)S(1)} %get-tuple-element.155, pred[128,32]{0,1:T(8,128)(4,1)S(1)} %get-tuple-element.183, pred[128,640]{1,0:T(8,128)(4,1)S(1)} %get-tuple-element.184), kind=kLoop, calls=%fused_computation.3.clone.1 | loop fusion | flops 13107072 | bytes 10572800 | tf_op jit(solution)/shard_map/while/body/eval_jaxpr/reduce_sum | solution.py:48
  116.9 3.8 %multiply_reduce_fusion.2 = f32[128,128]{1,0:T(8,128)S(1)} fusion(bf16[128,32,128]{2,0,1:T(8,128)(2,1)S(1)} %copy-done.2, f32[128,32,640]{2,0,1:T(8,128)S(1)} %get-tuple-element.154, f32[128]{0:T(128)S(1)} %get-tuple-element.155, pred[128,32]{0,1:T(8,128)(4,1)S(1)} %get-tuple-element.183, pred[128,640]{1,0:T(8,128)(4,1)S(1)} %get-tuple-element.184, ...), kind=kOutput, calls=%fused_computation.9.clone.1 | convolution fusion | flops 685752320 | bytes 11850240 | tf_op jit(solution)/shard_map/while/body/eval_jaxpr/dot_general | solution.py:49
  122.2 3.8 %fusion.97 = (f32[128]{0:T(128)S(1)}, f32[128,32,640]{2,0,1:T(8,128)S(1)}) fusion(pred[128,32]{0,1:T(8,128)(4,1)S(1)} %get-tuple-element.183, pred[128,640]{1,0:T(8,128)(4,1)S(1)} %get-tuple-element.184, bf16[640,128]{1,0:T(8,128)(2,1)S(1)} %get-tuple-element.181, bf16[128,32,128]{2,0,1:T(8,128)(2,1)} %get-tuple-element.180, ...), kind=kOutput, calls=%fused_computation.5.clone.1 | convolution fusion | flops 683147136 | bytes 11850240 | tf_op jit(solution)/shard_map/while/body/eval_jaxpr/dot_general | solution.py:38
  126.1 3.5 %fusion.98 = f32[128]{0:T(128)S(1)} fusion(f32[128,32,640]{2,0,1:T(8,128)S(1)} %get-tuple-element.154, f32[128]{0:T(128)S(1)} %get-tuple-element.155, pred[128,32]{0,1:T(8,128)(4,1)S(1)} %get-tuple-element.183, pred[128,640]{1,0:T(8,128)(4,1)S(1)} %get-tuple-element.184), kind=kLoop, calls=%fused_computation.3.clone.1 | loop fusion | flops 13107072 | bytes 10572800 | tf_op jit(solution)/shard_map/while/body/eval_jaxpr/reduce_sum | solution.py:48
  129.6 3.8 %multiply_reduce_fusion.2 = f32[128,128]{1,0:T(8,128)S(1)} fusion(bf16[128,32,128]{2,0,1:T(8,128)(2,1)S(1)} %copy-done.2, f32[128,32,640]{2,0,1:T(8,128)S(1)} %get-tuple-element.154, f32[128]{0:T(128)S(1)} %get-tuple-element.155, pred[128,32]{0,1:T(8,128)(4,1)S(1)} %get-tuple-element.183, pred[128,640]{1,0:T(8,128)(4,1)S(1)} %get-tuple-element.184, ...), kind=kOutput, calls=%fused_computation.9.clone.1 | convolution fusion | flops 685752320 | bytes 11850240 | tf_op jit(solution)/shard_map/while/body/eval_jaxpr/dot_general | solution.py:49
  135.0 3.8 %fusion.97 = (f32[128]{0:T(128)S(1)}, f32[128,32,640]{2,0,1:T(8,128)S(1)}) fusion(pred[128,32]{0,1:T(8,128)(4,1)S(1)} %get-tuple-element.183, pred[128,640]{1,0:T(8,128)(4,1)S(1)} %get-tuple-element.184, bf16[640,128]{1,0:T(8,128)(2,1)S(1)} %get-tuple-element.181, bf16[128,32,128]{2,0,1:T(8,128)(2,1)} %get-tuple-element.180, ...), kind=kOutput, calls=%fused_computation.5.clone.1 | convolution fusion | flops 683147136 | bytes 11850240 | tf_op jit(solution)/shard_map/while/body/eval_jaxpr/dot_general | solution.py:38
  138.8 3.5 %fusion.98 = f32[128]{0:T(128)S(1)} fusion(f32[128,32,640]{2,0,1:T(8,128)S(1)} %get-tuple-element.154, f32[128]{0:T(128)S(1)} %get-tuple-element.155, pred[128,32]{0,1:T(8,128)(4,1)S(1)} %get-tuple-element.183, pred[128,640]{1,0:T(8,128)(4,1)S(1)} %get-tuple-element.184), kind=kLoop, calls=%fused_computation.3.clone.1 | loop fusion | flops 13107072 | bytes 10572800 | tf_op jit(solution)/shard_map/while/body/eval_jaxpr/reduce_sum | solution.py:48
  142.3 3.8 %multiply_reduce_fusion.2 = f32[128,128]{1,0:T(8,128)S(1)} fusion(bf16[128,32,128]{2,0,1:T(8,128)(2,1)S(1)} %copy-done.2, f32[128,32,640]{2,0,1:T(8,128)S(1)} %get-tuple-element.154, f32[128]{0:T(128)S(1)} %get-tuple-element.155, pred[128,32]{0,1:T(8,128)(4,1)S(1)} %get-tuple-element.183, pred[128,640]{1,0:T(8,128)(4,1)S(1)} %get-tuple-element.184, ...), kind=kOutput, calls=%fused_computation.9.clone.1 | convolution fusion | flops 685752320 | bytes 11850240 | tf_op jit(solution)/shard_map/while/body/eval_jaxpr/dot_general | solution.py:49
  147.7 3.8 %fusion.97 = (f32[128]{0:T(128)S(1)}, f32[128,32,640]{2,0,1:T(8,128)S(1)}) fusion(pred[128,32]{0,1:T(8,128)(4,1)S(1)} %get-tuple-element.183, pred[128,640]{1,0:T(8,128)(4,1)S(1)} %get-tuple-element.184, bf16[640,128]{1,0:T(8,128)(2,1)S(1)} %get-tuple-element.181, bf16[128,32,128]{2,0,1:T(8,128)(2,1)} %get-tuple-element.180, ...), kind=kOutput, calls=%fused_computation.5.clone.1 | convolution fusion | flops 683147136 | bytes 11850240 | tf_op jit(solution)/shard_map/while/body/eval_jaxpr/dot_general | solution.py:38
  151.5 3.5 %fusion.98 = f32[128]{0:T(128)S(1)} fusion(f32[128,32,640]{2,0,1:T(8,128)S(1)} %get-tuple-element.154, f32[128]{0:T(128)S(1)} %get-tuple-element.155, pred[128,32]{0,1:T(8,128)(4,1)S(1)} %get-tuple-element.183, pred[128,640]{1,0:T(8,128)(4,1)S(1)} %get-tuple-element.184), kind=kLoop, calls=%fused_computation.3.clone.1 | loop fusion | flops 13107072 | bytes 10572800 | tf_op jit(solution)/shard_map/while/body/eval_jaxpr/reduce_sum | solution.py:48
  155.1 3.8 %multiply_reduce_fusion.2 = f32[128,128]{1,0:T(8,128)S(1)} fusion(bf16[128,32,128]{2,0,1:T(8,128)(2,1)S(1)} %copy-done.2, f32[128,32,640]{2,0,1:T(8,128)S(1)} %get-tuple-element.154, f32[128]{0:T(128)S(1)} %get-tuple-element.155, pred[128,32]{0,1:T(8,128)(4,1)S(1)} %get-tuple-element.183, pred[128,640]{1,0:T(8,128)(4,1)S(1)} %get-tuple-element.184, ...), kind=kOutput, calls=%fused_computation.9.clone.1 | convolution fusion | flops 685752320 | bytes 11850240 | tf_op jit(solution)/shard_map/while/body/eval_jaxpr/dot_general | solution.py:49
  160.4 3.8 %fusion.97 = (f32[128]{0:T(128)S(1)}, f32[128,32,640]{2,0,1:T(8,128)S(1)}) fusion(pred[128,32]{0,1:T(8,128)(4,1)S(1)} %get-tuple-element.183, pred[128,640]{1,0:T(8,128)(4,1)S(1)} %get-tuple-element.184, bf16[640,128]{1,0:T(8,128)(2,1)S(1)} %get-tuple-element.181, bf16[128,32,128]{2,0,1:T(8,128)(2,1)} %get-tuple-element.180, ...), kind=kOutput, calls=%fused_computation.5.clone.1 | convolution fusion | flops 683147136 | bytes 11850240 | tf_op jit(solution)/shard_map/while/body/eval_jaxpr/dot_general | solution.py:38
  164.3 3.5 %fusion.98 = f32[128]{0:T(128)S(1)} fusion(f32[128,32,640]{2,0,1:T(8,128)S(1)} %get-tuple-element.154, f32[128]{0:T(128)S(1)} %get-tuple-element.155, pred[128,32]{0,1:T(8,128)(4,1)S(1)} %get-tuple-element.183, pred[128,640]{1,0:T(8,128)(4,1)S(1)} %get-tuple-element.184), kind=kLoop, calls=%fused_computation.3.clone.1 | loop fusion | flops 13107072 | bytes 10572800 | tf_op jit(solution)/shard_map/while/body/eval_jaxpr/reduce_sum | solution.py:48
  167.8 3.8 %multiply_reduce_fusion.2 = f32[128,128]{1,0:T(8,128)S(1)} fusion(bf16[128,32,128]{2,0,1:T(8,128)(2,1)S(1)} %copy-done.2, f32[128,32,640]{2,0,1:T(8,128)S(1)} %get-tuple-element.154, f32[128]{0:T(128)S(1)} %get-tuple-element.155, pred[128,32]{0,1:T(8,128)(4,1)S(1)} %get-tuple-element.183, pred[128,640]{1,0:T(8,128)(4,1)S(1)} %get-tuple-element.184, ...), kind=kOutput, calls=%fused_computation.9.clone.1 | convolution fusion | flops 685752320 | bytes 11850240 | tf_op jit(solution)/shard_map/while/body/eval_jaxpr/dot_general | solution.py:49
  173.2 3.8 %fusion.97 = (f32[128]{0:T(128)S(1)}, f32[128,32,640]{2,0,1:T(8,128)S(1)}) fusion(pred[128,32]{0,1:T(8,128)(4,1)S(1)} %get-tuple-element.183, pred[128,640]{1,0:T(8,128)(4,1)S(1)} %get-tuple-element.184, bf16[640,128]{1,0:T(8,128)(2,1)S(1)} %get-tuple-element.181, bf16[128,32,128]{2,0,1:T(8,128)(2,1)} %get-tuple-element.180, ...), kind=kOutput, calls=%fused_computation.5.clone.1 | convolution fusion | flops 683147136 | bytes 11850240 | tf_op jit(solution)/shard_map/while/body/eval_jaxpr/dot_general | solution.py:38
  177.0 3.5 %fusion.98 = f32[128]{0:T(128)S(1)} fusion(f32[128,32,640]{2,0,1:T(8,128)S(1)} %get-tuple-element.154, f32[128]{0:T(128)S(1)} %get-tuple-element.155, pred[128,32]{0,1:T(8,128)(4,1)S(1)} %get-tuple-element.183, pred[128,640]{1,0:T(8,128)(4,1)S(1)} %get-tuple-element.184), kind=kLoop, calls=%fused_computation.3.clone.1 | loop fusion | flops 13107072 | bytes 10572800 | tf_op jit(solution)/shard_map/while/body/eval_jaxpr/reduce_sum | solution.py:48
  180.5 3.8 %multiply_reduce_fusion.2 = f32[128,128]{1,0:T(8,128)S(1)} fusion(bf16[128,32,128]{2,0,1:T(8,128)(2,1)S(1)} %copy-done.2, f32[128,32,640]{2,0,1:T(8,128)S(1)} %get-tuple-element.154, f32[128]{0:T(128)S(1)} %get-tuple-element.155, pred[128,32]{0,1:T(8,128)(4,1)S(1)} %get-tuple-element.183, pred[128,640]{1,0:T(8,128)(4,1)S(1)} %get-tuple-element.184, ...), kind=kOutput, calls=%fused_computation.9.clone.1 | convolution fusion | flops 685752320 | bytes 11850240 | tf_op jit(solution)/shard_map/while/body/eval_jaxpr/dot_general | solution.py:49
  185.9 3.8 %fusion.97 = (f32[128]{0:T(128)S(1)}, f32[128,32,640]{2,0,1:T(8,128)S(1)}) fusion(pred[128,32]{0,1:T(8,128)(4,1)S(1)} %get-tuple-element.183, pred[128,640]{1,0:T(8,128)(4,1)S(1)} %get-tuple-element.184, bf16[640,128]{1,0:T(8,128)(2,1)S(1)} %get-tuple-element.181, bf16[128,32,128]{2,0,1:T(8,128)(2,1)} %get-tuple-element.180, ...), kind=kOutput, calls=%fused_computation.5.clone.1 | convolution fusion | flops 683147136 | bytes 11850240 | tf_op jit(solution)/shard_map/while/body/eval_jaxpr/dot_general | solution.py:38
  189.7 3.5 %fusion.98 = f32[128]{0:T(128)S(1)} fusion(f32[128,32,640]{2,0,1:T(8,128)S(1)} %get-tuple-element.154, f32[128]{0:T(128)S(1)} %get-tuple-element.155, pred[128,32]{0,1:T(8,128)(4,1)S(1)} %get-tuple-element.183, pred[128,640]{1,0:T(8,128)(4,1)S(1)} %get-tuple-element.184), kind=kLoop, calls=%fused_computation.3.clone.1 | loop fusion | flops 13107072 | bytes 10572800 | tf_op jit(solution)/shard_map/while/body/eval_jaxpr/reduce_sum | solution.py:48
  193.3 3.8 %multiply_reduce_fusion.2 = f32[128,128]{1,0:T(8,128)S(1)} fusion(bf16[128,32,128]{2,0,1:T(8,128)(2,1)S(1)} %copy-done.2, f32[128,32,640]{2,0,1:T(8,128)S(1)} %get-tuple-element.154, f32[128]{0:T(128)S(1)} %get-tuple-element.155, pred[128,32]{0,1:T(8,128)(4,1)S(1)} %get-tuple-element.183, pred[128,640]{1,0:T(8,128)(4,1)S(1)} %get-tuple-element.184, ...), kind=kOutput, calls=%fused_computation.9.clone.1 | convolution fusion | flops 685752320 | bytes 11850240 | tf_op jit(solution)/shard_map/while/body/eval_jaxpr/dot_general | solution.py:49
  198.7 3.8 %fusion.97 = (f32[128]{0:T(128)S(1)}, f32[128,32,640]{2,0,1:T(8,128)S(1)}) fusion(pred[128,32]{0,1:T(8,128)(4,1)S(1)} %get-tuple-element.183, pred[128,640]{1,0:T(8,128)(4,1)S(1)} %get-tuple-element.184, bf16[640,128]{1,0:T(8,128)(2,1)S(1)} %get-tuple-element.181, bf16[128,32,128]{2,0,1:T(8,128)(2,1)} %get-tuple-element.180, ...), kind=kOutput, calls=%fused_computation.5.clone.1 | convolution fusion | flops 683147136 | bytes 11850240 | tf_op jit(solution)/shard_map/while/body/eval_jaxpr/dot_general | solution.py:38
  202.5 3.5 %fusion.98 = f32[128]{0:T(128)S(1)} fusion(f32[128,32,640]{2,0,1:T(8,128)S(1)} %get-tuple-element.154, f32[128]{0:T(128)S(1)} %get-tuple-element.155, pred[128,32]{0,1:T(8,128)(4,1)S(1)} %get-tuple-element.183, pred[128,640]{1,0:T(8,128)(4,1)S(1)} %get-tuple-element.184), kind=kLoop, calls=%fused_computation.3.clone.1 | loop fusion | flops 13107072 | bytes 10572800 | tf_op jit(solution)/shard_map/while/body/eval_jaxpr/reduce_sum | solution.py:48
  206.0 3.8 %multiply_reduce_fusion.2 = f32[128,128]{1,0:T(8,128)S(1)} fusion(bf16[128,32,128]{2,0,1:T(8,128)(2,1)S(1)} %copy-done.2, f32[128,32,640]{2,0,1:T(8,128)S(1)} %get-tuple-element.154, f32[128]{0:T(128)S(1)} %get-tuple-element.155, pred[128,32]{0,1:T(8,128)(4,1)S(1)} %get-tuple-element.183, pred[128,640]{1,0:T(8,128)(4,1)S(1)} %get-tuple-element.184, ...), kind=kOutput, calls=%fused_computation.9.clone.1 | convolution fusion | flops 685752320 | bytes 11850240 | tf_op jit(solution)/shard_map/while/body/eval_jaxpr/dot_general | solution.py:49
  211.4 3.8 %fusion.97 = (f32[128]{0:T(128)S(1)}, f32[128,32,640]{2,0,1:T(8,128)S(1)}) fusion(pred[128,32]{0,1:T(8,128)(4,1)S(1)} %get-tuple-element.183, pred[128,640]{1,0:T(8,128)(4,1)S(1)} %get-tuple-element.184, bf16[640,128]{1,0:T(8,128)(2,1)S(1)} %get-tuple-element.181, bf16[128,32,128]{2,0,1:T(8,128)(2,1)} %get-tuple-element.180, ...), kind=kOutput, calls=%fused_computation.5.clone.1 | convolution fusion | flops 683147136 | bytes 11850240 | tf_op jit(solution)/shard_map/while/body/eval_jaxpr/dot_general | solution.py:38
  215.2 3.5 %fusion.98 = f32[128]{0:T(128)S(1)} fusion(f32[128,32,640]{2,0,1:T(8,128)S(1)} %get-tuple-element.154, f32[128]{0:T(128)S(1)} %get-tuple-element.155, pred[128,32]{0,1:T(8,128)(4,1)S(1)} %get-tuple-element.183, pred[128,640]{1,0:T(8,128)(4,1)S(1)} %get-tuple-element.184), kind=kLoop, calls=%fused_computation.3.clone.1 | loop fusion | flops 13107072 | bytes 10572800 | tf_op jit(solution)/shard_map/while/body/eval_jaxpr/reduce_sum | solution.py:48
  218.8 3.8 %multiply_reduce_fusion.2 = f32[128,128]{1,0:T(8,128)S(1)} fusion(bf16[128,32,128]{2,0,1:T(8,128)(2,1)S(1)} %copy-done.2, f32[128,32,640]{2,0,1:T(8,128)S(1)} %get-tuple-element.154, f32[128]{0:T(128)S(1)} %get-tuple-element.155, pred[128,32]{0,1:T(8,128)(4,1)S(1)} %get-tuple-element.183, pred[128,640]{1,0:T(8,128)(4,1)S(1)} %get-tuple-element.184, ...), kind=kOutput, calls=%fused_computation.9.clone.1 | convolution fusion | flops 685752320 | bytes 11850240 | tf_op jit(solution)/shard_map/while/body/eval_jaxpr/dot_general | solution.py:49
  224.1 3.8 %fusion.97 = (f32[128]{0:T(128)S(1)}, f32[128,32,640]{2,0,1:T(8,128)S(1)}) fusion(pred[128,32]{0,1:T(8,128)(4,1)S(1)} %get-tuple-element.183, pred[128,640]{1,0:T(8,128)(4,1)S(1)} %get-tuple-element.184, bf16[640,128]{1,0:T(8,128)(2,1)S(1)} %get-tuple-element.181, bf16[128,32,128]{2,0,1:T(8,128)(2,1)} %get-tuple-element.180, ...), kind=kOutput, calls=%fused_computation.5.clone.1 | convolution fusion | flops 683147136 | bytes 11850240 | tf_op jit(solution)/shard_map/while/body/eval_jaxpr/dot_general | solution.py:38
  227.9 3.5 %fusion.98 = f32[128]{0:T(128)S(1)} fusion(f32[128,32,640]{2,0,1:T(8,128)S(1)} %get-tuple-element.154, f32[128]{0:T(128)S(1)} %get-tuple-element.155, pred[128,32]{0,1:T(8,128)(4,1)S(1)} %get-tuple-element.183, pred[128,640]{1,0:T(8,128)(4,1)S(1)} %get-tuple-element.184), kind=kLoop, calls=%fused_computation.3.clone.1 | loop fusion | flops 13107072 | bytes 10572800 | tf_op jit(solution)/shard_map/while/body/eval_jaxpr/reduce_sum | solution.py:48
  231.5 3.8 %multiply_reduce_fusion.2 = f32[128,128]{1,0:T(8,128)S(1)} fusion(bf16[128,32,128]{2,0,1:T(8,128)(2,1)S(1)} %copy-done.2, f32[128,32,640]{2,0,1:T(8,128)S(1)} %get-tuple-element.154, f32[128]{0:T(128)S(1)} %get-tuple-element.155, pred[128,32]{0,1:T(8,128)(4,1)S(1)} %get-tuple-element.183, pred[128,640]{1,0:T(8,128)(4,1)S(1)} %get-tuple-element.184, ...), kind=kOutput, calls=%fused_computation.9.clone.1 | convolution fusion | flops 685752320 | bytes 11850240 | tf_op jit(solution)/shard_map/while/body/eval_jaxpr/dot_general | solution.py:49
  236.9 3.8 %fusion.97 = (f32[128]{0:T(128)S(1)}, f32[128,32,640]{2,0,1:T(8,128)S(1)}) fusion(pred[128,32]{0,1:T(8,128)(4,1)S(1)} %get-tuple-element.183, pred[128,640]{1,0:T(8,128)(4,1)S(1)} %get-tuple-element.184, bf16[640,128]{1,0:T(8,128)(2,1)S(1)} %get-tuple-element.181, bf16[128,32,128]{2,0,1:T(8,128)(2,1)} %get-tuple-element.180, ...), kind=kOutput, calls=%fused_computation.5.clone.1 | convolution fusion | flops 683147136 | bytes 11850240 | tf_op jit(solution)/shard_map/while/body/eval_jaxpr/dot_general | solution.py:38
  240.7 3.5 %fusion.98 = f32[128]{0:T(128)S(1)} fusion(f32[128,32,640]{2,0,1:T(8,128)S(1)} %get-tuple-element.154, f32[128]{0:T(128)S(1)} %get-tuple-element.155, pred[128,32]{0,1:T(8,128)(4,1)S(1)} %get-tuple-element.183, pred[128,640]{1,0:T(8,128)(4,1)S(1)} %get-tuple-element.184), kind=kLoop, calls=%fused_computation.3.clone.1 | loop fusion | flops 13107072 | bytes 10572800 | tf_op jit(solution)/shard_map/while/body/eval_jaxpr/reduce_sum | solution.py:48
  244.2 3.8 %multiply_reduce_fusion.2 = f32[128,128]{1,0:T(8,128)S(1)} fusion(bf16[128,32,128]{2,0,1:T(8,128)(2,1)S(1)} %copy-done.2, f32[128,32,640]{2,0,1:T(8,128)S(1)} %get-tuple-element.154, f32[128]{0:T(128)S(1)} %get-tuple-element.155, pred[128,32]{0,1:T(8,128)(4,1)S(1)} %get-tuple-element.183, pred[128,640]{1,0:T(8,128)(4,1)S(1)} %get-tuple-element.184, ...), kind=kOutput, calls=%fused_computation.9.clone.1 | convolution fusion | flops 685752320 | bytes 11850240 | tf_op jit(solution)/shard_map/while/body/eval_jaxpr/dot_general | solution.py:49
  248.8 9.7 %fusion.84 = f32[128,4096]{1,0:T(8,128)} fusion(bf16[128,2048]{0,1:T(8,128)(2,1)} %bitcast.165, bf16[2048,4096]{1,0:T(8,128)(2,1)} %param.11), kind=kOutput, calls=%fused_computation.168 | convolution fusion | flops 2147483648 | bytes 19398656 | tf_op jit(solution)/shard_map/dot_general | solution.py:91
  258.6 32.0 %reduce-scatter.2.cloned.1.call-done = f32[32,4096]{1,0:T(8,128)} async-done(((f32[128,4096]{1,0:T(8,128)}), f32[32,4096]{1,0:T(8,128)}) %reduce-scatter.2.cloned.1.call-update) | async-done | bytes 524304 | tf_op jit(solution)/shard_map/reduce_scatter | solution.py:90
  290.6 1.2 fusion.18
  292.7 17.4 %all-gather.2.cloned.1.call-done = bf16[128,4096]{1,0:T(8,128)(2,1)} async-done(((bf16[32,4096]{1,0:T(8,128)(2,1)}), bf16[128,4096]{1,0:T(8,128)(2,1)}) %all-gather.2.cloned.1.call-update) | async-done | bytes 1048592 | tf_op jit(solution)/shard_map/all_gather | solution.py:100
  310.1 2.3 copy.64
  (161 shorter events, 31.0 us)
Async XLA Ops:
  7.2 1.2 copy-start
  7.2 283.4 %reduce-scatter.2.cloned.1.call-start = ((), (), s32[]{:S(2)}) async-start(), calls=%async_computation.1 | async-start | bytes 2621440 | tf_op jit(solution)/shard_map/reduce_scatter | solution.py:90
  16.0 23.7 %collective-permute-start.1 = (bf16[128,256]{1,0:T(8,128)(2,1)S(1)}, bf16[128,256]{1,0:T(8,128)(2,1)}, u32[]{:S(2)}, u32[]{:S(2)}) collective-permute-start(bf16[128,256]{1,0:T(8,128)(2,1)S(1)} %slice.217), channel_id=1, source_target_pairs={{0,16},{4,20},{8,24},{12,28},{1,17},{5,21},{9,25},{13,29},{2,18},{... | collective-permute-start | bytes 196616 | tf_op jit(solution)/shard_map/ppermute | solution.py:14
  20.8 19.7 %collective-permute-start.2 = (bf16[128,256]{1,0:T(8,128)(2,1)S(1)}, bf16[128,256]{1,0:T(8,128)(2,1)}, u32[]{:S(2)}, u32[]{:S(2)}) collective-permute-start(bf16[128,256]{1,0:T(8,128)(2,1)S(1)} %slice.217), channel_id=1, source_target_pairs={{0,12},{4,16},{8,20},{12,24},{16,28},{1,13},{5,17},{9,21},{13,25},... | collective-permute-start | bytes 196616 | tf_op jit(solution)/shard_map/ppermute | solution.py:14
  22.8 18.6 %collective-permute-start.3 = (bf16[128,256]{1,0:T(8,128)(2,1)S(1)}, bf16[128,256]{1,0:T(8,128)(2,1)}, u32[]{:S(2)}, u32[]{:S(2)}) collective-permute-start(bf16[128,256]{1,0:T(8,128)(2,1)S(1)} %slice.217), channel_id=1, source_target_pairs={{0,8},{4,12},{8,16},{12,20},{16,24},{20,28},{1,9},{5,13},{9,17},{1... | collective-permute-start | bytes 196616 | tf_op jit(solution)/shard_map/ppermute | solution.py:14
  24.7 17.5 %collective-permute-start.4 = (bf16[128,256]{1,0:T(8,128)(2,1)S(1)}, bf16[128,256]{1,0:T(8,128)(2,1)S(1)}, u32[]{:S(2)}, u32[]{:S(2)}) collective-permute-start(bf16[128,256]{1,0:T(8,128)(2,1)S(1)} %slice.217), channel_id=1, source_target_pairs={{0,4},{4,8},{8,12},{12,16},{16,20},{20,24},{24,28},{1,5},{5,9},{9,... | collective-permute-start | bytes 196616 | tf_op jit(solution)/shard_map/ppermute | solution.py:14
  26.6 15.6 %collective-permute-start = (bf16[32,256]{1,0:T(8,128)(2,1)S(1)}, bf16[32,256]{1,0:T(8,128)(2,1)S(1)}, u32[]{:S(2)}, u32[]{:S(2)}) collective-permute-start(bf16[32,256]{1,0:T(8,128)(2,1)S(1)} %slice.154), channel_id=1, source_target_pairs={{0,4},{4,8},{8,12},{12,16},{16,20},{20,24},{24,28},{1,5},{5,9},{9,... | collective-permute-start | bytes 49160 | tf_op jit(solution)/shard_map/ppermute | solution.py:14
  49.6 3.5 %copy-start.2 = (bf16[128,32,128]{2,0,1:T(8,128)(2,1)S(1)}, bf16[128,32,128]{2,0,1:T(8,128)(2,1)}, u32[]{:S(2)}) copy-start(bf16[128,32,128]{2,0,1:T(8,128)(2,1)} %get-tuple-element.178) | copy-start | bytes 3145732 | tf_op jit(solution)/shard_map/while
  62.4 3.5 %copy-start.2 = (bf16[128,32,128]{2,0,1:T(8,128)(2,1)S(1)}, bf16[128,32,128]{2,0,1:T(8,128)(2,1)}, u32[]{:S(2)}) copy-start(bf16[128,32,128]{2,0,1:T(8,128)(2,1)} %get-tuple-element.178) | copy-start | bytes 3145732 | tf_op jit(solution)/shard_map/while
  75.1 3.5 %copy-start.2 = (bf16[128,32,128]{2,0,1:T(8,128)(2,1)S(1)}, bf16[128,32,128]{2,0,1:T(8,128)(2,1)}, u32[]{:S(2)}) copy-start(bf16[128,32,128]{2,0,1:T(8,128)(2,1)} %get-tuple-element.178) | copy-start | bytes 3145732 | tf_op jit(solution)/shard_map/while
  87.9 3.5 %copy-start.2 = (bf16[128,32,128]{2,0,1:T(8,128)(2,1)S(1)}, bf16[128,32,128]{2,0,1:T(8,128)(2,1)}, u32[]{:S(2)}) copy-start(bf16[128,32,128]{2,0,1:T(8,128)(2,1)} %get-tuple-element.178) | copy-start | bytes 3145732 | tf_op jit(solution)/shard_map/while
  100.6 3.5 %copy-start.2 = (bf16[128,32,128]{2,0,1:T(8,128)(2,1)S(1)}, bf16[128,32,128]{2,0,1:T(8,128)(2,1)}, u32[]{:S(2)}) copy-start(bf16[128,32,128]{2,0,1:T(8,128)(2,1)} %get-tuple-element.178) | copy-start | bytes 3145732 | tf_op jit(solution)/shard_map/while
  113.3 3.5 %copy-start.2 = (bf16[128,32,128]{2,0,1:T(8,128)(2,1)S(1)}, bf16[128,32,128]{2,0,1:T(8,128)(2,1)}, u32[]{:S(2)}) copy-start(bf16[128,32,128]{2,0,1:T(8,128)(2,1)} %get-tuple-element.178) | copy-start | bytes 3145732 | tf_op jit(solution)/shard_map/while
  126.0 3.5 %copy-start.2 = (bf16[128,32,128]{2,0,1:T(8,128)(2,1)S(1)}, bf16[128,32,128]{2,0,1:T(8,128)(2,1)}, u32[]{:S(2)}) copy-start(bf16[128,32,128]{2,0,1:T(8,128)(2,1)} %get-tuple-element.178) | copy-start | bytes 3145732 | tf_op jit(solution)/shard_map/while
  138.8 3.5 %copy-start.2 = (bf16[128,32,128]{2,0,1:T(8,128)(2,1)S(1)}, bf16[128,32,128]{2,0,1:T(8,128)(2,1)}, u32[]{:S(2)}) copy-start(bf16[128,32,128]{2,0,1:T(8,128)(2,1)} %get-tuple-element.178) | copy-start | bytes 3145732 | tf_op jit(solution)/shard_map/while
  151.5 3.5 %copy-start.2 = (bf16[128,32,128]{2,0,1:T(8,128)(2,1)S(1)}, bf16[128,32,128]{2,0,1:T(8,128)(2,1)}, u32[]{:S(2)}) copy-start(bf16[128,32,128]{2,0,1:T(8,128)(2,1)} %get-tuple-element.178) | copy-start | bytes 3145732 | tf_op jit(solution)/shard_map/while
  164.2 3.5 %copy-start.2 = (bf16[128,32,128]{2,0,1:T(8,128)(2,1)S(1)}, bf16[128,32,128]{2,0,1:T(8,128)(2,1)}, u32[]{:S(2)}) copy-start(bf16[128,32,128]{2,0,1:T(8,128)(2,1)} %get-tuple-element.178) | copy-start | bytes 3145732 | tf_op jit(solution)/shard_map/while
  177.0 3.5 %copy-start.2 = (bf16[128,32,128]{2,0,1:T(8,128)(2,1)S(1)}, bf16[128,32,128]{2,0,1:T(8,128)(2,1)}, u32[]{:S(2)}) copy-start(bf16[128,32,128]{2,0,1:T(8,128)(2,1)} %get-tuple-element.178) | copy-start | bytes 3145732 | tf_op jit(solution)/shard_map/while
  189.7 3.5 %copy-start.2 = (bf16[128,32,128]{2,0,1:T(8,128)(2,1)S(1)}, bf16[128,32,128]{2,0,1:T(8,128)(2,1)}, u32[]{:S(2)}) copy-start(bf16[128,32,128]{2,0,1:T(8,128)(2,1)} %get-tuple-element.178) | copy-start | bytes 3145732 | tf_op jit(solution)/shard_map/while
  202.5 3.5 %copy-start.2 = (bf16[128,32,128]{2,0,1:T(8,128)(2,1)S(1)}, bf16[128,32,128]{2,0,1:T(8,128)(2,1)}, u32[]{:S(2)}) copy-start(bf16[128,32,128]{2,0,1:T(8,128)(2,1)} %get-tuple-element.178) | copy-start | bytes 3145732 | tf_op jit(solution)/shard_map/while
  215.2 3.5 %copy-start.2 = (bf16[128,32,128]{2,0,1:T(8,128)(2,1)S(1)}, bf16[128,32,128]{2,0,1:T(8,128)(2,1)}, u32[]{:S(2)}) copy-start(bf16[128,32,128]{2,0,1:T(8,128)(2,1)} %get-tuple-element.178) | copy-start | bytes 3145732 | tf_op jit(solution)/shard_map/while
  227.9 3.5 %copy-start.2 = (bf16[128,32,128]{2,0,1:T(8,128)(2,1)S(1)}, bf16[128,32,128]{2,0,1:T(8,128)(2,1)}, u32[]{:S(2)}) copy-start(bf16[128,32,128]{2,0,1:T(8,128)(2,1)} %get-tuple-element.178) | copy-start | bytes 3145732 | tf_op jit(solution)/shard_map/while
  240.7 3.5 %copy-start.2 = (bf16[128,32,128]{2,0,1:T(8,128)(2,1)S(1)}, bf16[128,32,128]{2,0,1:T(8,128)(2,1)}, u32[]{:S(2)}) copy-start(bf16[128,32,128]{2,0,1:T(8,128)(2,1)} %get-tuple-element.178) | copy-start | bytes 3145732 | tf_op jit(solution)/shard_map/while
  258.5 32.1 %copy-start.3 = (bf16[32,4096]{1,0:T(8,128)(2,1)S(1)}, bf16[32,4096]{1,0:T(8,128)(2,1)}, u32[]{:S(2)}) copy-start(bf16[32,4096]{1,0:T(8,128)(2,1)} %param.12) | copy-start | bytes 786436
  258.5 33.3 %copy-start.4 = (f32[4096]{0:T(1024)S(1)}, f32[4096]{0:T(1024)}, u32[]{:S(2)}) copy-start(f32[4096]{0:T(1024)} %param.13) | copy-start | bytes 49156
  258.5 51.6 %all-gather.2.cloned.1.call-start = ((), (), s32[]{:S(2)}) async-start(), calls=%async_computation.2 | async-start | bytes 1310720 | tf_op jit(solution)/shard_map/all_gather | solution.py:100
  291.8 20.6 %copy-start.1 = (bf16[32,4096]{1,0:T(8,128)(2,1)}, bf16[32,4096]{1,0:T(8,128)(2,1)S(1)}, u32[]{:S(2)}) copy-start(bf16[32,4096]{1,0:T(8,128)(2,1)S(1)} %get-tuple-element.188) | copy-start | bytes 786436
Sparse Core Ops, SparseCore 0:
  258.7 31.8 reduce-scatter.1
  292.8 17.2 all-gather.1
where the time goes:
time: 322 us; the launch traced here: 319 us
  matrix products  141 us (44%)
  other arithmetic  72.9 us (23%)
  waiting for transfers between devices  49.4 us (15%)
  local copies, waits for them, and re-layouts  21.8 us (7%)
  between operations  14.4 us (4%)
  starting transfers between devices  12.6 us (4%)
  blocking collectives  5.96 us (2%)
    dot_general x16, matrix products, attend_block(): lax.dot_general(mixed.reshape(rows * spread, width), key_one, (((1,), (1,...  60.8 us
    dot_general x16, matrix products, attend_block(): jnp.dot(weights.astype(jnp.bfloat16).reshape(rows * spread, -1), value_on...  60.4 us
    reduce_sum x16, other arithmetic, attend_block(): total = jnp.sum(weights, axis=(1, 2))  56.4 us
    reduce_scatter x1, waiting for transfers between devices, body(): lax.psum_scatter(jnp.dot(attention, out_weight, preferred_element_type=jn...  32 us
    all_gather x1, waiting for transfers between devices, body(): normed = lax.all_gather(normed_local, 'head', axis=0, tiled=True)  17.4 us
    ppermute x5, starting transfers between devices, from_behind(): lax.ppermute(value, axis, [(source, source + steps) for source in range(i...  12.5 us
    convert_element_type x16, other arithmetic, attend_block(): query[:, None, :].astype(jnp.float32) * key_two.astype(jnp.float32)  12.2 us
    dynamic_update_slice x32, local copies, waits for them, and re-layouts, body(): lax.map(lambda head: attend_block(head, key_one, value_one, key_two, valu...  11.8 us
  transfers between devices with their start and end apart: 7, of which 2 were waited for; matrix products, arithmetic and copies ran while one was open for 4% of the time, Pallas kernels for 0%

commit v1 on v0

v1 whole, which is shorter than its diff:
```python
import functools
import math

import jax
import jax.numpy as jnp
from jax import lax
from jax.experimental import pallas as pl
from jax.experimental.pallas import tpu as pltpu
from jax.sharding import PartitionSpec as P

HD = 128
W1 = 512
W2 = 32
ROWS = 32
GROUP = 16


def from_behind(value, axis, steps):
    count = lax.axis_size(axis)
    initial, last = (max(0, -steps), min(count, count - steps))
    return lax.ppermute(value, axis, [(source, source + steps) for source in range(initial, last)])


def attention_kernel(
    place, q_ref, k1_ref, v1_ref, k2_ref, v2_ref, out_ref,
    k1_diag, v1_diag, k2_near, v2_near, keep, scores_a, scores_b, peak_a, peak_b,
):
    tokens = q_ref.shape[0]
    blocks = k1_ref.shape[0] // tokens
    pairs = q_ref.shape[1] // (2 * HD)
    chunks = tokens // ROWS
    tasks = pairs * chunks
    rate = HD ** -0.5 * math.log2(math.e)
    slab = place[0]

    k1_diag[...] = jnp.zeros(k1_diag.shape, k1_diag.dtype)
    v1_diag[...] = jnp.zeros(v1_diag.shape, v1_diag.dtype)
    for j in range(blocks):
        key = k1_ref[j * tokens:(j + 1) * tokens, :].T
        value = v1_ref[j * tokens:(j + 1) * tokens, :]
        k1_diag[j, :HD, :tokens] = key
        k1_diag[j, HD:, tokens:] = key
        v1_diag[j, :tokens, :HD] = value
        v1_diag[j, tokens:, HD:] = value
    for r in range(W2):
        k2_near[r] = k2_ref[W2 - r:W2 - r + tokens, :].astype(jnp.bfloat16)
        v2_near[r] = v2_ref[W2 - r:W2 - r + tokens, :]
    row = lax.broadcasted_iota(jnp.int32, (tokens, 2 * tokens), 0)
    col = lax.broadcasted_iota(jnp.int32, (tokens, 2 * tokens), 1) % tokens
    keep[...] = (col <= row).astype(jnp.float32).astype(jnp.bfloat16)

    def twice(x):
        return jnp.concatenate([x, x], axis=-1)

    def split(task):
        pair, chunk = task // chunks, task % chunks
        return pl.multiple_of(chunk * ROWS, ROWS), pl.multiple_of(pair * 2 * HD, 2 * HD)

    def score(task, group, scores, full, peak):
        first, lane = split(task)
        query = q_ref[pl.ds(first, ROWS), pl.ds(lane, 2 * HD)]
        near = k2_near[group * GROUP:(group + 1) * GROUP, pl.ds(first, ROWS), :]
        mixed = (query[None] * twice(near)).reshape(GROUP * ROWS, 2 * HD)
        row = first + lax.broadcasted_iota(jnp.int32, (ROWS, 2 * tokens), 0)
        col = lax.broadcasted_iota(jnp.int32, (ROWS, 2 * tokens), 1) % tokens
        recent = (col <= row)[None]
        last = jnp.dot(mixed, k1_diag[blocks - 1], preferred_element_type=jnp.float32)
        last = last.reshape(GROUP, ROWS, 2 * tokens)
        if not full:
            offset = group * GROUP + lax.broadcasted_iota(jnp.int32, (GROUP, ROWS, 1), 0)
            place_row = slab * tokens + first + lax.broadcasted_iota(jnp.int32, (GROUP, ROWS, 1), 1)
            bias = jnp.where(place_row >= offset, 0.0, -jnp.inf)
            last = last + bias
        for j in range(blocks - 1):
            part = jnp.dot(mixed, k1_diag[j], preferred_element_type=jnp.float32)
            part = part.reshape(GROUP, ROWS, 2 * tokens)
            if not full:
                part = part + jnp.where(slab + j >= blocks - 1, bias, -jnp.inf)
            if j == 0:
                part = jnp.where(recent, last, part)
            scores[group, j] = part
            high = jnp.max(part, axis=0)
            peak = high if peak is None else jnp.maximum(peak, high)
        return peak

    def finish_peak(peak):
        left = jnp.max(peak[:, :tokens], axis=1, keepdims=True)
        right = jnp.max(peak[:, tokens:], axis=1, keepdims=True)
        return jnp.concatenate(
            [jnp.broadcast_to(left, (ROWS, tokens)), jnp.broadcast_to(right, (ROWS, tokens))], axis=1
        ) * rate

    def blend(task, group, scores, peak, acc, total):
        first, _ = split(task)
        mask = keep[pl.ds(first, ROWS), :][None]
        blended = None
        for j in range(blocks - 1):
            weights = jnp.exp2(scores[group, j] * rate - peak[None])
            part = jnp.sum(weights, axis=0)
            total = part if total is None else total + part
            weights = weights.astype(jnp.bfloat16)
            if j == 0:
                late = weights * mask
                weights = weights - late
                blended = jnp.dot(
                    late.reshape(GROUP * ROWS, 2 * tokens), v1_diag[blocks - 1],
                    preferred_element_type=jnp.float32,
                )
            blended = blended + jnp.dot(
                weights.reshape(GROUP * ROWS, 2 * tokens), v1_diag[j],
                preferred_element_type=jnp.float32,
            )
        near = v2_near[group * GROUP:(group + 1) * GROUP, pl.ds(first, ROWS), :]
        part = jnp.sum(twice(near) * blended.reshape(GROUP, ROWS, 2 * HD), axis=0)
        return (part if acc is None else acc + part), total

    def store(task, acc, total):
        first, lane = split(task)
        left = jnp.sum(total[:, :tokens], axis=1, keepdims=True)
        right = jnp.sum(total[:, tokens:], axis=1, keepdims=True)
        out = jnp.concatenate([acc[:, :HD] / left, acc[:, HD:] / right], axis=1)
        out_ref[pl.ds(first, ROWS), pl.ds(lane, 2 * HD)] = out.astype(out_ref.dtype)

    def step(task, ahead, here, here_peak, there, there_peak, full):
        peak_now = here_peak[...]
        acc = total = peak = None
        for group in range(W2 // GROUP):
            peak = score(ahead, group, there, full, peak)
            acc, total = blend(task, group, here, peak_now, acc, total)
        there_peak[...] = finish_peak(peak)
        store(task, acc, total)

    def run(full):
        peak = None
        for group in range(W2 // GROUP):
            peak = score(0, group, scores_a, full, peak)
        peak_a[...] = finish_peak(peak)

        def two(index, _):
            task = 2 * index
            step(task, task + 1, scores_a, peak_a, scores_b, peak_b, full)
            step(task + 1, jnp.minimum(task + 2, tasks - 1), scores_b, peak_b, scores_a, peak_a, full)
            return 0

        lax.fori_loop(0, tasks // 2, two, 0)

    @pl.when(slab >= blocks - 1)
    def _():
        run(True)

    @pl.when(slab < blocks - 1)
    def _():
        run(False)


def attention_of(place, queries, extended_one, extended_two):
    tokens, width = queries.shape
    blocks = extended_one.shape[0] // tokens
    vmem = pl.BlockSpec(memory_space=pltpu.VMEM)
    return pl.pallas_call(
        attention_kernel,
        out_shape=jax.ShapeDtypeStruct((tokens, width), jnp.bfloat16),
        in_specs=[pl.BlockSpec(memory_space=pltpu.SMEM)] + [vmem] * 5,
        out_specs=vmem,
        scratch_shapes=[
            pltpu.VMEM((blocks, 2 * HD, 2 * tokens), jnp.bfloat16),
            pltpu.VMEM((blocks, 2 * tokens, 2 * HD), jnp.bfloat16),
            pltpu.VMEM((W2, tokens, HD), jnp.bfloat16),
            pltpu.VMEM((W2, tokens, HD), jnp.float32),
            pltpu.VMEM((tokens, 2 * tokens), jnp.bfloat16),
        ]
        + [pltpu.VMEM((W2 // GROUP, blocks - 1, GROUP, ROWS, 2 * tokens), jnp.float32)] * 2
        + [pltpu.VMEM((ROWS, 2 * tokens), jnp.float32)] * 2,
        compiler_params=pltpu.CompilerParams(vmem_limit_bytes=48 * 1024 * 1024),
        name="attention",
    )(
        place,
        queries,
        extended_one[:, :HD],
        extended_one[:, HD:],
        extended_two[:, :HD].astype(jnp.float32),
        extended_two[:, HD:].astype(jnp.float32),
    )


def body(hidden_in, query_weight, shared_weight, out_weight, residual, norm_gain):
    tokens = hidden_in.shape[0]
    queries = jnp.dot(hidden_in, query_weight, preferred_element_type=jnp.float32).astype(
        jnp.bfloat16
    )
    local_part = jnp.dot(hidden_in, shared_weight, preferred_element_type=jnp.float32).astype(
        jnp.bfloat16
    )
    shared = lax.all_gather(local_part, "head", axis=1, tiled=True)
    first_pair = shared[:, : 2 * HD]
    second_pair = shared[:, 2 * HD :]
    reach = (W1 + tokens - 1) // tokens
    earlier, rim = from_behind((first_pair, second_pair[tokens - W2 :]), "ctx", 1)
    pieces = [earlier]
    for distance in range(2, reach + 1):
        pieces.append(from_behind(first_pair, "ctx", distance))
    extended_one = jnp.concatenate(pieces[::-1] + [first_pair], 0)
    extended_two = jnp.concatenate([rim, second_pair], 0)
    place = lax.axis_index("ctx").astype(jnp.int32).reshape(1)
    attention = attention_of(place, queries, extended_one, extended_two)
    summed = lax.psum_scatter(
        jnp.dot(attention, out_weight, preferred_element_type=jnp.float32),
        "head",
        scatter_dimension=0,
        tiled=True,
    )
    residual_out = (residual.astype(jnp.float32) + summed).astype(jnp.bfloat16)
    values = residual_out.astype(jnp.float32)
    scale = lax.rsqrt(jnp.mean(values * values, axis=1, keepdims=True) + 1e-05)
    normed_local = (values * scale * norm_gain).astype(jnp.bfloat16)
    normed = lax.all_gather(normed_local, "head", axis=0, tiled=True)
    return (residual_out, normed)


def solution(mesh):
    in_specs = (
        P("ctx", None),
        P(None, "head"),
        P(None, "head"),
        P("head", None),
        P(("ctx", "head"), None),
        P(),
    )
    out_specs = (P(("ctx", "head"), None), P("ctx", None))
    return jax.shard_map(body, mesh=mesh, in_specs=in_specs, out_specs=out_specs, check_vma=False)
```

time: 322 us -> 175 us (0.54)
  matrix products: 141 us -> 19.2 us
  other arithmetic: 72.9 us -> 2.08 us
  Pallas kernels: 0 us -> 67.3 us
  local copies, waits for them, and re-layouts: 21.8 us -> 3.55 us
    dot_general x32 -> x0, matrix products: 121 us -> none  [the longest x16 60.8 us: attend_block(): lax.dot_general(mixed.reshape(rows * spread, width), key_one, (((1,), (1,...]
    pallas_call x0 -> x1, Pallas kernels: none -> 67.3 us  [attention_of(): pl.pallas_call(attention_kernel, out_shape=jax.ShapeDtypeStruct((tokens,...]
    reduce_sum x16 -> x0, other arithmetic: 56.4 us -> none  [attend_block(): total = jnp.sum(weights, axis=(1, 2))]
    convert_element_type x16 -> x1, other arithmetic: 12.2 us -> 0.01 us  [attention_of(): extended_two[:, HD:].astype(jnp.float32)]
    dynamic_update_slice x32 -> x0, local copies, waits for them, and re-layouts: 11.8 us -> none  [body(): lax.map(lambda head: attend_block(head, key_one, value_one, key_two, valu...]
  transfers between devices with their start and end apart: 7 -> 7, of which waited for: 2 -> 2; matrix products, arithmetic and copies ran while one was open for 4% -> 5% of each run, Pallas kernels for 0% -> 0%
where the time goes in v1:
time: 175 us; the launch traced here: 174 us
  Pallas kernels  67.3 us (38%)
  waiting for transfers between devices  48.5 us (28%)
  matrix products  19.2 us (11%)
  between operations  14.3 us (8%)
  starting transfers between devices  12.8 us (7%)
  blocking collectives  5.96 us (3%)
  local copies, waits for them, and re-layouts  3.55 us (2%)
  other arithmetic  2.08 us (1%)
    pallas_call x1, Pallas kernels, attention_of(): pl.pallas_call(attention_kernel, out_shape=jax.ShapeDtypeStruct((tokens,...  67.3 us
    reduce_scatter x1, waiting for transfers between devices, body(): lax.psum_scatter(jnp.dot(attention, out_weight, preferred_element_type=jn...  31.1 us
    all_gather x1, waiting for transfers between devices, body(): normed = lax.all_gather(normed_local, 'head', axis=0, tiled=True)  17.4 us
    ppermute x5, starting transfers between devices, from_behind(): lax.ppermute(value, axis, [(source, source + steps) for source in range(i...  12.7 us
    dot_general x1, matrix products, body(): jnp.dot(attention, out_weight, preferred_element_type=jnp.float32)  9.44 us
    dot_general x1, matrix products, body(): jnp.dot(hidden_in, query_weight, preferred_element_type=jnp.float32)  8.11 us
    all_gather x1, blocking collectives, body(): shared = lax.all_gather(local_part, 'head', axis=1, tiled=True)  5.96 us
    unnamed x13, local copies, waits for them, and re-layouts  3.51 us
  transfers between devices with their start and end apart: 7, of which 2 were waited for; matrix products, arithmetic and copies ran while one was open for 5% of the time, Pallas kernels for 0%

profile of v1, /device:TPU:11, one launch (start us, length us, event | category | flops | bytes accessed | tf_op | source)
XLA Modules:
  0.0 173.6 jit_solution(16070681334061897180)
XLA Ops:
  7.2 0.0 copy-start
  7.2 0.0 reduce-scatter.2.cloned.1.call-start
  7.2 1.2 copy-done
  8.4 1.6 convolution_convert_fusion.1
  10.0 6.0 %all_gather.6 = bf16[128,512]{1,0:T(8,128)(2,1)S(1)} all-gather(bf16[128,128]{1,0:T(8,128)(2,1)S(1)} %convolution_convert_fusion.1), channel_id=1, replica_groups=mesh['ctx'=8,'head'=4] {'head'}, dimensions={1}, use_global_device_ids=true | all-gather | bytes 163840 | tf_op jit(solution)/shard_map/all_gather | solution.py:194
  16.0 3.2 %collective-permute-start.3 = (bf16[128,256]{1,0:T(8,128)(2,1)S(1)}, bf16[128,256]{1,0:T(8,128)(2,1)S(1)}, u32[]{:S(2)}, u32[]{:S(2)}) collective-permute-start(bf16[128,256]{1,0:T(8,128)(2,1)S(1)} %slice.29), channel_id=1, source_target_pairs={{0,4},{4,8},{8,12},{12,16},{16,20},{20,24},{24,28},{1,5},{5,9},{9,... | collective-permute-start | bytes 196616 | tf_op jit(solution)/shard_map/ppermute | solution.py:21
  19.2 3.2 %collective-permute-start.2 = (bf16[128,256]{1,0:T(8,128)(2,1)S(1)}, bf16[128,256]{1,0:T(8,128)(2,1)S(1)}, u32[]{:S(2)}, u32[]{:S(2)}) collective-permute-start(bf16[128,256]{1,0:T(8,128)(2,1)S(1)} %slice.29), channel_id=1, source_target_pairs={{0,8},{4,12},{8,16},{12,20},{16,24},{20,28},{1,9},{5,13},{9,17},{1... | collective-permute-start | bytes 196616 | tf_op jit(solution)/shard_map/ppermute | solution.py:21
  22.4 2.2 %collective-permute-start.1 = (bf16[128,256]{1,0:T(8,128)(2,1)S(1)}, bf16[128,256]{1,0:T(8,128)(2,1)S(1)}, u32[]{:S(2)}, u32[]{:S(2)}) collective-permute-start(bf16[128,256]{1,0:T(8,128)(2,1)S(1)} %slice.29), channel_id=1, source_target_pairs={{0,12},{4,16},{8,20},{12,24},{16,28},{1,13},{5,17},{9,21},{13,25},... | collective-permute-start | bytes 196616 | tf_op jit(solution)/shard_map/ppermute | solution.py:21
  24.6 1.3 collective-permute-start
  25.9 2.8 %collective-permute-start.4 = (bf16[32,256]{1,0:T(8,128)(2,1)S(1)}, bf16[32,256]{1,0:T(8,128)(2,1)S(1)}, u32[]{:S(2)}, u32[]{:S(2)}) collective-permute-start(bf16[32,256]{1,0:T(8,128)(2,1)S(1)} %slice.32), channel_id=1, source_target_pairs={{0,4},{4,8},{8,12},{12,16},{16,20},{20,24},{24,28},{1,5},{5,9},{9,... | collective-permute-start | bytes 49160 | tf_op jit(solution)/shard_map/ppermute | solution.py:21
  28.8 8.1 %convolution_convert_fusion.q_ref = bf16[128,2048]{1,0:T(8,128)(2,1)S(1)} fusion(bf16[128,4096]{1,0:T(8,128)(2,1)S(1)} %copy-done, bf16[4096,2048]{1,0:T(8,128)(2,1)} %param.7), kind=kOutput, calls=%fused_computation | convolution fusion | flops 2147745792 | bytes 18350080 | tf_op jit(solution)/shard_map/dot_general | solution.py:188
  36.9 0.0 copy-start.2
  36.9 0.0 copy-start.3
  36.9 0.0 collective-permute-done
  36.9 0.0 collective-permute-done.1
  37.0 0.0 collective-permute-done.2
  37.0 0.0 collective-permute-done.3
  37.1 0.0 collective-permute-done.4
  37.1 67.3 %attention.1 = bf16[128,2048]{1,0:T(8,128)(2,1)S(1)} custom-call(s32[1]{0:T(128)} %bitcast.place, bf16[128,2048]{1,0:T(8,128)(2,1)S(1)} %convolution_convert_fusion.q_ref, bf16[640,128]{1,0:T(8,128)(2,1)S(1)} %get-tuple-element.5.k1_ref, bf16[640,128]{1,0:T(8,128)(2,1)S(1)} %get-tuple-element.4.v1_ref, f32[160,128]{1,0:T(8,128)S(1)} %get-tuple-element.9.k2_ref, ...), custom_call_target="tpu_custom_call" | custom-call | tf_op jit(solution)/shard_map/attention/pallas_call | solution.py:160
  104.4 9.4 %fusion.8 = f32[128,4096]{1,0:T(8,128)} fusion(bf16[128,2048]{1,0:T(8,128)(2,1)S(1)} %attention.1, bf16[2048,4096]{1,0:T(8,128)(2,1)} %param.9), kind=kOutput, calls=%fused_computation.22 | convolution fusion | flops 2147483648 | bytes 19398656 | tf_op jit(solution)/shard_map/dot_general | solution.py:207
  113.8 0.0 reduce-scatter.2.cloned.1.call-update
  113.8 0.0 all-gather.2.cloned.1.call-start
  113.9 31.1 %reduce-scatter.2.cloned.1.call-done = f32[32,4096]{1,0:T(8,128)} async-done(((f32[128,4096]{1,0:T(8,128)}), f32[32,4096]{1,0:T(8,128)}) %reduce-scatter.2.cloned.1.call-update) | async-done | bytes 524304 | tf_op jit(solution)/shard_map/reduce_scatter | solution.py:206
  145.0 0.0 copy-done.2
  145.0 1.2 fusion
  146.2 0.0 copy-start.1
  146.2 0.0 copy-done.3
  146.2 0.8 fusion.2
  147.1 0.0 all-gather.2.cloned.1.call-update
  147.1 17.4 %all-gather.2.cloned.1.call-done = bf16[128,4096]{1,0:T(8,128)(2,1)} async-done(((bf16[32,4096]{1,0:T(8,128)(2,1)}), bf16[128,4096]{1,0:T(8,128)(2,1)}) %all-gather.2.cloned.1.call-update) | async-done | bytes 1048592 | tf_op jit(solution)/shard_map/all_gather | solution.py:216
  164.5 2.3 %copy.13 = bf16[128,4096]{1,0:T(8,128)(2,1)} copy(bf16[128,4096]{1,0:T(8,128)(2,1)} %all-gather.2.cloned.1.call-done) | data formatting | bytes 2097152
  166.8 0.0 copy-done.1
  (10 shorter events, 0.1 us)
Async XLA Ops:
  7.2 1.2 copy-start
  7.2 137.8 %reduce-scatter.2.cloned.1.call-start = ((), (), s32[]{:S(2)}) async-start(), calls=%async_computation.1 | async-start | bytes 2621440 | tf_op jit(solution)/shard_map/reduce_scatter | solution.py:206
  16.0 21.0 %collective-permute-start.3 = (bf16[128,256]{1,0:T(8,128)(2,1)S(1)}, bf16[128,256]{1,0:T(8,128)(2,1)S(1)}, u32[]{:S(2)}, u32[]{:S(2)}) collective-permute-start(bf16[128,256]{1,0:T(8,128)(2,1)S(1)} %slice.29), channel_id=1, source_target_pairs={{0,4},{4,8},{8,12},{12,16},{16,20},{20,24},{24,28},{1,5},{5,9},{9,... | collective-permute-start | bytes 196616 | tf_op jit(solution)/shard_map/ppermute | solution.py:21
  19.2 17.8 %collective-permute-start.2 = (bf16[128,256]{1,0:T(8,128)(2,1)S(1)}, bf16[128,256]{1,0:T(8,128)(2,1)S(1)}, u32[]{:S(2)}, u32[]{:S(2)}) collective-permute-start(bf16[128,256]{1,0:T(8,128)(2,1)S(1)} %slice.29), channel_id=1, source_target_pairs={{0,8},{4,12},{8,16},{12,20},{16,24},{20,28},{1,9},{5,13},{9,17},{1... | collective-permute-start | bytes 196616 | tf_op jit(solution)/shard_map/ppermute | solution.py:21
  22.4 14.5 %collective-permute-start.1 = (bf16[128,256]{1,0:T(8,128)(2,1)S(1)}, bf16[128,256]{1,0:T(8,128)(2,1)S(1)}, u32[]{:S(2)}, u32[]{:S(2)}) collective-permute-start(bf16[128,256]{1,0:T(8,128)(2,1)S(1)} %slice.29), channel_id=1, source_target_pairs={{0,12},{4,16},{8,20},{12,24},{16,28},{1,13},{5,17},{9,21},{13,25},... | collective-permute-start | bytes 196616 | tf_op jit(solution)/shard_map/ppermute | solution.py:21
  24.6 12.3 %collective-permute-start = (bf16[128,256]{1,0:T(8,128)(2,1)S(1)}, bf16[128,256]{1,0:T(8,128)(2,1)S(1)}, u32[]{:S(2)}, u32[]{:S(2)}) collective-permute-start(bf16[128,256]{1,0:T(8,128)(2,1)S(1)} %slice.29), channel_id=1, source_target_pairs={{0,16},{4,20},{8,24},{12,28},{1,17},{5,21},{9,25},{13,29},{2,18},{... | collective-permute-start | bytes 196616 | tf_op jit(solution)/shard_map/ppermute | solution.py:21
  25.9 11.1 %collective-permute-start.4 = (bf16[32,256]{1,0:T(8,128)(2,1)S(1)}, bf16[32,256]{1,0:T(8,128)(2,1)S(1)}, u32[]{:S(2)}, u32[]{:S(2)}) collective-permute-start(bf16[32,256]{1,0:T(8,128)(2,1)S(1)} %slice.32), channel_id=1, source_target_pairs={{0,4},{4,8},{8,12},{12,16},{16,20},{20,24},{24,28},{1,5},{5,9},{9,... | collective-permute-start | bytes 49160 | tf_op jit(solution)/shard_map/ppermute | solution.py:21
  36.9 108.1 %copy-start.2 = (bf16[32,4096]{1,0:T(8,128)(2,1)S(1)}, bf16[32,4096]{1,0:T(8,128)(2,1)}, u32[]{:S(2)}) copy-start(bf16[32,4096]{1,0:T(8,128)(2,1)} %param.10) | copy-start | bytes 786436
  36.9 109.3 %copy-start.3 = (f32[4096]{0:T(1024)S(1)}, f32[4096]{0:T(1024)}, u32[]{:S(2)}) copy-start(f32[4096]{0:T(1024)} %param.11) | copy-start | bytes 49156
  113.8 50.7 %all-gather.2.cloned.1.call-start = ((), (), s32[]{:S(2)}) async-start(), calls=%async_computation.2 | async-start | bytes 1310720 | tf_op jit(solution)/shard_map/all_gather | solution.py:216
  146.2 20.6 %copy-start.1 = (bf16[32,4096]{1,0:T(8,128)(2,1)}, bf16[32,4096]{1,0:T(8,128)(2,1)S(1)}, u32[]{:S(2)}) copy-start(bf16[32,4096]{1,0:T(8,128)(2,1)S(1)} %get-tuple-element.12) | copy-start | bytes 786436
Sparse Core Ops, SparseCore 0:
  113.9 30.9 reduce-scatter.1
  147.2 17.2 all-gather.1

commit v2 on v1

--- a/solution.py
+++ b/solution.py
@@ -19,6 +19,45 @@
     count = lax.axis_size(axis)
     initial, last = (max(0, -steps), min(count, count - steps))
     return lax.ppermute(value, axis, [(source, source + steps) for source in range(initial, last)])
+
+
+def swap(value, axis, bit):
+    count = lax.axis_size(axis)
+    return lax.ppermute(value, axis, [(source, source ^ (1 << bit)) for source in range(count)])
+
+
+def pick(value, place, dim):
+    return lax.dynamic_index_in_dim(value, place, dim, keepdims=False)
+
+
+def sum_to_owner(value, axis):
+    count = lax.axis_size(axis)
+    if count & (count - 1):
+        return lax.psum_scatter(value, axis, scatter_dimension=0, tiled=True)
+    place = lax.axis_index(axis)
+    value = value.reshape(count, value.shape[0] // count, value.shape[1])
+    for bit in range(count.bit_length() - 1):
+        value = value.reshape(value.shape[0] // 2, 2, *value.shape[1:])
+        mine = (place >> bit) & 1
+        value = pick(value, mine, 1) + swap(
+            pick(value, 1 - mine, 1).astype(jnp.bfloat16), axis, bit
+        ).astype(jnp.float32)
+    return value[0]
+
+
+def share_rows(value, axis):
+    count = lax.axis_size(axis)
+    if count & (count - 1):
+        return lax.all_gather(value, axis, axis=0, tiled=True)
+    place = lax.axis_index(axis)
+    rows, width = value.shape
+    value = value[None]
+    for bit in reversed(range(count.bit_length() - 1)):
+        mine = (place >> bit) & 1
+        other = swap(value, axis, bit)
+        value = jnp.where(mine == 0, jnp.stack([value, other], 1), jnp.stack([other, value], 1))
+        value = value.reshape(-1, rows, width)
+    return value.reshape(-1, width)
 
 
 def attention_kernel(
@@ -203,17 +242,14 @@
     extended_two = jnp.concatenate([rim, second_pair], 0)
     place = lax.axis_index("ctx").astype(jnp.int32).reshape(1)
     attention = attention_of(place, queries, extended_one, extended_two)
-    summed = lax.psum_scatter(
-        jnp.dot(attention, out_weight, preferred_element_type=jnp.float32),
-        "head",
-        scatter_dimension=0,
-        tiled=True,
+    summed = sum_to_owner(
+        jnp.dot(attention, out_weight, preferred_element_type=jnp.float32), "head"
     )
     residual_out = (residual.astype(jnp.float32) + summed).astype(jnp.bfloat16)
     values = residual_out.astype(jnp.float32)
     scale = lax.rsqrt(jnp.mean(values * values, axis=1, keepdims=True) + 1e-05)
     normed_local = (values * scale * norm_gain).astype(jnp.bfloat16)
-    normed = lax.all_gather(normed_local, "head", axis=0, tiled=True)
+    normed = share_rows(normed_local, "head")
     return (residual_out, normed)
 
 

time: 175 us -> 137 us (0.78)
  the two profiles are of different devices: /device:TPU:11 before, /device:TPU:0 now
where the time goes in v2:
time: 137 us; the launch traced here: 136 us
  Pallas kernels  67.3 us (49%)
  starting transfers between devices  19.6 us (14%)
  matrix products  17.9 us (13%)
  waiting for transfers between devices  16.9 us (12%)
  blocking collectives  6.58 us (5%)
  local copies, waits for them, and re-layouts  4.2 us (3%)
  other arithmetic  2.87 us (2%)
    pallas_call x1, Pallas kernels, attention_of(): pl.pallas_call(attention_kernel, out_shape=jax.ShapeDtypeStruct((tokens,...  67.3 us
    ppermute x4, waiting for transfers between devices, swap(): lax.ppermute(value, axis, [(source, source ^ 1 << bit) for source in rang...  16.9 us
    ppermute x5, starting transfers between devices, from_behind(): lax.ppermute(value, axis, [(source, source + steps) for source in range(i...  16.4 us
    dot_general x1, matrix products, body(): jnp.dot(hidden_in, query_weight, preferred_element_type=jnp.float32)  8.11 us
    dot_general x1, matrix products, body(): jnp.dot(attention, out_weight, preferred_element_type=jnp.float32)  8.1 us
    all_gather x1, blocking collectives, body(): shared = lax.all_gather(local_part, 'head', axis=1, tiled=True)  6.58 us
    ppermute x4, starting transfers between devices, swap(): lax.ppermute(value, axis, [(source, source ^ 1 << bit) for source in rang...  3.24 us
  transfers between devices with their start and end apart: 9, of which 4 were waited for; matrix products, arithmetic and copies ran while one was open for 6% of the time, Pallas kernels for 0%

profile of v2, /device:TPU:0, one launch (start us, length us, event | category | flops | bytes accessed | tf_op | source)
XLA Modules:
  0.0 136.2 jit_solution(16272607504824584895)
XLA Ops:
  0.6 0.0 copy-start
  0.6 1.2 copy-done
  1.9 1.6 %convolution_convert_fusion.1 = bf16[128,128]{1,0:T(8,128)(2,1)S(1)} fusion(bf16[128,4096]{1,0:T(8,128)(2,1)S(1)} %copy-done, bf16[4096,128]{1,0:T(8,128)(2,1)} %param.8), kind=kOutput, calls=%fused_computation.1 | convolution fusion | flops 134234112 | bytes 2129920 | tf_op jit(solution)/shard_map/dot_general | solution.py:230
  3.5 6.6 %all_gather.3 = bf16[128,512]{1,0:T(8,128)(2,1)S(1)} all-gather(bf16[128,128]{1,0:T(8,128)(2,1)S(1)} %convolution_convert_fusion.1), channel_id=1, replica_groups=mesh['ctx'=8,'head'=4] {'head'}, dimensions={1}, use_global_device_ids=true | all-gather | bytes 163840 | tf_op jit(solution)/shard_map/all_gather | solution.py:233
  10.1 4.8 %collective-permute-start = (bf16[128,256]{1,0:T(8,128)(2,1)S(1)}, bf16[128,256]{1,0:T(8,128)(2,1)S(1)}, u32[]{:S(2)}, u32[]{:S(2)}) collective-permute-start(bf16[128,256]{1,0:T(8,128)(2,1)S(1)} %slice.29), channel_id=1, source_target_pairs={{0,16},{4,20},{8,24},{12,28},{1,17},{5,21},{9,25},{13,29},{2,18},{... | collective-permute-start | bytes 196616 | tf_op jit(solution)/shard_map/ppermute | solution.py:21
  14.9 4.4 %collective-permute-start.1 = (bf16[128,256]{1,0:T(8,128)(2,1)S(1)}, bf16[128,256]{1,0:T(8,128)(2,1)S(1)}, u32[]{:S(2)}, u32[]{:S(2)}) collective-permute-start(bf16[128,256]{1,0:T(8,128)(2,1)S(1)} %slice.29), channel_id=1, source_target_pairs={{0,12},{4,16},{8,20},{12,24},{16,28},{1,13},{5,17},{9,21},{13,25},... | collective-permute-start | bytes 196616 | tf_op jit(solution)/shard_map/ppermute | solution.py:21
  19.4 1.3 collective-permute-start.2
  20.7 3.1 %collective-permute-start.3 = (bf16[128,256]{1,0:T(8,128)(2,1)S(1)}, bf16[128,256]{1,0:T(8,128)(2,1)S(1)}, u32[]{:S(2)}, u32[]{:S(2)}) collective-permute-start(bf16[128,256]{1,0:T(8,128)(2,1)S(1)} %slice.29), channel_id=1, source_target_pairs={{0,4},{4,8},{8,12},{12,16},{16,20},{20,24},{24,28},{1,5},{5,9},{9,... | collective-permute-start | bytes 196616 | tf_op jit(solution)/shard_map/ppermute | solution.py:21
  23.8 2.7 %collective-permute-start.4 = (bf16[32,256]{1,0:T(8,128)(2,1)S(1)}, bf16[32,256]{1,0:T(8,128)(2,1)S(1)}, u32[]{:S(2)}, u32[]{:S(2)}) collective-permute-start(bf16[32,256]{1,0:T(8,128)(2,1)S(1)} %slice.32), channel_id=1, source_target_pairs={{0,4},{4,8},{8,12},{12,16},{16,20},{20,24},{24,28},{1,5},{5,9},{9,... | collective-permute-start | bytes 49160 | tf_op jit(solution)/shard_map/ppermute | solution.py:21
  26.5 8.1 %convolution_convert_fusion.q_ref = bf16[128,2048]{1,0:T(8,128)(2,1)S(1)} fusion(bf16[128,4096]{1,0:T(8,128)(2,1)S(1)} %copy-done, bf16[4096,2048]{1,0:T(8,128)(2,1)} %param.7), kind=kOutput, calls=%fused_computation | convolution fusion | flops 2147745792 | bytes 18350080 | tf_op jit(solution)/shard_map/dot_general | solution.py:227
  34.6 0.0 copy-start.3
  34.6 0.0 copy-start.4
  34.7 0.0 collective-permute-done
  34.7 0.0 collective-permute-done.1
  34.7 0.0 collective-permute-done.2
  34.7 0.0 collective-permute-done.3
  34.8 0.0 collective-permute-done.4
  34.8 67.3 %attention.1 = bf16[128,2048]{1,0:T(8,128)(2,1)S(1)} custom-call(s32[1]{0:T(128)} %bitcast.place, bf16[128,2048]{1,0:T(8,128)(2,1)S(1)} %convolution_convert_fusion.q_ref, bf16[640,128]{1,0:T(8,128)(2,1)S(1)} %get-tuple-element.5.k1_ref, bf16[640,128]{1,0:T(8,128)(2,1)S(1)} %get-tuple-element.4.v1_ref, f32[160,128]{1,0:T(8,128)S(1)} %get-tuple-element.11.k2_ref, ...), custom_call_target="tpu_custom_call" | custom-call | tf_op jit(solution)/shard_map/attention/pallas_call | solution.py:199
  102.1 8.1 %fusion.13 = f32[128,4096]{1,0:T(8,128)S(1)} fusion(bf16[128,2048]{1,0:T(8,128)(2,1)S(1)} %attention.1, bf16[2048,4096]{1,0:T(8,128)(2,1)} %param.9), kind=kOutput, calls=%fused_computation.32 | convolution fusion | flops 2147483648 | bytes 19398656 | tf_op jit(solution)/shard_map/dot_general | solution.py:246
  110.2 0.9 fusion.3
  111.1 0.0 collective-permute-start.5
  111.1 2.2 %collective-permute-done.5 = bf16[2,32,4096]{2,1,0:T(8,128)(2,1)} collective-permute-done((bf16[2,32,4096]{2,1,0:T(8,128)(2,1)}, bf16[2,32,4096]{2,1,0:T(8,128)(2,1)}, u32[]{:S(2)}, u32[]{:S(2)}) %collective-permute-start.5) | collective-permute-done | bytes 524320 | tf_op jit(solution)/shard_map/ppermute | solution.py:26
  113.3 1.1 bitcast_add_fusion
  114.5 0.0 copy-start.1
  114.5 1.0 copy-done.1
  115.5 1.6 %collective-permute-start.6 = (bf16[1,32,4096]{2,1,0:T(8,128)(2,1)S(1)}, bf16[1,32,4096]{2,1,0:T(8,128)(2,1)S(1)}, u32[]{:S(2)}, u32[]{:S(2)}) collective-permute-start(bf16[1,32,4096]{2,1,0:T(8,128)(2,1)S(1)} %dynamic-slice_convert_fusion), channel_id=1, source_target_pairs={{0,2},{1,3},{2,0},{3,1},{4,6},{5,7},{6,4},{7,5},{8,10},{9,11},{10,... | collective-permute-start | bytes 786440 | tf_op jit(solution)/shard_map/ppermute | solution.py:26
  117.1 6.8 %collective-permute-done.6 = bf16[1,32,4096]{2,1,0:T(8,128)(2,1)S(1)} collective-permute-done((bf16[1,32,4096]{2,1,0:T(8,128)(2,1)S(1)}, bf16[1,32,4096]{2,1,0:T(8,128)(2,1)S(1)}, u32[]{:S(2)}, u32[]{:S(2)}) %collective-permute-start.6) | collective-permute-done | bytes 262176 | tf_op jit(solution)/shard_map/ppermute | solution.py:26
  123.9 0.0 copy-done.3
  123.9 1.3 fusion
  125.2 0.0 copy-start.2
  125.2 0.0 copy-done.4
  125.2 0.1 fusion.6
  125.3 1.6 %collective-permute-start.7 = (bf16[1,32,4096]{2,1,0:T(8,128)(2,1)S(1)}, bf16[1,32,4096]{2,1,0:T(8,128)(2,1)S(1)}, u32[]{:S(2)}, u32[]{:S(2)}) collective-permute-start(bf16[1,32,4096]{2,1,0:T(8,128)(2,1)S(1)} %get-tuple-element.7), channel_id=1, source_target_pairs={{0,2},{1,3},{2,0},{3,1},{4,6},{5,7},{6,4},{7,5},{8,10},{9,11},{10,... | collective-permute-start | bytes 786440 | tf_op jit(solution)/shard_map/ppermute | solution.py:26
  126.9 6.0 %collective-permute-done.7 = bf16[1,32,4096]{2,1,0:T(8,128)(2,1)S(1)} collective-permute-done((bf16[1,32,4096]{2,1,0:T(8,128)(2,1)S(1)}, bf16[1,32,4096]{2,1,0:T(8,128)(2,1)S(1)}, u32[]{:S(2)}, u32[]{:S(2)}) %collective-permute-start.7) | collective-permute-done | bytes 262176 | tf_op jit(solution)/shard_map/ppermute | solution.py:26
  132.9 0.1 maximum_select_fusion.2
  133.0 0.1 collective-permute-start.8
  133.0 0.1 maximum_select_fusion.1
  133.1 1.8 %collective-permute-done.8 = bf16[2,32,4096]{2,1,0:T(8,128)(2,1)S(1)} collective-permute-done((bf16[2,32,4096]{2,1,0:T(8,128)(2,1)S(1)}, bf16[2,32,4096]{2,1,0:T(8,128)(2,1)S(1)}, u32[]{:S(2)}, u32[]{:S(2)}) %collective-permute-start.8) | collective-permute-done | bytes 524320 | tf_op jit(solution)/shard_map/ppermute | solution.py:26
  134.9 0.2 maximum_select_fusion
  135.1 1.0 copy.9
  136.2 0.0 copy-done.2
  (11 shorter events, 0.1 us)
Async XLA Ops:
  0.6 1.2 copy-start
  10.1 24.6 %collective-permute-start = (bf16[128,256]{1,0:T(8,128)(2,1)S(1)}, bf16[128,256]{1,0:T(8,128)(2,1)S(1)}, u32[]{:S(2)}, u32[]{:S(2)}) collective-permute-start(bf16[128,256]{1,0:T(8,128)(2,1)S(1)} %slice.29), channel_id=1, source_target_pairs={{0,16},{4,20},{8,24},{12,28},{1,17},{5,21},{9,25},{13,29},{2,18},{... | collective-permute-start | bytes 196616 | tf_op jit(solution)/shard_map/ppermute | solution.py:21
  14.9 19.8 %collective-permute-start.1 = (bf16[128,256]{1,0:T(8,128)(2,1)S(1)}, bf16[128,256]{1,0:T(8,128)(2,1)S(1)}, u32[]{:S(2)}, u32[]{:S(2)}) collective-permute-start(bf16[128,256]{1,0:T(8,128)(2,1)S(1)} %slice.29), channel_id=1, source_target_pairs={{0,12},{4,16},{8,20},{12,24},{16,28},{1,13},{5,17},{9,21},{13,25},... | collective-permute-start | bytes 196616 | tf_op jit(solution)/shard_map/ppermute | solution.py:21
  19.4 15.4 %collective-permute-start.2 = (bf16[128,256]{1,0:T(8,128)(2,1)S(1)}, bf16[128,256]{1,0:T(8,128)(2,1)S(1)}, u32[]{:S(2)}, u32[]{:S(2)}) collective-permute-start(bf16[128,256]{1,0:T(8,128)(2,1)S(1)} %slice.29), channel_id=1, source_target_pairs={{0,8},{4,12},{8,16},{12,20},{16,24},{20,28},{1,9},{5,13},{9,17},{1... | collective-permute-start | bytes 196616 | tf_op jit(solution)/shard_map/ppermute | solution.py:21
  20.7 14.1 %collective-permute-start.3 = (bf16[128,256]{1,0:T(8,128)(2,1)S(1)}, bf16[128,256]{1,0:T(8,128)(2,1)S(1)}, u32[]{:S(2)}, u32[]{:S(2)}) collective-permute-start(bf16[128,256]{1,0:T(8,128)(2,1)S(1)} %slice.29), channel_id=1, source_target_pairs={{0,4},{4,8},{8,12},{12,16},{16,20},{20,24},{24,28},{1,5},{5,9},{9,... | collective-permute-start | bytes 196616 | tf_op jit(solution)/shard_map/ppermute | solution.py:21
  23.8 11.0 %collective-permute-start.4 = (bf16[32,256]{1,0:T(8,128)(2,1)S(1)}, bf16[32,256]{1,0:T(8,128)(2,1)S(1)}, u32[]{:S(2)}, u32[]{:S(2)}) collective-permute-start(bf16[32,256]{1,0:T(8,128)(2,1)S(1)} %slice.32), channel_id=1, source_target_pairs={{0,4},{4,8},{8,12},{12,16},{16,20},{20,24},{24,28},{1,5},{5,9},{9,... | collective-permute-start | bytes 49160 | tf_op jit(solution)/shard_map/ppermute | solution.py:21
  34.6 89.3 %copy-start.3 = (bf16[32,4096]{1,0:T(8,128)(2,1)S(1)}, bf16[32,4096]{1,0:T(8,128)(2,1)}, u32[]{:S(2)}) copy-start(bf16[32,4096]{1,0:T(8,128)(2,1)} %param.10) | copy-start | bytes 786436
  34.6 90.5 %copy-start.4 = (f32[4096]{0:T(1024)S(1)}, f32[4096]{0:T(1024)}, u32[]{:S(2)}) copy-start(f32[4096]{0:T(1024)} %param.11) | copy-start | bytes 49156
  111.1 2.3 %collective-permute-start.5 = (bf16[2,32,4096]{2,1,0:T(8,128)(2,1)}, bf16[2,32,4096]{2,1,0:T(8,128)(2,1)}, u32[]{:S(2)}, u32[]{:S(2)}) collective-permute-start(bf16[2,32,4096]{2,1,0:T(8,128)(2,1)} %fusion.3), channel_id=1, source_target_pairs={{0,1},{1,0},{2,3},{3,2},{4,5},{5,4},{6,7},{7,6},{8,9},{9,8},{10,11... | collective-permute-start | bytes 1572872 | tf_op jit(solution)/shard_map/ppermute | solution.py:26
  114.5 1.0 copy-start.1
  115.5 8.4 %collective-permute-start.6 = (bf16[1,32,4096]{2,1,0:T(8,128)(2,1)S(1)}, bf16[1,32,4096]{2,1,0:T(8,128)(2,1)S(1)}, u32[]{:S(2)}, u32[]{:S(2)}) collective-permute-start(bf16[1,32,4096]{2,1,0:T(8,128)(2,1)S(1)} %dynamic-slice_convert_fusion), channel_id=1, source_target_pairs={{0,2},{1,3},{2,0},{3,1},{4,6},{5,7},{6,4},{7,5},{8,10},{9,11},{10,... | collective-permute-start | bytes 786440 | tf_op jit(solution)/shard_map/ppermute | solution.py:26
  125.2 11.0 %copy-start.2 = (bf16[32,4096]{1,0:T(8,128)(2,1)}, bf16[32,4096]{1,0:T(8,128)(2,1)S(1)}, u32[]{:S(2)}) copy-start(bf16[32,4096]{1,0:T(8,128)(2,1)S(1)} %get-tuple-element.3) | copy-start | bytes 786436
  125.3 7.6 %collective-permute-start.7 = (bf16[1,32,4096]{2,1,0:T(8,128)(2,1)S(1)}, bf16[1,32,4096]{2,1,0:T(8,128)(2,1)S(1)}, u32[]{:S(2)}, u32[]{:S(2)}) collective-permute-start(bf16[1,32,4096]{2,1,0:T(8,128)(2,1)S(1)} %get-tuple-element.7), channel_id=1, source_target_pairs={{0,2},{1,3},{2,0},{3,1},{4,6},{5,7},{6,4},{7,5},{8,10},{9,11},{10,... | collective-permute-start | bytes 786440 | tf_op jit(solution)/shard_map/ppermute | solution.py:26
  133.0 2.0 %collective-permute-start.8 = (bf16[2,32,4096]{2,1,0:T(8,128)(2,1)S(1)}, bf16[2,32,4096]{2,1,0:T(8,128)(2,1)S(1)}, u32[]{:S(2)}, u32[]{:S(2)}) collective-permute-start(bf16[2,32,4096]{2,1,0:T(8,128)(2,1)S(1)} %maximum_select_fusion.2), channel_id=1, source_target_pairs={{0,1},{1,0},{2,3},{3,2},{4,5},{5,4},{6,7},{7,6},{8,9},{9,8},{10,11... | collective-permute-start | bytes 1572872 | tf_op jit(solution)/shard_map/ppermute | solution.py:26

commit v3 on v2

v3 whole, which is shorter than its diff:
```python
import math

import jax
import jax.numpy as jnp
from jax import lax
from jax.experimental import pallas as pl
from jax.experimental.pallas import tpu as pltpu
from jax.sharding import PartitionSpec as P

HD = 128
W1 = 512
W2 = 32
GROUP = 2


def from_behind(value, axis, steps):
    count = lax.axis_size(axis)
    initial, last = (max(0, -steps), min(count, count - steps))
    return lax.ppermute(value, axis, [(source, source + steps) for source in range(initial, last)])


def swap(value, axis, bit):
    count = lax.axis_size(axis)
    return lax.ppermute(value, axis, [(source, source ^ (1 << bit)) for source in range(count)])


def pick(value, place, dim):
    return lax.dynamic_index_in_dim(value, place, dim, keepdims=False)


def sum_to_owner(value, axis):
    count = lax.axis_size(axis)
    if count & (count - 1):
        return lax.psum_scatter(value, axis, scatter_dimension=0, tiled=True)
    place = lax.axis_index(axis)
    value = value.reshape(count, value.shape[0] // count, value.shape[1])
    for bit in range(count.bit_length() - 1):
        value = value.reshape(value.shape[0] // 2, 2, *value.shape[1:])
        mine = (place >> bit) & 1
        value = pick(value, mine, 1) + swap(
            pick(value, 1 - mine, 1).astype(jnp.bfloat16), axis, bit
        ).astype(jnp.float32)
    return value[0]


def share_rows(value, axis):
    count = lax.axis_size(axis)
    if count & (count - 1):
        return lax.all_gather(value, axis, axis=0, tiled=True)
    place = lax.axis_index(axis)
    rows, width = value.shape
    value = value[None]
    for bit in reversed(range(count.bit_length() - 1)):
        mine = (place >> bit) & 1
        other = swap(value, axis, bit)
        value = jnp.where(mine == 0, jnp.stack([value, other], 1), jnp.stack([other, value], 1))
        value = value.reshape(-1, rows, width)
    return value.reshape(-1, width)


def attention_kernel(
    place, q_ref, k1_ref, v1_ref, k2_ref, v2_ref, out_ref,
    query, last_key, first_key, key_diag, value_diag, column, order, result, scores, peaks,
):
    tokens = q_ref.shape[0]
    blocks = k1_ref.shape[0] // tokens
    pairs = q_ref.shape[1] // (2 * HD)
    lines = query.shape[1]
    rows = lines * W2
    rate = HD ** -0.5 * math.log2(math.e)
    slab = place[0]

    def twice(x):
        return jnp.concatenate([x, x], axis=-1)

    def diag(x):
        zero = jnp.zeros_like(x)
        return jnp.concatenate(
            [jnp.concatenate([x, zero], axis=1), jnp.concatenate([zero, x], axis=1)], axis=0
        )

    if lines > pairs:
        query[...] = jnp.zeros(query.shape, query.dtype)
    for pair in range(pairs):
        query[:, pair, :] = q_ref[:, pair * 2 * HD:(pair + 1) * 2 * HD].astype(jnp.float32)
    first_key[...] = k1_ref[:tokens, :].T
    last_key[...] = k1_ref[(blocks - 1) * tokens:, :].T
    for j in range(blocks - 1):
        value_diag[j] = diag(v1_ref[j * tokens:(j + 1) * tokens, :])
        if j > 0:
            key_diag[j - 1] = diag(k1_ref[j * tokens:(j + 1) * tokens, :].T)
    order[...] = lax.broadcasted_iota(jnp.int32, order.shape, 0).astype(jnp.float32).astype(order.dtype)
    column[...] = lax.broadcasted_iota(jnp.int32, column.shape, 1).astype(jnp.float32).astype(column.dtype)

    def score(position, slot, full):
        line = query[position]
        line = jnp.concatenate([line] * (16 // lines), axis=0).astype(jnp.bfloat16)
        mixed = []
        for start in range(0, W2, 16 // lines):
            near = [
                jnp.broadcast_to(k2_ref[pl.ds(position + 1 + start + step, 1), :], (lines, HD))
                for step in range(16 // lines)
            ]
            mixed.append(line * twice(jnp.concatenate(near, axis=0).astype(jnp.bfloat16)))
        mixed = jnp.concatenate(mixed, axis=0)
        here = jnp.broadcast_to(position, (16, tokens)).astype(jnp.float32).astype(jnp.bfloat16)
        late = jnp.concatenate([column[...] <= here] * (HD // 16), axis=0)
        if not full:
            shown = lax.broadcasted_iota(jnp.int32, (W2, 1, 1), 0) + (slab * tokens + position - W2 + 1)
            shown = jnp.where(shown >= 0, 0.0, -jnp.inf)
            allowed = lax.broadcasted_iota(jnp.int32, (1, 2 * tokens), 1) % tokens <= position
            allowed = jnp.where(allowed, 0.0, -jnp.inf)
        peak = None
        for j in range(blocks - 1):
            if j == 0:
                weights = diag(jnp.where(late, last_key[...], first_key[...]))
            else:
                weights = key_diag[j - 1]
            part = jnp.dot(mixed, weights, preferred_element_type=jnp.float32)
            if not full:
                bias = jnp.where(slab + j >= blocks - 1, 0.0, -jnp.inf)
                bias = jnp.maximum(bias, allowed) if j == 0 else jnp.broadcast_to(bias, allowed.shape)
                part = (part.reshape(W2, lines, 2 * tokens) + (shown + bias[None])).reshape(part.shape)
            scores[slot, j] = part
            high = jnp.max(part.reshape(W2, lines, 2 * tokens), axis=0)
            peak = high if peak is None else jnp.maximum(peak, high)
        left = jnp.max(peak[:, :tokens], axis=1, keepdims=True) * rate
        right = jnp.max(peak[:, tokens:], axis=1, keepdims=True) * rate
        peaks[slot] = jnp.concatenate(
            [jnp.broadcast_to(left, (lines, tokens)), jnp.broadcast_to(right, (lines, tokens))], axis=1
        )

    def blend(position, slot):
        base = pl.multiple_of(position // 16 * 16, 16)
        far = pl.multiple_of((blocks - 1) * tokens + base, 16)
        late = order[...] <= jnp.broadcast_to(position - base, (16, HD)).astype(jnp.float32).astype(jnp.bfloat16)
        value = jnp.where(late, v1_ref[pl.ds(far, 16), :], v1_ref[pl.ds(base, 16), :])
        value_diag[0, pl.ds(base, 16), :HD] = value
        value_diag[0, pl.ds(pl.multiple_of(tokens + base, 16), 16), HD:] = value
        peak = peaks[slot][None]
        blended = total = None
        for j in range(blocks - 1):
            part = scores[slot, j].reshape(W2, lines, 2 * tokens)
            part = jnp.exp2(part * rate - peak)
            add = jnp.sum(part, axis=0)
            total = add if total is None else total + add
            part = jnp.dot(
                part.reshape(rows, 2 * tokens).astype(jnp.bfloat16), value_diag[j],
                preferred_element_type=jnp.float32,
            )
            blended = part if blended is None else blended + part
        acc = None
        for step in range(W2):
            near = jnp.broadcast_to(v2_ref[pl.ds(position + 1 + step, 1), :], (lines, HD))
            part = twice(near) * blended[step * lines:(step + 1) * lines]
            acc = part if acc is None else acc + part
        left = jnp.sum(total[:, :tokens], axis=1, keepdims=True)
        right = jnp.sum(total[:, tokens:], axis=1, keepdims=True)
        result[position] = jnp.concatenate([acc[:, :HD] / left, acc[:, HD:] / right], axis=1)

    def run(full):
        for step in range(GROUP):
            score(step, step, full)

        def trip(index, _):
            for half in range(2):
                first = (2 * index + half) * GROUP
                for step in range(GROUP):
                    ahead = jnp.minimum(first + GROUP + step, tokens - 1)
                    score(ahead, (1 - half) * GROUP + step, full)
                    blend(first + step, half * GROUP + step)
            return 0

        lax.fori_loop(0, tokens // (2 * GROUP), trip, 0)

    @pl.when(slab >= blocks - 1)
    def _():
        run(True)

    @pl.when(slab < blocks - 1)
    def _():
        run(False)

    for pair in range(pairs):
        out_ref[:, pair * 2 * HD:(pair + 1) * 2 * HD] = result[:, pair, :].astype(out_ref.dtype)


def attention_of(place, queries, extended_one, extended_two):
    tokens, width = queries.shape
    blocks = extended_one.shape[0] // tokens
    pairs = width // (2 * HD)
    lines = -(-pairs // 8) * 8
    rows = lines * W2
    vmem = pl.BlockSpec(memory_space=pltpu.VMEM)
    return pl.pallas_call(
        attention_kernel,
        out_shape=jax.ShapeDtypeStruct((tokens, width), jnp.bfloat16),
        in_specs=[pl.BlockSpec(memory_space=pltpu.SMEM)] + [vmem] * 5,
        out_specs=vmem,
        scratch_shapes=[
            pltpu.VMEM((tokens, lines, 2 * HD), jnp.float32),
            pltpu.VMEM((HD, tokens), jnp.bfloat16),
            pltpu.VMEM((HD, tokens), jnp.bfloat16),
            pltpu.VMEM((blocks - 2, 2 * HD, 2 * tokens), jnp.bfloat16),
            pltpu.VMEM((blocks - 1, 2 * tokens, 2 * HD), jnp.bfloat16),
            pltpu.VMEM((16, tokens), jnp.bfloat16),
            pltpu.VMEM((16, HD), jnp.bfloat16),
            pltpu.VMEM((tokens, lines, 2 * HD), jnp.float32),
            pltpu.VMEM((2 * GROUP, blocks - 1, rows, 2 * tokens), jnp.float32),
            pltpu.VMEM((2 * GROUP, lines, 2 * tokens), jnp.float32),
        ],
        compiler_params=pltpu.CompilerParams(vmem_limit_bytes=48 * 1024 * 1024),
        name="attention",
    )(
        place,
        queries,
        extended_one[:, :HD],
        extended_one[:, HD:],
        extended_two[:, :HD].astype(jnp.float32),
        extended_two[:, HD:].astype(jnp.float32),
    )


def body(hidden_in, query_weight, shared_weight, out_weight, residual, norm_gain):
    tokens = hidden_in.shape[0]
    queries = jnp.dot(hidden_in, query_weight, preferred_element_type=jnp.float32).astype(
        jnp.bfloat16
    )
    local_part = jnp.dot(hidden_in, shared_weight, preferred_element_type=jnp.float32).astype(
        jnp.bfloat16
    )
    shared = lax.all_gather(local_part, "head", axis=1, tiled=True)
    first_pair = shared[:, : 2 * HD]
    second_pair = shared[:, 2 * HD :]
    reach = (W1 + tokens - 1) // tokens
    earlier, rim = from_behind((first_pair, second_pair[tokens - W2 :]), "ctx", 1)
    pieces = [earlier]
    for distance in range(2, reach + 1):
        pieces.append(from_behind(first_pair, "ctx", distance))
    extended_one = jnp.concatenate(pieces[::-1] + [first_pair], 0)
    extended_two = jnp.concatenate([rim, second_pair], 0)
    place = lax.axis_index("ctx").astype(jnp.int32).reshape(1)
    attention = attention_of(place, queries, extended_one, extended_two)
    summed = sum_to_owner(
        jnp.dot(attention, out_weight, preferred_element_type=jnp.float32), "head"
    )
    residual_out = (residual.astype(jnp.float32) + summed).astype(jnp.bfloat16)
    values = residual_out.astype(jnp.float32)
    scale = lax.rsqrt(jnp.mean(values * values, axis=1, keepdims=True) + 1e-05)
    normed_local = (values * scale * norm_gain).astype(jnp.bfloat16)
    normed = share_rows(normed_local, "head")
    return (residual_out, normed)


def solution(mesh):
    in_specs = (
        P("ctx", None),
        P(None, "head"),
        P(None, "head"),
        P("head", None),
        P(("ctx", "head"), None),
        P(),
    )
    out_specs = (P(("ctx", "head"), None), P("ctx", None))
    return jax.shard_map(body, mesh=mesh, in_specs=in_specs, out_specs=out_specs, check_vma=False)
```

time: 137 us -> 127 us (0.927)
  Pallas kernels: 67.3 us -> 57.5 us
    pallas_call x1, Pallas kernels: 67.3 us -> 57.5 us  [attention_of(): pl.pallas_call(attention_kernel, out_shape=jax.ShapeDtypeStruct((tokens,...]
  transfers between devices with their start and end apart: 9 -> 9, of which waited for: 4 -> 4; matrix products, arithmetic and copies ran while one was open for 6% -> 7% of each run, Pallas kernels for 0% -> 0%
where the time goes in v3:
time: 127 us; the launch traced here: 126 us
  Pallas kernels  57.5 us (45%)
  starting transfers between devices  19.6 us (15%)
  matrix products  17.9 us (14%)
  waiting for transfers between devices  16.9 us (13%)
  blocking collectives  6.58 us (5%)
  local copies, waits for them, and re-layouts  4.2 us (3%)
  other arithmetic  2.87 us (2%)
    pallas_call x1, Pallas kernels, attention_of(): pl.pallas_call(attention_kernel, out_shape=jax.ShapeDtypeStruct((tokens,...  57.5 us
    ppermute x4, waiting for transfers between devices, swap(): lax.ppermute(value, axis, [(source, source ^ 1 << bit) for source in rang...  16.9 us
    ppermute x5, starting transfers between devices, from_behind(): lax.ppermute(value, axis, [(source, source + steps) for source in range(i...  16.4 us
    dot_general x1, matrix products, body(): jnp.dot(hidden_in, query_weight, preferred_element_type=jnp.float32)  8.11 us
    dot_general x1, matrix products, body(): jnp.dot(attention, out_weight, preferred_element_type=jnp.float32)  8.1 us
    all_gather x1, blocking collectives, body(): shared = lax.all_gather(local_part, 'head', axis=1, tiled=True)  6.58 us
    ppermute x4, starting transfers between devices, swap(): lax.ppermute(value, axis, [(source, source ^ 1 << bit) for source in rang...  3.24 us
  transfers between devices with their start and end apart: 9, of which 4 were waited for; matrix products, arithmetic and copies ran while one was open for 7% of the time, Pallas kernels for 0%

profile of v3, /device:TPU:0, one launch (start us, length us, event | category | flops | bytes accessed | tf_op | source)
XLA Modules:
  0.0 126.4 jit_solution(8037443314602333082)
XLA Ops:
  0.6 0.0 copy-start
  0.6 1.2 copy-done
  1.9 1.6 %convolution_convert_fusion.1 = bf16[128,128]{1,0:T(8,128)(2,1)S(1)} fusion(bf16[128,4096]{1,0:T(8,128)(2,1)S(1)} %copy-done, bf16[4096,128]{1,0:T(8,128)(2,1)} %param.8), kind=kOutput, calls=%fused_computation.1 | convolution fusion | flops 134234112 | bytes 2129920 | tf_op jit(solution)/shard_map/dot_general | solution.py:229
  3.5 6.6 %all_gather.3 = bf16[128,512]{1,0:T(8,128)(2,1)S(1)} all-gather(bf16[128,128]{1,0:T(8,128)(2,1)S(1)} %convolution_convert_fusion.1), channel_id=1, replica_groups=mesh['ctx'=8,'head'=4] {'head'}, dimensions={1}, use_global_device_ids=true | all-gather | bytes 163840 | tf_op jit(solution)/shard_map/all_gather | solution.py:232
  10.1 4.8 %collective-permute-start = (bf16[128,256]{1,0:T(8,128)(2,1)S(1)}, bf16[128,256]{1,0:T(8,128)(2,1)S(1)}, u32[]{:S(2)}, u32[]{:S(2)}) collective-permute-start(bf16[128,256]{1,0:T(8,128)(2,1)S(1)} %slice.29), channel_id=1, source_target_pairs={{0,16},{4,20},{8,24},{12,28},{1,17},{5,21},{9,25},{13,29},{2,18},{... | collective-permute-start | bytes 196616 | tf_op jit(solution)/shard_map/ppermute | solution.py:19
  14.9 4.4 %collective-permute-start.1 = (bf16[128,256]{1,0:T(8,128)(2,1)S(1)}, bf16[128,256]{1,0:T(8,128)(2,1)S(1)}, u32[]{:S(2)}, u32[]{:S(2)}) collective-permute-start(bf16[128,256]{1,0:T(8,128)(2,1)S(1)} %slice.29), channel_id=1, source_target_pairs={{0,12},{4,16},{8,20},{12,24},{16,28},{1,13},{5,17},{9,21},{13,25},... | collective-permute-start | bytes 196616 | tf_op jit(solution)/shard_map/ppermute | solution.py:19
  19.4 1.3 %collective-permute-start.2 = (bf16[128,256]{1,0:T(8,128)(2,1)S(1)}, bf16[128,256]{1,0:T(8,128)(2,1)S(1)}, u32[]{:S(2)}, u32[]{:S(2)}) collective-permute-start(bf16[128,256]{1,0:T(8,128)(2,1)S(1)} %slice.29), channel_id=1, source_target_pairs={{0,8},{4,12},{8,16},{12,20},{16,24},{20,28},{1,9},{5,13},{9,17},{1... | collective-permute-start | bytes 196616 | tf_op jit(solution)/shard_map/ppermute | solution.py:19
  20.7 3.1 %collective-permute-start.3 = (bf16[128,256]{1,0:T(8,128)(2,1)S(1)}, bf16[128,256]{1,0:T(8,128)(2,1)S(1)}, u32[]{:S(2)}, u32[]{:S(2)}) collective-permute-start(bf16[128,256]{1,0:T(8,128)(2,1)S(1)} %slice.29), channel_id=1, source_target_pairs={{0,4},{4,8},{8,12},{12,16},{16,20},{20,24},{24,28},{1,5},{5,9},{9,... | collective-permute-start | bytes 196616 | tf_op jit(solution)/shard_map/ppermute | solution.py:19
  23.8 2.7 %collective-permute-start.4 = (bf16[32,256]{1,0:T(8,128)(2,1)S(1)}, bf16[32,256]{1,0:T(8,128)(2,1)S(1)}, u32[]{:S(2)}, u32[]{:S(2)}) collective-permute-start(bf16[32,256]{1,0:T(8,128)(2,1)S(1)} %slice.32), channel_id=1, source_target_pairs={{0,4},{4,8},{8,12},{12,16},{16,20},{20,24},{24,28},{1,5},{5,9},{9,... | collective-permute-start | bytes 49160 | tf_op jit(solution)/shard_map/ppermute | solution.py:19
  26.5 8.1 %convolution_convert_fusion.q_ref = bf16[128,2048]{1,0:T(8,128)(2,1)S(1)} fusion(bf16[128,4096]{1,0:T(8,128)(2,1)S(1)} %copy-done, bf16[4096,2048]{1,0:T(8,128)(2,1)} %param.7), kind=kOutput, calls=%fused_computation | convolution fusion | flops 2147745792 | bytes 18350080 | tf_op jit(solution)/shard_map/dot_general | solution.py:226
  34.6 0.0 copy-start.3
  34.6 0.0 copy-start.4
  34.7 0.0 collective-permute-done
  34.7 0.0 collective-permute-done.1
  34.7 0.0 collective-permute-done.2
  34.7 0.0 collective-permute-done.3
  34.8 0.0 collective-permute-done.4
  34.8 57.5 %attention.1 = bf16[128,2048]{1,0:T(8,128)(2,1)S(1)} custom-call(s32[1]{0:T(128)} %bitcast.place, bf16[128,2048]{1,0:T(8,128)(2,1)S(1)} %convolution_convert_fusion.q_ref, bf16[640,128]{1,0:T(8,128)(2,1)S(1)} %get-tuple-element.5.k1_ref, bf16[640,128]{1,0:T(8,128)(2,1)S(1)} %get-tuple-element.4.v1_ref, f32[160,128]{1,0:T(8,128)S(1)} %get-tuple-element.11.k2_ref, ...), custom_call_target="tpu_custom_call" | custom-call | tf_op jit(solution)/shard_map/attention/pallas_call | solution.py:195
  92.3 8.1 %fusion.13 = f32[128,4096]{1,0:T(8,128)S(1)} fusion(bf16[128,2048]{1,0:T(8,128)(2,1)S(1)} %attention.1, bf16[2048,4096]{1,0:T(8,128)(2,1)} %param.9), kind=kOutput, calls=%fused_computation.32 | convolution fusion | flops 2147483648 | bytes 19398656 | tf_op jit(solution)/shard_map/dot_general | solution.py:245
  100.4 0.9 fusion.3
  101.3 0.0 collective-permute-start.5
  101.3 2.2 %collective-permute-done.5 = bf16[2,32,4096]{2,1,0:T(8,128)(2,1)} collective-permute-done((bf16[2,32,4096]{2,1,0:T(8,128)(2,1)}, bf16[2,32,4096]{2,1,0:T(8,128)(2,1)}, u32[]{:S(2)}, u32[]{:S(2)}) %collective-permute-start.5) | collective-permute-done | bytes 524320 | tf_op jit(solution)/shard_map/ppermute | solution.py:24
  103.5 1.1 bitcast_add_fusion
  104.7 0.0 copy-start.1
  104.7 1.0 copy-done.1
  105.7 1.6 %collective-permute-start.6 = (bf16[1,32,4096]{2,1,0:T(8,128)(2,1)S(1)}, bf16[1,32,4096]{2,1,0:T(8,128)(2,1)S(1)}, u32[]{:S(2)}, u32[]{:S(2)}) collective-permute-start(bf16[1,32,4096]{2,1,0:T(8,128)(2,1)S(1)} %dynamic-slice_convert_fusion), channel_id=1, source_target_pairs={{0,2},{1,3},{2,0},{3,1},{4,6},{5,7},{6,4},{7,5},{8,10},{9,11},{10,... | collective-permute-start | bytes 786440 | tf_op jit(solution)/shard_map/ppermute | solution.py:24
  107.3 6.8 %collective-permute-done.6 = bf16[1,32,4096]{2,1,0:T(8,128)(2,1)S(1)} collective-permute-done((bf16[1,32,4096]{2,1,0:T(8,128)(2,1)S(1)}, bf16[1,32,4096]{2,1,0:T(8,128)(2,1)S(1)}, u32[]{:S(2)}, u32[]{:S(2)}) %collective-permute-start.6) | collective-permute-done | bytes 262176 | tf_op jit(solution)/shard_map/ppermute | solution.py:24
  114.1 0.0 copy-done.3
  114.1 1.3 fusion
  115.4 0.0 copy-start.2
  115.4 0.0 copy-done.4
  115.4 0.1 fusion.6
  115.5 1.6 %collective-permute-start.7 = (bf16[1,32,4096]{2,1,0:T(8,128)(2,1)S(1)}, bf16[1,32,4096]{2,1,0:T(8,128)(2,1)S(1)}, u32[]{:S(2)}, u32[]{:S(2)}) collective-permute-start(bf16[1,32,4096]{2,1,0:T(8,128)(2,1)S(1)} %get-tuple-element.7), channel_id=1, source_target_pairs={{0,2},{1,3},{2,0},{3,1},{4,6},{5,7},{6,4},{7,5},{8,10},{9,11},{10,... | collective-permute-start | bytes 786440 | tf_op jit(solution)/shard_map/ppermute | solution.py:24
  117.1 6.0 %collective-permute-done.7 = bf16[1,32,4096]{2,1,0:T(8,128)(2,1)S(1)} collective-permute-done((bf16[1,32,4096]{2,1,0:T(8,128)(2,1)S(1)}, bf16[1,32,4096]{2,1,0:T(8,128)(2,1)S(1)}, u32[]{:S(2)}, u32[]{:S(2)}) %collective-permute-start.7) | collective-permute-done | bytes 262176 | tf_op jit(solution)/shard_map/ppermute | solution.py:24
  123.1 0.1 maximum_select_fusion.2
  123.2 0.1 collective-permute-start.8
  123.3 0.1 maximum_select_fusion.1
  123.3 1.8 %collective-permute-done.8 = bf16[2,32,4096]{2,1,0:T(8,128)(2,1)S(1)} collective-permute-done((bf16[2,32,4096]{2,1,0:T(8,128)(2,1)S(1)}, bf16[2,32,4096]{2,1,0:T(8,128)(2,1)S(1)}, u32[]{:S(2)}, u32[]{:S(2)}) %collective-permute-start.8) | collective-permute-done | bytes 524320 | tf_op jit(solution)/shard_map/ppermute | solution.py:24
  125.1 0.2 maximum_select_fusion
  125.3 1.0 copy.9
  126.4 0.0 copy-done.2
  (11 shorter events, 0.1 us)
Async XLA Ops:
  0.6 1.2 copy-start
  10.1 24.6 %collective-permute-start = (bf16[128,256]{1,0:T(8,128)(2,1)S(1)}, bf16[128,256]{1,0:T(8,128)(2,1)S(1)}, u32[]{:S(2)}, u32[]{:S(2)}) collective-permute-start(bf16[128,256]{1,0:T(8,128)(2,1)S(1)} %slice.29), channel_id=1, source_target_pairs={{0,16},{4,20},{8,24},{12,28},{1,17},{5,21},{9,25},{13,29},{2,18},{... | collective-permute-start | bytes 196616 | tf_op jit(solution)/shard_map/ppermute | solution.py:19
  14.9 19.8 %collective-permute-start.1 = (bf16[128,256]{1,0:T(8,128)(2,1)S(1)}, bf16[128,256]{1,0:T(8,128)(2,1)S(1)}, u32[]{:S(2)}, u32[]{:S(2)}) collective-permute-start(bf16[128,256]{1,0:T(8,128)(2,1)S(1)} %slice.29), channel_id=1, source_target_pairs={{0,12},{4,16},{8,20},{12,24},{16,28},{1,13},{5,17},{9,21},{13,25},... | collective-permute-start | bytes 196616 | tf_op jit(solution)/shard_map/ppermute | solution.py:19
  19.4 15.4 %collective-permute-start.2 = (bf16[128,256]{1,0:T(8,128)(2,1)S(1)}, bf16[128,256]{1,0:T(8,128)(2,1)S(1)}, u32[]{:S(2)}, u32[]{:S(2)}) collective-permute-start(bf16[128,256]{1,0:T(8,128)(2,1)S(1)} %slice.29), channel_id=1, source_target_pairs={{0,8},{4,12},{8,16},{12,20},{16,24},{20,28},{1,9},{5,13},{9,17},{1... | collective-permute-start | bytes 196616 | tf_op jit(solution)/shard_map/ppermute | solution.py:19
  20.7 14.1 %collective-permute-start.3 = (bf16[128,256]{1,0:T(8,128)(2,1)S(1)}, bf16[128,256]{1,0:T(8,128)(2,1)S(1)}, u32[]{:S(2)}, u32[]{:S(2)}) collective-permute-start(bf16[128,256]{1,0:T(8,128)(2,1)S(1)} %slice.29), channel_id=1, source_target_pairs={{0,4},{4,8},{8,12},{12,16},{16,20},{20,24},{24,28},{1,5},{5,9},{9,... | collective-permute-start | bytes 196616 | tf_op jit(solution)/shard_map/ppermute | solution.py:19
  23.8 11.0 %collective-permute-start.4 = (bf16[32,256]{1,0:T(8,128)(2,1)S(1)}, bf16[32,256]{1,0:T(8,128)(2,1)S(1)}, u32[]{:S(2)}, u32[]{:S(2)}) collective-permute-start(bf16[32,256]{1,0:T(8,128)(2,1)S(1)} %slice.32), channel_id=1, source_target_pairs={{0,4},{4,8},{8,12},{12,16},{16,20},{20,24},{24,28},{1,5},{5,9},{9,... | collective-permute-start | bytes 49160 | tf_op jit(solution)/shard_map/ppermute | solution.py:19
  34.6 79.5 %copy-start.3 = (bf16[32,4096]{1,0:T(8,128)(2,1)S(1)}, bf16[32,4096]{1,0:T(8,128)(2,1)}, u32[]{:S(2)}) copy-start(bf16[32,4096]{1,0:T(8,128)(2,1)} %param.10) | copy-start | bytes 786436
  34.6 80.7 %copy-start.4 = (f32[4096]{0:T(1024)S(1)}, f32[4096]{0:T(1024)}, u32[]{:S(2)}) copy-start(f32[4096]{0:T(1024)} %param.11) | copy-start | bytes 49156
  101.3 2.3 %collective-permute-start.5 = (bf16[2,32,4096]{2,1,0:T(8,128)(2,1)}, bf16[2,32,4096]{2,1,0:T(8,128)(2,1)}, u32[]{:S(2)}, u32[]{:S(2)}) collective-permute-start(bf16[2,32,4096]{2,1,0:T(8,128)(2,1)} %fusion.3), channel_id=1, source_target_pairs={{0,1},{1,0},{2,3},{3,2},{4,5},{5,4},{6,7},{7,6},{8,9},{9,8},{10,11... | collective-permute-start | bytes 1572872 | tf_op jit(solution)/shard_map/ppermute | solution.py:24
  104.7 1.0 copy-start.1
  105.7 8.4 %collective-permute-start.6 = (bf16[1,32,4096]{2,1,0:T(8,128)(2,1)S(1)}, bf16[1,32,4096]{2,1,0:T(8,128)(2,1)S(1)}, u32[]{:S(2)}, u32[]{:S(2)}) collective-permute-start(bf16[1,32,4096]{2,1,0:T(8,128)(2,1)S(1)} %dynamic-slice_convert_fusion), channel_id=1, source_target_pairs={{0,2},{1,3},{2,0},{3,1},{4,6},{5,7},{6,4},{7,5},{8,10},{9,11},{10,... | collective-permute-start | bytes 786440 | tf_op jit(solution)/shard_map/ppermute | solution.py:24
  115.4 11.0 %copy-start.2 = (bf16[32,4096]{1,0:T(8,128)(2,1)}, bf16[32,4096]{1,0:T(8,128)(2,1)S(1)}, u32[]{:S(2)}) copy-start(bf16[32,4096]{1,0:T(8,128)(2,1)S(1)} %get-tuple-element.3) | copy-start | bytes 786436
  115.5 7.6 %collective-permute-start.7 = (bf16[1,32,4096]{2,1,0:T(8,128)(2,1)S(1)}, bf16[1,32,4096]{2,1,0:T(8,128)(2,1)S(1)}, u32[]{:S(2)}, u32[]{:S(2)}) collective-permute-start(bf16[1,32,4096]{2,1,0:T(8,128)(2,1)S(1)} %get-tuple-element.7), channel_id=1, source_target_pairs={{0,2},{1,3},{2,0},{3,1},{4,6},{5,7},{6,4},{7,5},{8,10},{9,11},{10,... | collective-permute-start | bytes 786440 | tf_op jit(solution)/shard_map/ppermute | solution.py:24
  123.2 2.0 %collective-permute-start.8 = (bf16[2,32,4096]{2,1,0:T(8,128)(2,1)S(1)}, bf16[2,32,4096]{2,1,0:T(8,128)(2,1)S(1)}, u32[]{:S(2)}, u32[]{:S(2)}) collective-permute-start(bf16[2,32,4096]{2,1,0:T(8,128)(2,1)S(1)} %maximum_select_fusion.2), channel_id=1, source_target_pairs={{0,1},{1,0},{2,3},{3,2},{4,5},{5,4},{6,7},{7,6},{8,9},{9,8},{10,11... | collective-permute-start | bytes 1572872 | tf_op jit(solution)/shard_map/ppermute | solution.py:24

commit v4 on v3

--- a/solution.py
+++ b/solution.py
@@ -1,3 +1,4 @@
+import functools
 import math
 
 import jax
@@ -11,6 +12,7 @@
 W1 = 512
 W2 = 32
 GROUP = 2
+PIECES = 4
 
 
 def from_behind(value, axis, steps):
@@ -58,17 +60,98 @@
     return value.reshape(-1, width)
 
 
+def gather_columns(value):
+    count = value.shape[0] * value.shape[1]
+    return value.reshape(count, *value.shape[2:]).transpose(1, 0, 2).reshape(value.shape[2], -1)
+
+
+def place_pair(mine, value, other, dim):
+    return jnp.where(
+        mine == 0, jnp.concatenate([value, other], dim), jnp.concatenate([other, value], dim)
+    )
+
+
+def simple_window(local_part):
+    tokens = local_part.shape[0]
+    shared = lax.all_gather(local_part, "head", axis=1, tiled=True)
+    first_pair = shared[:, : 2 * HD]
+    second_pair = shared[:, 2 * HD :]
+    reach = W1 // tokens
+    earlier, rim = from_behind((first_pair, second_pair[tokens - W2 :]), "ctx", 1)
+    pieces = [earlier]
+    for distance in range(2, reach + 1):
+        pieces.append(from_behind(first_pair, "ctx", distance))
+    one = jnp.concatenate(pieces[::-1] + [first_pair], 0)
+    two = jnp.concatenate([rim, second_pair], 0)
+    return one[:, :HD], one[:, HD:], two[:, :HD], two[:, HD:]
+
+
+def window_of(local_part, source, work):
+    tokens = local_part.shape[0]
+    heads = lax.axis_size("head")
+    slab = lax.axis_index("ctx")
+    done = []
+
+    def beside(value):
+        nonlocal source
+        if work:
+            value, source = lax.optimization_barrier((value, source))
+            done.append(work.pop(0)(source))
+        return value
+
+    short = (
+        heads & (heads - 1) == 0 and heads >= 4 and lax.axis_size("ctx") % 2 == 0 and W1 == 4 * tokens
+    )
+    if not short:
+        out = simple_window(local_part)
+        while work:
+            done.append(work.pop(0)(source))
+        return out, jnp.int32(0), done
+
+    place = lax.axis_index("head")
+    done.append(work.pop(0)(source))
+    value = local_part[None]
+    for bit in reversed(range(1, heads.bit_length() - 1)):
+        other = swap(value, "head", bit)
+        value = jnp.stack(
+            [jnp.where((place >> bit) & 1 == 0, value, other), jnp.where((place >> bit) & 1 == 0, other, value)], 1
+        )
+        value = value.reshape(-1, *local_part.shape)
+    half = value.shape[0] // 2
+    first, second = value[:half], value[half:]
+
+    odd = slab & 1
+    rim = second[:, tokens - W2 :]
+    other = swap(beside(jnp.concatenate([first, rim], 1)), "ctx", 0)
+    other, other_rim = other[:, :tokens], other[:, tokens:]
+    pair = place_pair(odd, first, other, 1)
+    pair_rim = jnp.where(odd == 0, other_rim, rim)
+    behind = from_behind(beside(jnp.concatenate([pair, pair_rim], 1)), "ctx", 2)
+    behind, behind_rim = behind[:, : 2 * tokens], behind[:, 2 * tokens :]
+    further = from_behind(beside(behind), "ctx", 2)
+    rim = jnp.where(odd == 0, behind_rim, other_rim)
+    value = jnp.concatenate([further, behind, pair, rim, second], 1)
+    other = swap(beside(value), "head", 0)
+    value = place_pair(place & 1, value[:, None], other[:, None], 1)
+    one, two = value[:, :, : 6 * tokens], value[:, :, 6 * tokens :]
+    one, two = gather_columns(one), gather_columns(two)
+    while work:
+        done.append(work.pop(0)(source))
+    return (one[:, :HD], one[:, HD:], two[:, :HD], two[:, HD:]), odd, done
+
+
 def attention_kernel(
     place, q_ref, k1_ref, v1_ref, k2_ref, v2_ref, out_ref,
     query, last_key, first_key, key_diag, value_diag, column, order, result, scores, peaks,
 ):
     tokens = q_ref.shape[0]
-    blocks = k1_ref.shape[0] // tokens
+    blocks = W1 // tokens + 1
     pairs = q_ref.shape[1] // (2 * HD)
     lines = query.shape[1]
     rows = lines * W2
     rate = HD ** -0.5 * math.log2(math.e)
     slab = place[0]
+    start = pl.multiple_of(place[1] * tokens, tokens)
 
     def twice(x):
         return jnp.concatenate([x, x], axis=-1)
@@ -83,16 +166,24 @@
         query[...] = jnp.zeros(query.shape, query.dtype)
     for pair in range(pairs):
         query[:, pair, :] = q_ref[:, pair * 2 * HD:(pair + 1) * 2 * HD].astype(jnp.float32)
-    first_key[...] = k1_ref[:tokens, :].T
-    last_key[...] = k1_ref[(blocks - 1) * tokens:, :].T
-    for j in range(blocks - 1):
-        value_diag[j] = diag(v1_ref[j * tokens:(j + 1) * tokens, :])
-        if j > 0:
-            key_diag[j - 1] = diag(k1_ref[j * tokens:(j + 1) * tokens, :].T)
+    for j in range(blocks):
+        there = pl.ds(start + j * tokens, tokens)
+        key = k1_ref[there, :].T
+        if j < blocks - 1:
+            value_diag[j] = diag(v1_ref[there, :])
+        if j == 0:
+            first_key[...] = key
+        elif j == blocks - 1:
+            last_key[...] = key
+        else:
+            key_diag[j - 1] = diag(key)
     order[...] = lax.broadcasted_iota(jnp.int32, order.shape, 0).astype(jnp.float32).astype(order.dtype)
     column[...] = lax.broadcasted_iota(jnp.int32, column.shape, 1).astype(jnp.float32).astype(column.dtype)
 
-    def score(position, slot, full):
+    def used(behind):
+        return [0] + list(range(blocks - 1 - behind, blocks - 1))[-(blocks - 2):] if behind else [0]
+
+    def score(position, slot, behind):
         line = query[position]
         line = jnp.concatenate([line] * (16 // lines), axis=0).astype(jnp.bfloat16)
         mixed = []
@@ -105,22 +196,21 @@
         mixed = jnp.concatenate(mixed, axis=0)
         here = jnp.broadcast_to(position, (16, tokens)).astype(jnp.float32).astype(jnp.bfloat16)
         late = jnp.concatenate([column[...] <= here] * (HD // 16), axis=0)
-        if not full:
-            shown = lax.broadcasted_iota(jnp.int32, (W2, 1, 1), 0) + (slab * tokens + position - W2 + 1)
-            shown = jnp.where(shown >= 0, 0.0, -jnp.inf)
-            allowed = lax.broadcasted_iota(jnp.int32, (1, 2 * tokens), 1) % tokens <= position
-            allowed = jnp.where(allowed, 0.0, -jnp.inf)
+        if behind < blocks - 1:
+            bias = lax.broadcasted_iota(jnp.int32, (1, 2 * tokens), 1) % tokens <= position
+            bias = jnp.where(bias, 0.0, -jnp.inf)[None]
+            if behind * tokens < W2 - 1:
+                shown = lax.broadcasted_iota(jnp.int32, (W2, 1, 1), 0) + (position + behind * tokens)
+                bias = bias + jnp.where(shown >= W2 - 1, 0.0, -jnp.inf)
         peak = None
-        for j in range(blocks - 1):
+        for j in used(behind):
             if j == 0:
                 weights = diag(jnp.where(late, last_key[...], first_key[...]))
             else:
                 weights = key_diag[j - 1]
             part = jnp.dot(mixed, weights, preferred_element_type=jnp.float32)
-            if not full:
-                bias = jnp.where(slab + j >= blocks - 1, 0.0, -jnp.inf)
-                bias = jnp.maximum(bias, allowed) if j == 0 else jnp.broadcast_to(bias, allowed.shape)
-                part = (part.reshape(W2, lines, 2 * tokens) + (shown + bias[None])).reshape(part.shape)
+            if j == 0 and behind < blocks - 1:
+                part = (part.reshape(W2, lines, 2 * tokens) + bias).reshape(part.shape)
             scores[slot, j] = part
             high = jnp.max(part.reshape(W2, lines, 2 * tokens), axis=0)
             peak = high if peak is None else jnp.maximum(peak, high)
@@ -130,16 +220,17 @@
             [jnp.broadcast_to(left, (lines, tokens)), jnp.broadcast_to(right, (lines, tokens))], axis=1
         )
 
-    def blend(position, slot):
+    def blend(position, slot, behind):
         base = pl.multiple_of(position // 16 * 16, 16)
-        far = pl.multiple_of((blocks - 1) * tokens + base, 16)
+        close = pl.multiple_of(start + base, 16)
+        far = pl.multiple_of(start + (blocks - 1) * tokens + base, 16)
         late = order[...] <= jnp.broadcast_to(position - base, (16, HD)).astype(jnp.float32).astype(jnp.bfloat16)
-        value = jnp.where(late, v1_ref[pl.ds(far, 16), :], v1_ref[pl.ds(base, 16), :])
+        value = jnp.where(late, v1_ref[pl.ds(far, 16), :], v1_ref[pl.ds(close, 16), :])
         value_diag[0, pl.ds(base, 16), :HD] = value
         value_diag[0, pl.ds(pl.multiple_of(tokens + base, 16), 16), HD:] = value
         peak = peaks[slot][None]
         blended = total = None
-        for j in range(blocks - 1):
+        for j in used(behind):
             part = scores[slot, j].reshape(W2, lines, 2 * tokens)
             part = jnp.exp2(part * rate - peak)
             add = jnp.sum(part, axis=0)
@@ -158,36 +249,31 @@
         right = jnp.sum(total[:, tokens:], axis=1, keepdims=True)
         result[position] = jnp.concatenate([acc[:, :HD] / left, acc[:, HD:] / right], axis=1)
 
-    def run(full):
+    def run(behind):
         for step in range(GROUP):
-            score(step, step, full)
+            score(step, step, behind)
 
         def trip(index, _):
             for half in range(2):
                 first = (2 * index + half) * GROUP
                 for step in range(GROUP):
                     ahead = jnp.minimum(first + GROUP + step, tokens - 1)
-                    score(ahead, (1 - half) * GROUP + step, full)
-                    blend(first + step, half * GROUP + step)
+                    score(ahead, (1 - half) * GROUP + step, behind)
+                    blend(first + step, half * GROUP + step, behind)
             return 0
 
         lax.fori_loop(0, tokens // (2 * GROUP), trip, 0)
 
-    @pl.when(slab >= blocks - 1)
-    def _():
-        run(True)
-
-    @pl.when(slab < blocks - 1)
-    def _():
-        run(False)
+    for behind in range(blocks):
+        pl.when(jnp.minimum(slab, blocks - 1) == behind)(functools.partial(run, behind))
 
     for pair in range(pairs):
         out_ref[:, pair * 2 * HD:(pair + 1) * 2 * HD] = result[:, pair, :].astype(out_ref.dtype)
 
 
-def attention_of(place, queries, extended_one, extended_two):
+def attention_of(place, queries, key_one, value_one, key_two, value_two):
     tokens, width = queries.shape
-    blocks = extended_one.shape[0] // tokens
+    blocks = W1 // tokens + 1
     pairs = width // (2 * HD)
     lines = -(-pairs // 8) * 8
     rows = lines * W2
@@ -214,33 +300,29 @@
     )(
         place,
         queries,
-        extended_one[:, :HD],
-        extended_one[:, HD:],
-        extended_two[:, :HD].astype(jnp.float32),
-        extended_two[:, HD:].astype(jnp.float32),
+        key_one,
+        value_one,
+        key_two.astype(jnp.float32),
+        value_two.astype(jnp.float32),
     )
 
 
 def body(hidden_in, query_weight, shared_weight, out_weight, residual, norm_gain):
-    tokens = hidden_in.shape[0]
-    queries = jnp.dot(hidden_in, query_weight, preferred_element_type=jnp.float32).astype(
-        jnp.bfloat16
-    )
     local_part = jnp.dot(hidden_in, shared_weight, preferred_element_type=jnp.float32).astype(
         jnp.bfloat16
     )
-    shared = lax.all_gather(local_part, "head", axis=1, tiled=True)
-    first_pair = shared[:, : 2 * HD]
-    second_pair = shared[:, 2 * HD :]
-    reach = (W1 + tokens - 1) // tokens
-    earlier, rim = from_behind((first_pair, second_pair[tokens - W2 :]), "ctx", 1)
-    pieces = [earlier]
-    for distance in range(2, reach + 1):
-        pieces.append(from_behind(first_pair, "ctx", distance))
-    extended_one = jnp.concatenate(pieces[::-1] + [first_pair], 0)
-    extended_two = jnp.concatenate([rim, second_pair], 0)
-    place = lax.axis_index("ctx").astype(jnp.int32).reshape(1)
-    attention = attention_of(place, queries, extended_one, extended_two)
+    width = query_weight.shape[1] // PIECES
+
+    def project(piece, source):
+        weight = query_weight[:, piece * width : (piece + 1) * width]
+        return jnp.dot(source, weight, preferred_element_type=jnp.float32).astype(jnp.bfloat16)
+
+    window, start, queries = window_of(
+        local_part, hidden_in, [functools.partial(project, piece) for piece in range(PIECES)]
+    )
+    queries = jnp.concatenate(queries, axis=1)
+    place = jnp.stack([lax.axis_index("ctx"), start]).astype(jnp.int32)
+    attention = attention_of(place, queries, *window)
     summed = sum_to_owner(
         jnp.dot(attention, out_weight, preferred_element_type=jnp.float32), "head"
     )

time: 127 us -> 118 us (0.929)
  the two profiles are of different devices: /device:TPU:0 before, /device:TPU:11 now
where the time goes in v4:
time: 118 us
  Pallas kernels  54.6 us (46%)
  matrix products  21.4 us (18%)
  waiting for transfers between devices  19.4 us (16%)
  starting transfers between devices  14.2 us (12%)
  local copies, waits for them, and re-layouts  4.25 us (4%)
  other arithmetic  3.17 us (3%)
    pallas_call x1, Pallas kernels, attention_of(): pl.pallas_call(attention_kernel, out_shape=jax.ShapeDtypeStruct((tokens,...  54.6 us
    ppermute x7, waiting for transfers between devices, swap(): lax.ppermute(value, axis, [(source, source ^ 1 << bit) for source in rang...  19.4 us
    dot_general x4, matrix products, project(): jnp.dot(source, weight, preferred_element_type=jnp.float32)  11.6 us
    dot_general x1, matrix products, body(): jnp.dot(attention, out_weight, preferred_element_type=jnp.float32)  8.11 us
    ppermute x7, starting transfers between devices, swap(): lax.ppermute(value, axis, [(source, source ^ 1 << bit) for source in rang...  7.8 us
    ppermute x2, starting transfers between devices, from_behind(): lax.ppermute(value, axis, [(source, source + steps) for source in range(i...  6.41 us
  transfers between devices with their start and end apart: 9, of which 5 were waited for; matrix products, arithmetic and copies ran while one was open for 10% of the time, Pallas kernels for 0%

profile of v4, /device:TPU:11, one launch (start us, length us, event | category | flops | bytes accessed | tf_op | source)
XLA Modules:
  0.0 117.9 jit_solution(9500618738872725713)
XLA Ops:
  0.6 0.0 copy-start
  0.6 1.2 %copy-done = bf16[128,4096]{1,0:T(8,128)(2,1)S(1)} copy-done((bf16[128,4096]{1,0:T(8,128)(2,1)S(1)}, bf16[128,4096]{1,0:T(8,128)(2,1)}, u32[]{:S(2)}) %copy-start) | copy-done | bytes 1048600
  1.9 1.6 %fusion.20 = bf16[1,128,128]{2,1,0:T(8,128)(2,1)S(1)} fusion(bf16[128,4096]{1,0:T(8,128)(2,1)S(1)} %copy-done, bf16[4096,128]{1,0:T(8,128)(2,1)} %param.8), kind=kOutput, calls=%fused_computation.13 | convolution fusion | flops 134234112 | bytes 2129920 | tf_op jit(solution)/shard_map/dot_general | solution.py:311
  3.5 1.3 %collective-permute-start = (bf16[1,128,128]{2,1,0:T(8,128)(2,1)S(1)}, bf16[1,128,128]{2,1,0:T(8,128)(2,1)S(1)}, u32[]{:S(2)}, u32[]{:S(2)}) collective-permute-start(bf16[1,128,128]{2,1,0:T(8,128)(2,1)S(1)} %fusion.20), channel_id=1, source_target_pairs={{0,2},{1,3},{2,0},{3,1},{4,6},{5,7},{6,4},{7,5},{8,10},{9,11},{10,... | collective-permute-start | bytes 98312 | tf_op jit(solution)/shard_map/ppermute | solution.py:26
  4.8 2.9 %fusion.8 = bf16[128,512]{1,0:T(8,128)(2,1)S(1)} fusion(bf16[128,4096]{1,0:T(8,128)(2,1)S(1)} %copy-done, bf16[4096,2048]{1,0:T(8,128)(2,1)} %param.7), kind=kOutput, calls=%fused_computation.8 | convolution fusion | flops 536936448 | bytes 5373952 | tf_op jit(solution)/shard_map/dot_general | solution.py:318
  7.7 0.0 collective-permute-done
  7.8 0.3 collective-permute-start.1
  8.1 0.1 pad_add_fusion.place
  8.2 2.5 %collective-permute-done.1 = bf16[1,160,128]{2,1,0:T(8,128)(2,1)S(1)} collective-permute-done((bf16[1,160,128]{2,1,0:T(8,128)(2,1)S(1)}, bf16[1,160,128]{2,1,0:T(8,128)(2,1)S(1)}, u32[]{:S(2)}, u32[]{:S(2)}) %collective-permute-start.1) | collective-permute-done | bytes 40992 | tf_op jit(solution)/shard_map/ppermute | solution.py:26
  10.8 3.2 %collective-permute-start.2 = (bf16[1,288,128]{2,1,0:T(8,128)(2,1)S(1)}, bf16[1,288,128]{2,1,0:T(8,128)(2,1)S(1)}, u32[]{:S(2)}, u32[]{:S(2)}) collective-permute-start(bf16[1,288,128]{2,1,0:T(8,128)(2,1)S(1)} %pad_maximum_fusion.1), channel_id=1, source_target_pairs={{0,8},{4,12},{8,16},{12,20},{16,24},{20,28},{1,9},{5,13},{9,17},{1... | collective-permute-start | bytes 221192 | tf_op jit(solution)/shard_map/ppermute | solution.py:21
  14.0 2.9 %fusion.11 = bf16[128,512]{1,0:T(8,128)(2,1)S(1)} fusion(bf16[128,4096]{1,0:T(8,128)(2,1)S(1)} %copy-done, bf16[4096,2048]{1,0:T(8,128)(2,1)} %param.7), kind=kOutput, calls=%fused_computation.9 | convolution fusion | flops 536936448 | bytes 5373952 | tf_op jit(solution)/shard_map/dot_general | solution.py:318
  16.9 0.0 collective-permute-done.2
  16.9 3.2 %collective-permute-start.3 = (bf16[1,256,128]{2,1,0:T(8,128)(2,1)S(1)}, bf16[1,256,128]{2,1,0:T(8,128)(2,1)S(1)}, u32[]{:S(2)}, u32[]{:S(2)}) collective-permute-start(bf16[1,256,128]{2,1,0:T(8,128)(2,1)S(1)} %slice.67), channel_id=1, source_target_pairs={{0,8},{4,12},{8,16},{12,20},{16,24},{20,28},{1,9},{5,13},{9,17},{1... | collective-permute-start | bytes 196616 | tf_op jit(solution)/shard_map/ppermute | solution.py:21
  20.1 2.9 %fusion.14 = bf16[128,512]{1,0:T(8,128)(2,1)S(1)} fusion(bf16[128,4096]{1,0:T(8,128)(2,1)S(1)} %copy-done, bf16[4096,2048]{1,0:T(8,128)(2,1)} %param.7), kind=kOutput, calls=%fused_computation.10 | convolution fusion | flops 536936448 | bytes 5373952 | tf_op jit(solution)/shard_map/dot_general | solution.py:318
  23.1 0.0 collective-permute-done.3
  23.1 2.7 %collective-permute-start.4 = (bf16[1,928,128]{2,1,0:T(8,128)(2,1)S(1)}, bf16[1,928,128]{2,1,0:T(8,128)(2,1)S(1)}, u32[]{:S(2)}, u32[]{:S(2)}) collective-permute-start(bf16[1,928,128]{2,1,0:T(8,128)(2,1)S(1)} %constant_dynamic-update-slice_fusion), channel_id=1, source_target_pairs={{0,1},{1,0},{2,3},{3,2},{4,5},{5,4},{6,7},{7,6},{8,9},{9,8},{10,11... | collective-permute-start | bytes 712712 | tf_op jit(solution)/shard_map/ppermute | solution.py:26
  25.9 2.9 %fusion.17 = bf16[128,512]{1,0:T(8,128)(2,1)S(1)} fusion(bf16[128,4096]{1,0:T(8,128)(2,1)S(1)} %copy-done, bf16[4096,2048]{1,0:T(8,128)(2,1)} %param.7), kind=kOutput, calls=%fused_computation.11 | convolution fusion | flops 536936448 | bytes 5373952 | tf_op jit(solution)/shard_map/dot_general | solution.py:318
  28.8 0.0 copy-start.3
  28.9 0.0 collective-permute-done.4
  28.9 0.0 copy-start.4
  28.9 0.1 maximum_select_fusion.3
  29.1 54.6 %attention.1 = bf16[128,2048]{1,0:T(8,128)(2,1)S(1)} custom-call(s32[2]{0:T(128)S(1)} %pad_add_fusion.place, bf16[128,2048]{1,0:T(8,128)(2,1)S(1)} %pad_maximum_fusion.q_ref, bf16[768,128]{1,0:T(8,128)(2,1)S(1)} %get-tuple-element.17.k1_ref, bf16[768,128]{1,0:T(8,128)(2,1)S(1)} %get-tuple-element.16.v1_ref, f32[160,128]{1,0:T(8,128)S(1)} %get-tuple-element.21.k2_ref, ...), custom_call_target="tpu_custom_call" | custom-call | tf_op jit(solution)/shard_map/attention/pallas_call | solution.py:281
  83.6 8.1 %fusion.30 = f32[128,4096]{1,0:T(8,128)S(1)} fusion(bf16[128,2048]{1,0:T(8,128)(2,1)S(1)} %attention.1, bf16[2048,4096]{1,0:T(8,128)(2,1)} %param.9), kind=kOutput, calls=%fused_computation.53 | convolution fusion | flops 2147483648 | bytes 19398656 | tf_op jit(solution)/shard_map/dot_general | solution.py:327
  91.7 0.9 fusion.24
  92.6 0.0 collective-permute-start.5
  92.6 2.2 %collective-permute-done.5 = bf16[2,32,4096]{2,1,0:T(8,128)(2,1)} collective-permute-done((bf16[2,32,4096]{2,1,0:T(8,128)(2,1)}, bf16[2,32,4096]{2,1,0:T(8,128)(2,1)}, u32[]{:S(2)}, u32[]{:S(2)}) %collective-permute-start.5) | collective-permute-done | bytes 524320 | tf_op jit(solution)/shard_map/ppermute | solution.py:26
  94.8 1.2 bitcast_add_fusion
  96.0 0.0 copy-start.1
  96.0 1.0 copy-done.1
  97.0 0.8 collective-permute-start.6
  97.8 7.0 %collective-permute-done.6 = bf16[1,32,4096]{2,1,0:T(8,128)(2,1)S(1)} collective-permute-done((bf16[1,32,4096]{2,1,0:T(8,128)(2,1)S(1)}, bf16[1,32,4096]{2,1,0:T(8,128)(2,1)S(1)}, u32[]{:S(2)}, u32[]{:S(2)}) %collective-permute-start.6) | collective-permute-done | bytes 262176 | tf_op jit(solution)/shard_map/ppermute | solution.py:26
  104.8 0.0 copy-done.3
  104.8 1.3 %fusion.21 = (f32[32]{0:T(128)S(1)}, bf16[32,4096]{1,0:T(8,128)(2,1)S(1)}) fusion(bf16[1,32,4096]{2,1,0:T(8,128)(2,1)S(1)} %collective-permute-done.6, f32[2,32,4096]{2,1,0:T(8,128)} %copy-done.1, s32[]{:T(128)S(6)} %select_n.116, bf16[32,4096]{1,0:T(8,128)(2,1)S(1)} %copy-done.3), kind=kLoop, calls=%fused_computation.19 | loop fusion | flops 1048544 | bytes 1310852 | tf_op jit(solution)/shard_map/reduce_sum | solution.py:331
  106.1 0.0 copy-start.2
  106.1 0.0 copy-done.4
  106.1 0.1 fusion.27
  106.2 0.8 collective-permute-start.7
  107.0 6.2 %collective-permute-done.7 = bf16[1,32,4096]{2,1,0:T(8,128)(2,1)S(1)} collective-permute-done((bf16[1,32,4096]{2,1,0:T(8,128)(2,1)S(1)}, bf16[1,32,4096]{2,1,0:T(8,128)(2,1)S(1)}, u32[]{:S(2)}, u32[]{:S(2)}) %collective-permute-start.7) | collective-permute-done | bytes 262176 | tf_op jit(solution)/shard_map/ppermute | solution.py:26
  113.2 0.1 maximum_select_fusion.2
  113.3 1.9 %collective-permute-start.8 = (bf16[2,32,4096]{2,1,0:T(8,128)(2,1)S(1)}, bf16[2,32,4096]{2,1,0:T(8,128)(2,1)S(1)}, u32[]{:S(2)}, u32[]{:S(2)}) collective-permute-start(bf16[2,32,4096]{2,1,0:T(8,128)(2,1)S(1)} %maximum_select_fusion.2), channel_id=1, source_target_pairs={{0,1},{1,0},{2,3},{3,2},{4,5},{5,4},{6,7},{7,6},{8,9},{9,8},{10,11... | collective-permute-start | bytes 1572872 | tf_op jit(solution)/shard_map/ppermute | solution.py:26
  115.2 0.1 maximum_select_fusion.1
  115.3 1.5 %collective-permute-done.8 = bf16[2,32,4096]{2,1,0:T(8,128)(2,1)S(1)} collective-permute-done((bf16[2,32,4096]{2,1,0:T(8,128)(2,1)S(1)}, bf16[2,32,4096]{2,1,0:T(8,128)(2,1)S(1)}, u32[]{:S(2)}, u32[]{:S(2)}) %collective-permute-start.8) | collective-permute-done | bytes 524320 | tf_op jit(solution)/shard_map/ppermute | solution.py:26
  116.7 0.2 maximum_select_fusion
  116.9 1.0 copy.11
  117.9 0.0 copy-done.2
  (20 shorter events, 0.3 us)
Async XLA Ops:
  0.6 1.2 %copy-start = (bf16[128,4096]{1,0:T(8,128)(2,1)S(1)}, bf16[128,4096]{1,0:T(8,128)(2,1)}, u32[]{:S(2)}) copy-start(bf16[128,4096]{1,0:T(8,128)(2,1)} %param.6) | copy-start | bytes 3145732
  3.5 4.2 %collective-permute-start = (bf16[1,128,128]{2,1,0:T(8,128)(2,1)S(1)}, bf16[1,128,128]{2,1,0:T(8,128)(2,1)S(1)}, u32[]{:S(2)}, u32[]{:S(2)}) collective-permute-start(bf16[1,128,128]{2,1,0:T(8,128)(2,1)S(1)} %fusion.20), channel_id=1, source_target_pairs={{0,2},{1,3},{2,0},{3,1},{4,6},{5,7},{6,4},{7,5},{8,10},{9,11},{10,... | collective-permute-start | bytes 98312 | tf_op jit(solution)/shard_map/ppermute | solution.py:26
  7.8 2.9 %collective-permute-start.1 = (bf16[1,160,128]{2,1,0:T(8,128)(2,1)S(1)}, bf16[1,160,128]{2,1,0:T(8,128)(2,1)S(1)}, u32[]{:S(2)}, u32[]{:S(2)}) collective-permute-start(bf16[1,160,128]{2,1,0:T(8,128)(2,1)S(1)} %pad_maximum_fusion.2), channel_id=1, source_target_pairs={{0,4},{4,0},{8,12},{12,8},{16,20},{20,16},{24,28},{28,24},{1,5},{5... | collective-permute-start | bytes 122888 | tf_op jit(solution)/shard_map/ppermute | solution.py:26
  10.8 6.1 %collective-permute-start.2 = (bf16[1,288,128]{2,1,0:T(8,128)(2,1)S(1)}, bf16[1,288,128]{2,1,0:T(8,128)(2,1)S(1)}, u32[]{:S(2)}, u32[]{:S(2)}) collective-permute-start(bf16[1,288,128]{2,1,0:T(8,128)(2,1)S(1)} %pad_maximum_fusion.1), channel_id=1, source_target_pairs={{0,8},{4,12},{8,16},{12,20},{16,24},{20,28},{1,9},{5,13},{9,17},{1... | collective-permute-start | bytes 221192 | tf_op jit(solution)/shard_map/ppermute | solution.py:21
  16.9 6.1 %collective-permute-start.3 = (bf16[1,256,128]{2,1,0:T(8,128)(2,1)S(1)}, bf16[1,256,128]{2,1,0:T(8,128)(2,1)S(1)}, u32[]{:S(2)}, u32[]{:S(2)}) collective-permute-start(bf16[1,256,128]{2,1,0:T(8,128)(2,1)S(1)} %slice.67), channel_id=1, source_target_pairs={{0,8},{4,12},{8,16},{12,20},{16,24},{20,28},{1,9},{5,13},{9,17},{1... | collective-permute-start | bytes 196616 | tf_op jit(solution)/shard_map/ppermute | solution.py:21
  23.1 5.7 %collective-permute-start.4 = (bf16[1,928,128]{2,1,0:T(8,128)(2,1)S(1)}, bf16[1,928,128]{2,1,0:T(8,128)(2,1)S(1)}, u32[]{:S(2)}, u32[]{:S(2)}) collective-permute-start(bf16[1,928,128]{2,1,0:T(8,128)(2,1)S(1)} %constant_dynamic-update-slice_fusion), channel_id=1, source_target_pairs={{0,1},{1,0},{2,3},{3,2},{4,5},{5,4},{6,7},{7,6},{8,9},{9,8},{10,11... | collective-permute-start | bytes 712712 | tf_op jit(solution)/shard_map/ppermute | solution.py:26
  28.8 76.0 %copy-start.3 = (bf16[32,4096]{1,0:T(8,128)(2,1)S(1)}, bf16[32,4096]{1,0:T(8,128)(2,1)}, u32[]{:S(2)}) copy-start(bf16[32,4096]{1,0:T(8,128)(2,1)} %param.10) | copy-start | bytes 786436
  28.9 77.2 %copy-start.4 = (f32[4096]{0:T(1024)S(1)}, f32[4096]{0:T(1024)}, u32[]{:S(2)}) copy-start(f32[4096]{0:T(1024)} %param.11) | copy-start | bytes 49156
  92.6 2.3 %collective-permute-start.5 = (bf16[2,32,4096]{2,1,0:T(8,128)(2,1)}, bf16[2,32,4096]{2,1,0:T(8,128)(2,1)}, u32[]{:S(2)}, u32[]{:S(2)}) collective-permute-start(bf16[2,32,4096]{2,1,0:T(8,128)(2,1)} %fusion.24), channel_id=1, source_target_pairs={{0,1},{1,0},{2,3},{3,2},{4,5},{5,4},{6,7},{7,6},{8,9},{9,8},{10,11... | collective-permute-start | bytes 1572872 | tf_op jit(solution)/shard_map/ppermute | solution.py:26
  96.0 1.0 copy-start.1
  97.0 7.8 %collective-permute-start.6 = (bf16[1,32,4096]{2,1,0:T(8,128)(2,1)S(1)}, bf16[1,32,4096]{2,1,0:T(8,128)(2,1)S(1)}, u32[]{:S(2)}, u32[]{:S(2)}) collective-permute-start(bf16[1,32,4096]{2,1,0:T(8,128)(2,1)S(1)} %dynamic-slice_convert_fusion), channel_id=1, source_target_pairs={{0,2},{1,3},{2,0},{3,1},{4,6},{5,7},{6,4},{7,5},{8,10},{9,11},{10,... | collective-permute-start | bytes 786440 | tf_op jit(solution)/shard_map/ppermute | solution.py:26
  106.1 11.9 %copy-start.2 = (bf16[32,4096]{1,0:T(8,128)(2,1)}, bf16[32,4096]{1,0:T(8,128)(2,1)S(1)}, u32[]{:S(2)}) copy-start(bf16[32,4096]{1,0:T(8,128)(2,1)S(1)} %get-tuple-element.15) | copy-start | bytes 786436
  106.2 6.9 %collective-permute-start.7 = (bf16[1,32,4096]{2,1,0:T(8,128)(2,1)S(1)}, bf16[1,32,4096]{2,1,0:T(8,128)(2,1)S(1)}, u32[]{:S(2)}, u32[]{:S(2)}) collective-permute-start(bf16[1,32,4096]{2,1,0:T(8,128)(2,1)S(1)} %get-tuple-element.19), channel_id=1, source_target_pairs={{0,2},{1,3},{2,0},{3,1},{4,6},{5,7},{6,4},{7,5},{8,10},{9,11},{10,... | collective-permute-start | bytes 786440 | tf_op jit(solution)/shard_map/ppermute | solution.py:26
  113.3 3.5 %collective-permute-start.8 = (bf16[2,32,4096]{2,1,0:T(8,128)(2,1)S(1)}, bf16[2,32,4096]{2,1,0:T(8,128)(2,1)S(1)}, u32[]{:S(2)}, u32[]{:S(2)}) collective-permute-start(bf16[2,32,4096]{2,1,0:T(8,128)(2,1)S(1)} %maximum_select_fusion.2), channel_id=1, source_target_pairs={{0,1},{1,0},{2,3},{3,2},{4,5},{5,4},{6,7},{7,6},{8,9},{9,8},{10,11... | collective-permute-start | bytes 1572872 | tf_op jit(solution)/shard_map/ppermute | solution.py:26

commit v5 on v4

--- a/solution.py
+++ b/solution.py
@@ -12,7 +12,7 @@
 W1 = 512
 W2 = 32
 GROUP = 2
-PIECES = 4
+PIECES = 8
 
 
 def from_behind(value, axis, steps):
@@ -30,13 +30,12 @@
     return lax.dynamic_index_in_dim(value, place, dim, keepdims=False)
 
 
-def sum_to_owner(value, axis):
+def sum_to_owner(kept, sent, axis):
     count = lax.axis_size(axis)
-    if count & (count - 1):
-        return lax.psum_scatter(value, axis, scatter_dimension=0, tiled=True)
     place = lax.axis_index(axis)
-    value = value.reshape(count, value.shape[0] // count, value.shape[1])
-    for bit in range(count.bit_length() - 1):
+    value = kept + swap(sent, axis, 0).astype(jnp.float32)
+    value = value.reshape(count // 2, -1, value.shape[1])
+    for bit in range(1, count.bit_length() - 1):
         value = value.reshape(value.shape[0] // 2, 2, *value.shape[1:])
         mine = (place >> bit) & 1
         value = pick(value, mine, 1) + swap(
@@ -47,8 +46,6 @@
 
 def share_rows(value, axis):
     count = lax.axis_size(axis)
-    if count & (count - 1):
-        return lax.all_gather(value, axis, axis=0, tiled=True)
     place = lax.axis_index(axis)
     rows, width = value.shape
     value = value[None]
@@ -63,12 +60,6 @@
 def gather_columns(value):
     count = value.shape[0] * value.shape[1]
     return value.reshape(count, *value.shape[2:]).transpose(1, 0, 2).reshape(value.shape[2], -1)
-
-
-def place_pair(mine, value, other, dim):
-    return jnp.where(
-        mine == 0, jnp.concatenate([value, other], dim), jnp.concatenate([other, value], dim)
-    )
 
 
 def simple_window(local_part):
@@ -87,71 +78,72 @@
 
 
 def window_of(local_part, source, work):
+    done = []
+
+    def beside(values):
+        nonlocal source
+        if done:
+            values, source, done[-1] = lax.optimization_barrier((values, source, done[-1]))
+        done.append(work[len(done)](source))
+        return values
+
     tokens = local_part.shape[0]
     heads = lax.axis_size("head")
-    slab = lax.axis_index("ctx")
-    done = []
-
-    def beside(value):
-        nonlocal source
-        if work:
-            value, source = lax.optimization_barrier((value, source))
-            done.append(work.pop(0)(source))
-        return value
-
-    short = (
-        heads & (heads - 1) == 0 and heads >= 4 and lax.axis_size("ctx") % 2 == 0 and W1 == 4 * tokens
-    )
-    if not short:
-        out = simple_window(local_part)
-        while work:
-            done.append(work.pop(0)(source))
-        return out, jnp.int32(0), done
-
+    odd = lax.axis_index("ctx") & 1
     place = lax.axis_index("head")
-    done.append(work.pop(0)(source))
-    value = local_part[None]
+    if heads < 4 or lax.axis_size("ctx") % 2 or W1 != 4 * tokens:
+        return simple_window(local_part), [piece(source) for piece in work]
+    value = beside(local_part[None])
     for bit in reversed(range(1, heads.bit_length() - 1)):
         other = swap(value, "head", bit)
-        value = jnp.stack(
-            [jnp.where((place >> bit) & 1 == 0, value, other), jnp.where((place >> bit) & 1 == 0, other, value)], 1
-        )
+        mine = (place >> bit) & 1
+        value = jnp.stack([jnp.where(mine == 0, value, other), jnp.where(mine == 0, other, value)], 1)
         value = value.reshape(-1, *local_part.shape)
     half = value.shape[0] // 2
     first, second = value[:half], value[half:]
-
-    odd = slab & 1
     rim = second[:, tokens - W2 :]
-    other = swap(beside(jnp.concatenate([first, rim], 1)), "ctx", 0)
-    other, other_rim = other[:, :tokens], other[:, tokens:]
-    pair = place_pair(odd, first, other, 1)
-    pair_rim = jnp.where(odd == 0, other_rim, rim)
-    behind = from_behind(beside(jnp.concatenate([pair, pair_rim], 1)), "ctx", 2)
-    behind, behind_rim = behind[:, : 2 * tokens], behind[:, 2 * tokens :]
-    further = from_behind(beside(behind), "ctx", 2)
-    rim = jnp.where(odd == 0, behind_rim, other_rim)
-    value = jnp.concatenate([further, behind, pair, rim, second], 1)
-    other = swap(beside(value), "head", 0)
-    value = place_pair(place & 1, value[:, None], other[:, None], 1)
-    one, two = value[:, :, : 6 * tokens], value[:, :, 6 * tokens :]
+    first_rim, first = beside((jnp.concatenate([first, rim], 1), first))
+    two_back = from_behind(first_rim, "ctx", 2)
+    four_back = from_behind(first, "ctx", 4)
+    two_back, two_rim = two_back[:, :tokens], two_back[:, tokens:]
+    sent = jnp.concatenate([four_back, two_back, first, jnp.where(odd == 0, rim, two_rim)], 1)
+    other = swap(beside(sent), "ctx", 0)
+    far, near, there = (other[:, step * tokens : (step + 1) * tokens] for step in range(3))
+    value = jnp.concatenate(
+        [
+            four_back,
+            jnp.where(odd == 0, far, near),
+            two_back,
+            jnp.where(odd == 0, near, there),
+            first,
+            other[:, 3 * tokens :],
+            second,
+        ],
+        1,
+    )
+    other = swap(value, "head", 0)
+    mine = place & 1
+    value = jnp.stack([jnp.where(mine == 0, value, other), jnp.where(mine == 0, other, value)], 1)
+    one, two = value[:, :, : W1 + tokens], value[:, :, W1 + tokens :]
     one, two = gather_columns(one), gather_columns(two)
-    while work:
-        done.append(work.pop(0)(source))
-    return (one[:, :HD], one[:, HD:], two[:, :HD], two[:, HD:]), odd, done
+    return (one[:, :HD], one[:, HD:], two[:, :HD], two[:, HD:]), done
 
 
 def attention_kernel(
-    place, q_ref, k1_ref, v1_ref, k2_ref, v2_ref, out_ref,
-    query, last_key, first_key, key_diag, value_diag, column, order, result, scores, peaks,
+    place, q_first, q_middle, q_last, k1_ref, v1_ref, k2_ref, v2_ref, weight_hbm, kept_ref, sent_ref,
+    weight, arrived, attention, query, last_key, first_key, key_diag, value_diag, column, order, result, scores, peaks,
+    *, count,
 ):
-    tokens = q_ref.shape[0]
+    tokens = q_first.shape[0]
+    share = tokens // count
     blocks = W1 // tokens + 1
-    pairs = q_ref.shape[1] // (2 * HD)
+    width = q_first.shape[1] + q_middle.shape[1] + q_last.shape[1]
+    pairs = width // (2 * HD)
     lines = query.shape[1]
     rows = lines * W2
     rate = HD ** -0.5 * math.log2(math.e)
     slab = place[0]
-    start = pl.multiple_of(place[1] * tokens, tokens)
+    side = place[1]
 
     def twice(x):
         return jnp.concatenate([x, x], axis=-1)
@@ -162,12 +154,25 @@
             [jnp.concatenate([x, zero], axis=1), jnp.concatenate([zero, x], axis=1)], axis=0
         )
 
+    copies = [
+        pltpu.make_async_copy(
+            weight_hbm.at[pair * 2 * HD:(pair + 1) * 2 * HD], weight.at[pair * 2 * HD:(pair + 1) * 2 * HD],
+            arrived.at[pair],
+        )
+        for pair in range(pairs)
+    ]
+    for copy in copies:
+        copy.start()
     if lines > pairs:
         query[...] = jnp.zeros(query.shape, query.dtype)
-    for pair in range(pairs):
-        query[:, pair, :] = q_ref[:, pair * 2 * HD:(pair + 1) * 2 * HD].astype(jnp.float32)
+    line = 0
+    for part in (q_first, q_middle, q_last):
+        for lane in range(0, part.shape[1], HD):
+            half = line % 2 * HD
+            query[:, line // 2, half:half + HD] = part[:, lane:lane + HD].astype(jnp.float32)
+            line += 1
     for j in range(blocks):
-        there = pl.ds(start + j * tokens, tokens)
+        there = slice(j * tokens, (j + 1) * tokens)
         key = k1_ref[there, :].T
         if j < blocks - 1:
             value_diag[j] = diag(v1_ref[there, :])
@@ -222,10 +227,9 @@
 
     def blend(position, slot, behind):
         base = pl.multiple_of(position // 16 * 16, 16)
-        close = pl.multiple_of(start + base, 16)
-        far = pl.multiple_of(start + (blocks - 1) * tokens + base, 16)
+        far = pl.multiple_of((blocks - 1) * tokens + base, 16)
         late = order[...] <= jnp.broadcast_to(position - base, (16, HD)).astype(jnp.float32).astype(jnp.bfloat16)
-        value = jnp.where(late, v1_ref[pl.ds(far, 16), :], v1_ref[pl.ds(close, 16), :])
+        value = jnp.where(late, v1_ref[pl.ds(far, 16), :], v1_ref[pl.ds(base, 16), :])
         value_diag[0, pl.ds(base, 16), :HD] = value
         value_diag[0, pl.ds(pl.multiple_of(tokens + base, 16), 16), HD:] = value
         peak = peaks[slot][None]
@@ -268,22 +272,79 @@
         pl.when(jnp.minimum(slab, blocks - 1) == behind)(functools.partial(run, behind))
 
     for pair in range(pairs):
-        out_ref[:, pair * 2 * HD:(pair + 1) * 2 * HD] = result[:, pair, :].astype(out_ref.dtype)
-
-
-def attention_of(place, queries, key_one, value_one, key_two, value_two):
-    tokens, width = queries.shape
+        attention[:, pair * 2 * HD:(pair + 1) * 2 * HD] = result[:, pair, :].astype(attention.dtype)
+    for copy in copies:
+        copy.wait()
+    step = min(1024, weight.shape[1])
+    for lane in range(0, weight.shape[1], step):
+        product = jnp.dot(
+            attention[...], weight[:, lane:lane + step], preferred_element_type=jnp.float32
+        ).reshape(-1, 2, share, step)
+        even, odd = product[:, 0], product[:, 1]
+        kept = jnp.where(side == 0, even, odd)
+        sent = jnp.where(side == 0, odd, even)
+        kept_ref[:, lane:lane + step] = kept.reshape(-1, step)
+        sent_ref[:, lane:lane + step] = sent.reshape(-1, step).astype(sent_ref.dtype)
+
+
+def project_kernel(source, weight_hbm, out, weight, arrived, *, lane):
+    width = out.shape[1]
+    size = weight.shape[0] // PIECES
+    rows = [slice(step * size, (step + 1) * size) for step in range(PIECES)]
+    copies = [
+        pltpu.make_async_copy(weight_hbm.at[part, lane:lane + width], weight.at[part], arrived.at[step])
+        for step, part in enumerate(rows)
+    ]
+    for copy in copies:
+        copy.start()
+    product = None
+    for copy, part in zip(copies, rows):
+        copy.wait()
+        add = jnp.dot(source[:, part], weight[part, :], preferred_element_type=jnp.float32)
+        product = add if product is None else product + add
+    out[...] = product.astype(out.dtype)
+
+
+def project(weight, lane, width, source):
+    vmem = pl.BlockSpec(memory_space=pltpu.VMEM)
+    return pl.pallas_call(
+        functools.partial(project_kernel, lane=lane),
+        out_shape=jax.ShapeDtypeStruct((source.shape[0], width), jnp.bfloat16),
+        in_specs=[vmem, pl.BlockSpec(memory_space=pl.ANY)],
+        out_specs=vmem,
+        scratch_shapes=[
+            pltpu.VMEM((weight.shape[0], width), weight.dtype), pltpu.SemaphoreType.DMA((PIECES,)),
+        ],
+        compiler_params=pltpu.CompilerParams(vmem_limit_bytes=16 * 1024 * 1024),
+        cost_estimate=pl.CostEstimate(
+            flops=2 * source.shape[0] * weight.shape[0] * width,
+            bytes_accessed=2 * weight.shape[0] * width,
+            transcendentals=0,
+        ),
+        name="project",
+    )(source, weight)
+
+
+def attention_of(place, count, queries, key_one, value_one, key_two, value_two, out_weight):
+    tokens = queries[0].shape[0]
+    width = out_weight.shape[0]
     blocks = W1 // tokens + 1
     pairs = width // (2 * HD)
     lines = -(-pairs // 8) * 8
     rows = lines * W2
     vmem = pl.BlockSpec(memory_space=pltpu.VMEM)
     return pl.pallas_call(
-        attention_kernel,
-        out_shape=jax.ShapeDtypeStruct((tokens, width), jnp.bfloat16),
-        in_specs=[pl.BlockSpec(memory_space=pltpu.SMEM)] + [vmem] * 5,
-        out_specs=vmem,
+        functools.partial(attention_kernel, count=count),
+        out_shape=(
+            jax.ShapeDtypeStruct((tokens // 2, out_weight.shape[1]), jnp.float32),
+            jax.ShapeDtypeStruct((tokens // 2, out_weight.shape[1]), jnp.bfloat16),
+        ),
+        in_specs=[pl.BlockSpec(memory_space=pltpu.SMEM)] + [vmem] * 7 + [pl.BlockSpec(memory_space=pl.ANY)],
+        out_specs=(vmem, vmem),
         scratch_shapes=[
+            pltpu.VMEM(out_weight.shape, out_weight.dtype),
+            pltpu.SemaphoreType.DMA((pairs,)),
+            pltpu.VMEM((tokens, width), jnp.bfloat16),
             pltpu.VMEM((tokens, lines, 2 * HD), jnp.float32),
             pltpu.VMEM((HD, tokens), jnp.bfloat16),
             pltpu.VMEM((HD, tokens), jnp.bfloat16),
@@ -295,15 +356,16 @@
             pltpu.VMEM((2 * GROUP, blocks - 1, rows, 2 * tokens), jnp.float32),
             pltpu.VMEM((2 * GROUP, lines, 2 * tokens), jnp.float32),
         ],
-        compiler_params=pltpu.CompilerParams(vmem_limit_bytes=48 * 1024 * 1024),
+        compiler_params=pltpu.CompilerParams(vmem_limit_bytes=40 * 1024 * 1024),
         name="attention",
     )(
         place,
-        queries,
+        *queries,
         key_one,
         value_one,
         key_two.astype(jnp.float32),
         value_two.astype(jnp.float32),
+        out_weight,
     )
 
 
@@ -311,21 +373,19 @@
     local_part = jnp.dot(hidden_in, shared_weight, preferred_element_type=jnp.float32).astype(
         jnp.bfloat16
     )
-    width = query_weight.shape[1] // PIECES
-
-    def project(piece, source):
-        weight = query_weight[:, piece * width : (piece + 1) * width]
-        return jnp.dot(source, weight, preferred_element_type=jnp.float32).astype(jnp.bfloat16)
-
-    window, start, queries = window_of(
-        local_part, hidden_in, [functools.partial(project, piece) for piece in range(PIECES)]
+    half = query_weight.shape[1] // 2
+    query_weight = pltpu.with_memory_space_constraint(query_weight, pltpu.HBM)
+    window, queries = window_of(
+        local_part,
+        hidden_in,
+        [
+            functools.partial(project, query_weight, lane, width)
+            for lane, width in ((0, half // 2), (half // 2, half), (half // 2 + half, half // 2))
+        ],
     )
-    queries = jnp.concatenate(queries, axis=1)
-    place = jnp.stack([lax.axis_index("ctx"), start]).astype(jnp.int32)
-    attention = attention_of(place, queries, *window)
-    summed = sum_to_owner(
-        jnp.dot(attention, out_weight, preferred_element_type=jnp.float32), "head"
-    )
+    place = jnp.stack([lax.axis_index("ctx"), lax.axis_index("head") & 1]).astype(jnp.int32)
+    kept, sent = attention_of(place, lax.axis_size("head"), queries, *window, out_weight)
+    summed = sum_to_owner(kept, sent, "head")
     residual_out = (residual.astype(jnp.float32) + summed).astype(jnp.bfloat16)
     values = residual_out.astype(jnp.float32)
     scale = lax.rsqrt(jnp.mean(values * values, axis=1, keepdims=True) + 1e-05)

time: 118 us -> 110 us (0.932)
  matrix products: 21.4 us -> 1.64 us
  Pallas kernels: 54.6 us -> 66.2 us
  starting transfers between devices: 14.2 us -> 12.2 us
  waiting for transfers between devices: 19.4 us -> 20.8 us
    dot_general x5 -> x0, matrix products: 19.7 us -> none  [the longest x4 11.6 us: project(): jnp.dot(source, weight, preferred_element_type=jnp.float32)]
    pallas_call x1 -> x4, Pallas kernels: 54.6 us -> 66.2 us  [the longest x1 57.4 us: attention_of(): pl.pallas_call(functools.partial(attention_kernel, count=count), out_shap...]
    ppermute x7, waiting for transfers between devices: 19.4 us -> 20.8 us  [swap(): lax.ppermute(value, axis, [(source, source ^ 1 << bit) for source in rang...]
    unnamed x13 -> x16, local copies, waits for them, and re-layouts: 2.24 us -> 3.29 us
  transfers between devices with their start and end apart: 9 -> 9, of which waited for: 5 -> 5; matrix products, arithmetic and copies ran while one was open for 10% -> 0% of each run, Pallas kernels for 0% -> 8%
where the time goes in v5:
time: 110 us; the launch traced here: 109 us
  Pallas kernels  66.2 us (60%)
  waiting for transfers between devices  20.8 us (19%)
  starting transfers between devices  12.2 us (11%)
  local copies, waits for them, and re-layouts  4.41 us (4%)
  other arithmetic  3.02 us (3%)
  matrix products  1.64 us (1%)
    pallas_call x1, Pallas kernels, attention_of(): pl.pallas_call(functools.partial(attention_kernel, count=count), out_shap...  57.4 us
    ppermute x7, waiting for transfers between devices, swap(): lax.ppermute(value, axis, [(source, source ^ 1 << bit) for source in rang...  20.8 us
    pallas_call x3, Pallas kernels, project(): pl.pallas_call(functools.partial(project_kernel, lane=lane), out_shape=ja...  8.84 us
    ppermute x7, starting transfers between devices, swap(): lax.ppermute(value, axis, [(source, source ^ 1 << bit) for source in rang...  6.65 us
    ppermute x2, starting transfers between devices, from_behind(): lax.ppermute(value, axis, [(source, source + steps) for source in range(i...  5.51 us
    unnamed x16, local copies, waits for them, and re-layouts  3.29 us
  transfers between devices with their start and end apart: 9, of which 5 were waited for; matrix products, arithmetic and copies ran while one was open for 0% of the time, Pallas kernels for 8%

profile of v5, /device:TPU:11, one launch (start us, length us, event | category | flops | bytes accessed | tf_op | source)
XLA Modules:
  0.0 109.2 jit_solution(15045393684202630487)
XLA Ops:
  0.6 0.0 copy-start
  0.6 1.2 %copy-done = bf16[4096,128]{1,0:T(8,128)(2,1)S(1)} copy-done((bf16[4096,128]{1,0:T(8,128)(2,1)S(1)}, bf16[4096,128]{1,0:T(8,128)(2,1)}, u32[]{:S(2)}) %copy-start) | copy-done | bytes 1048600
  1.9 1.6 %fusion = bf16[1,128,128]{2,1,0:T(8,128)(2,1)S(1)} fusion(bf16[128,4096]{1,0:T(8,128)(2,1)} %source.3, bf16[4096,128]{1,0:T(8,128)(2,1)S(1)} %copy-done), kind=kOutput, calls=%fused_computation.1 | convolution fusion | flops 134234112 | bytes 2129920 | tf_op jit(solution)/shard_map/dot_general | solution.py:373
  3.5 1.3 %collective-permute-start = (bf16[1,128,128]{2,1,0:T(8,128)(2,1)S(1)}, bf16[1,128,128]{2,1,0:T(8,128)(2,1)S(1)}, u32[]{:S(2)}, u32[]{:S(2)}) collective-permute-start(bf16[1,128,128]{2,1,0:T(8,128)(2,1)S(1)} %fusion), channel_id=1, source_target_pairs={{0,2},{1,3},{2,0},{3,1},{4,6},{5,7},{6,4},{7,5},{8,10},{9,11},{10,... | collective-permute-start | bytes 98312 | tf_op jit(solution)/shard_map/ppermute | solution.py:26
  4.8 0.0 copy-start.1
  4.8 1.2 %copy-done.1 = bf16[128,4096]{1,0:T(8,128)(2,1)S(1)} copy-done((bf16[128,4096]{1,0:T(8,128)(2,1)S(1)}, bf16[128,4096]{1,0:T(8,128)(2,1)}, u32[]{:S(2)}) %copy-start.1) | copy-done | bytes 1048600
  6.0 0.0 copy-start.2
  6.0 2.6 %project.3.q_first = bf16[128,512]{1,0:T(8,128)(2,1)S(1)} custom-call(bf16[128,4096]{1,0:T(8,128)(2,1)S(1)} %copy-done.1, bf16[4096,2048]{1,0:T(8,128)(2,1)} %weight_hbm.6), custom_call_target="tpu_custom_call" | custom-call | flops 536870912 | bytes 4194304 | tf_op jit(solution)/shard_map/project/pallas_call | solution.py:310
  8.6 0.0 collective-permute-done
  8.7 3.2 %collective-permute-start.2 = (bf16[1,160,128]{2,1,0:T(8,128)(2,1)S(1)}, bf16[1,160,128]{2,1,0:T(8,128)(2,1)S(1)}, u32[]{:S(2)}, u32[]{:S(2)}) collective-permute-start(bf16[1,160,128]{2,1,0:T(8,128)(2,1)S(1)} %pad_maximum_fusion.2), channel_id=1, source_target_pairs={{0,8},{4,12},{8,16},{12,20},{16,24},{20,28},{1,9},{5,13},{9,17},{1... | collective-permute-start | bytes 122888 | tf_op jit(solution)/shard_map/ppermute | solution.py:21
  11.9 2.3 %collective-permute-start.1 = (bf16[1,128,128]{2,1,0:T(8,128)(2,1)S(1)}, bf16[1,128,128]{2,1,0:T(8,128)(2,1)S(1)}, u32[]{:S(2)}, u32[]{:S(2)}) collective-permute-start(bf16[1,128,128]{2,1,0:T(8,128)(2,1)S(1)} %get-tuple-element.12), channel_id=1, source_target_pairs={{0,16},{4,20},{8,24},{12,28},{1,17},{5,21},{9,25},{13,29},{2,18},{... | collective-permute-start | bytes 98312 | tf_op jit(solution)/shard_map/ppermute | solution.py:21
  14.2 3.8 %project.4.q_middle = bf16[128,1024]{1,0:T(8,128)(2,1)S(1)} custom-call(bf16[128,4096]{1,0:T(8,128)(2,1)S(1)} %copy-done.1, bf16[4096,2048]{1,0:T(8,128)(2,1)} %weight_hbm.6), custom_call_target="tpu_custom_call" | custom-call | flops 1073741824 | bytes 8388608 | tf_op jit(solution)/shard_map/project/pallas_call | solution.py:310
  18.0 0.0 collective-permute-done.2
  18.0 0.0 collective-permute-done.1
  18.1 0.3 collective-permute-start.3
  18.4 3.3 %collective-permute-done.3 = bf16[1,416,128]{2,1,0:T(8,128)(2,1)S(1)} collective-permute-done((bf16[1,416,128]{2,1,0:T(8,128)(2,1)S(1)}, bf16[1,416,128]{2,1,0:T(8,128)(2,1)S(1)}, u32[]{:S(2)}, u32[]{:S(2)}) %collective-permute-start.3) | collective-permute-done | bytes 106528 | tf_op jit(solution)/shard_map/ppermute | solution.py:26
  21.8 2.5 %collective-permute-start.4 = (bf16[1,800,128]{2,1,0:T(8,128)(2,1)S(1)}, bf16[1,800,128]{2,1,0:T(8,128)(2,1)S(1)}, u32[]{:S(2)}, u32[]{:S(2)}) collective-permute-start(bf16[1,800,128]{2,1,0:T(8,128)(2,1)S(1)} %constant_dynamic-update-slice_fusion), channel_id=1, source_target_pairs={{0,1},{1,0},{2,3},{3,2},{4,5},{5,4},{6,7},{7,6},{8,9},{9,8},{10,11... | collective-permute-start | bytes 614408 | tf_op jit(solution)/shard_map/ppermute | solution.py:26
  24.2 0.1 pad_add_fusion.place
  24.3 0.0 copy-done.2
  24.3 2.5 %project.5.q_last = bf16[128,512]{1,0:T(8,128)(2,1)S(1)} custom-call(bf16[128,4096]{1,0:T(8,128)(2,1)S(1)} %copy-done.2, bf16[4096,2048]{1,0:T(8,128)(2,1)} %weight_hbm.6), custom_call_target="tpu_custom_call" | custom-call | flops 536870912 | bytes 4194304 | tf_op jit(solution)/shard_map/project/pallas_call | solution.py:310
  26.8 0.0 copy-start.5
  26.8 0.0 collective-permute-done.4
  27.0 57.4 %attention.1 = (f32[64,4096]{1,0:T(8,128)S(1)}, bf16[64,4096]{1,0:T(8,128)(2,1)S(1)}) custom-call(s32[2]{0:T(128)S(1)} %pad_add_fusion.place, bf16[128,512]{1,0:T(8,128)(2,1)S(1)} %project.3.q_first, bf16[128,1024]{1,0:T(8,128)(2,1)S(1)} %project.4.q_middle, bf16[128,512]{1,0:T(8,128)(2,1)S(1)} %project.5.q_last, ...), custom_call_target="tpu_custom_call" | custom-call | tf_op jit(solution)/shard_map/attention/pallas_call | solution.py:336
  84.4 0.1 collective-permute-start.5
  84.5 1.9 %collective-permute-done.5 = bf16[64,4096]{1,0:T(8,128)(2,1)S(1)} collective-permute-done((bf16[64,4096]{1,0:T(8,128)(2,1)S(1)}, bf16[64,4096]{1,0:T(8,128)(2,1)S(1)}, u32[]{:S(2)}, u32[]{:S(2)}) %collective-permute-start.5) | collective-permute-done | bytes 524320 | tf_op jit(solution)/shard_map/ppermute | solution.py:26
  86.4 0.0 copy-start.4
  86.4 0.8 copy-done.4
  87.2 1.1 %convert_add_fusion = f32[64,4096]{1,0:T(8,128)S(1)} fusion(f32[64,4096]{1,0:T(8,128)S(1)} %get-tuple-element.18, bf16[64,4096]{1,0:T(8,128)(2,1)} %copy-done.4), kind=kLoop, calls=%fused_computation.3 | loop fusion | flops 524288 | bytes 2621440 | tf_op jit(solution)/shard_map/add | solution.py:36
  88.3 0.3 collective-permute-start.6
  88.6 7.5 %collective-permute-done.6 = bf16[1,32,4096]{2,1,0:T(8,128)(2,1)S(1)} collective-permute-done((bf16[1,32,4096]{2,1,0:T(8,128)(2,1)S(1)}, bf16[1,32,4096]{2,1,0:T(8,128)(2,1)S(1)}, u32[]{:S(2)}, u32[]{:S(2)}) %collective-permute-start.6) | collective-permute-done | bytes 262176 | tf_op jit(solution)/shard_map/ppermute | solution.py:26
  96.1 1.2 %fusion.1 = (f32[32]{0:T(128)S(1)}, bf16[32,4096]{1,0:T(8,128)(2,1)S(1)}) fusion(bf16[1,32,4096]{2,1,0:T(8,128)(2,1)S(1)} %collective-permute-done.6, f32[1,2,32,4096]{3,2,1,0:T(8,128)S(1)} %bitcast.47, s32[]{:T(128)S(6)} %select_n.94, bf16[32,4096]{1,0:T(8,128)(2,1)} %param.10), kind=kLoop, calls=%fused_computation.6 | loop fusion | flops 1048544 | bytes 1310852 | tf_op jit(solution)/shard_map/reduce_sum | solution.py:391
  97.3 0.0 copy-start.3
  97.3 0.0 copy-done.5
  97.3 0.1 fusion.10
  97.5 0.3 collective-permute-start.7
  97.7 6.7 %collective-permute-done.7 = bf16[1,32,4096]{2,1,0:T(8,128)(2,1)S(1)} collective-permute-done((bf16[1,32,4096]{2,1,0:T(8,128)(2,1)S(1)}, bf16[1,32,4096]{2,1,0:T(8,128)(2,1)S(1)}, u32[]{:S(2)}, u32[]{:S(2)}) %collective-permute-start.7) | collective-permute-done | bytes 262176 | tf_op jit(solution)/shard_map/ppermute | solution.py:26
  104.4 0.1 maximum_select_fusion.2
  104.5 1.9 %collective-permute-start.8 = (bf16[2,32,4096]{2,1,0:T(8,128)(2,1)S(1)}, bf16[2,32,4096]{2,1,0:T(8,128)(2,1)S(1)}, u32[]{:S(2)}, u32[]{:S(2)}) collective-permute-start(bf16[2,32,4096]{2,1,0:T(8,128)(2,1)S(1)} %maximum_select_fusion.2), channel_id=1, source_target_pairs={{0,1},{1,0},{2,3},{3,2},{4,5},{5,4},{6,7},{7,6},{8,9},{9,8},{10,11... | collective-permute-start | bytes 1572872 | tf_op jit(solution)/shard_map/ppermute | solution.py:26
  106.4 0.1 maximum_select_fusion.1
  106.5 1.5 %collective-permute-done.8 = bf16[2,32,4096]{2,1,0:T(8,128)(2,1)S(1)} collective-permute-done((bf16[2,32,4096]{2,1,0:T(8,128)(2,1)S(1)}, bf16[2,32,4096]{2,1,0:T(8,128)(2,1)S(1)}, u32[]{:S(2)}, u32[]{:S(2)}) %collective-permute-start.8) | collective-permute-done | bytes 524320 | tf_op jit(solution)/shard_map/ppermute | solution.py:26
  107.9 0.2 maximum_select_fusion
  108.1 1.0 copy.10
  109.2 0.0 copy-done.3
  (20 shorter events, 0.3 us)
Async XLA Ops:
  0.6 1.2 %copy-start = (bf16[4096,128]{1,0:T(8,128)(2,1)S(1)}, bf16[4096,128]{1,0:T(8,128)(2,1)}, u32[]{:S(2)}) copy-start(bf16[4096,128]{1,0:T(8,128)(2,1)} %param.8) | copy-start | bytes 3145732
  3.5 5.1 %collective-permute-start = (bf16[1,128,128]{2,1,0:T(8,128)(2,1)S(1)}, bf16[1,128,128]{2,1,0:T(8,128)(2,1)S(1)}, u32[]{:S(2)}, u32[]{:S(2)}) collective-permute-start(bf16[1,128,128]{2,1,0:T(8,128)(2,1)S(1)} %fusion), channel_id=1, source_target_pairs={{0,2},{1,3},{2,0},{3,1},{4,6},{5,7},{6,4},{7,5},{8,10},{9,11},{10,... | collective-permute-start | bytes 98312 | tf_op jit(solution)/shard_map/ppermute | solution.py:26
  4.8 1.2 %copy-start.1 = (bf16[128,4096]{1,0:T(8,128)(2,1)S(1)}, bf16[128,4096]{1,0:T(8,128)(2,1)}, u32[]{:S(2)}) copy-start(bf16[128,4096]{1,0:T(8,128)(2,1)} %source.3) | copy-start | bytes 3145732
  6.0 18.3 %copy-start.2 = (bf16[128,4096]{1,0:T(8,128)(2,1)S(1)}, bf16[128,4096]{1,0:T(8,128)(2,1)}, u32[]{:S(2)}) copy-start(bf16[128,4096]{1,0:T(8,128)(2,1)} %source.3) | copy-start | bytes 3145732
  8.7 9.3 %collective-permute-start.2 = (bf16[1,160,128]{2,1,0:T(8,128)(2,1)S(1)}, bf16[1,160,128]{2,1,0:T(8,128)(2,1)S(1)}, u32[]{:S(2)}, u32[]{:S(2)}) collective-permute-start(bf16[1,160,128]{2,1,0:T(8,128)(2,1)S(1)} %pad_maximum_fusion.2), channel_id=1, source_target_pairs={{0,8},{4,12},{8,16},{12,20},{16,24},{20,28},{1,9},{5,13},{9,17},{1... | collective-permute-start | bytes 122888 | tf_op jit(solution)/shard_map/ppermute | solution.py:21
  11.9 6.2 %collective-permute-start.1 = (bf16[1,128,128]{2,1,0:T(8,128)(2,1)S(1)}, bf16[1,128,128]{2,1,0:T(8,128)(2,1)S(1)}, u32[]{:S(2)}, u32[]{:S(2)}) collective-permute-start(bf16[1,128,128]{2,1,0:T(8,128)(2,1)S(1)} %get-tuple-element.12), channel_id=1, source_target_pairs={{0,16},{4,20},{8,24},{12,28},{1,17},{5,21},{9,25},{13,29},{2,18},{... | collective-permute-start | bytes 98312 | tf_op jit(solution)/shard_map/ppermute | solution.py:21
  18.1 3.6 %collective-permute-start.3 = (bf16[1,416,128]{2,1,0:T(8,128)(2,1)S(1)}, bf16[1,416,128]{2,1,0:T(8,128)(2,1)S(1)}, u32[]{:S(2)}, u32[]{:S(2)}) collective-permute-start(bf16[1,416,128]{2,1,0:T(8,128)(2,1)S(1)} %pad_maximum_fusion), channel_id=1, source_target_pairs={{0,4},{4,0},{8,12},{12,8},{16,20},{20,16},{24,28},{28,24},{1,5},{5... | collective-permute-start | bytes 319496 | tf_op jit(solution)/shard_map/ppermute | solution.py:26
  21.8 5.0 %collective-permute-start.4 = (bf16[1,800,128]{2,1,0:T(8,128)(2,1)S(1)}, bf16[1,800,128]{2,1,0:T(8,128)(2,1)S(1)}, u32[]{:S(2)}, u32[]{:S(2)}) collective-permute-start(bf16[1,800,128]{2,1,0:T(8,128)(2,1)S(1)} %constant_dynamic-update-slice_fusion), channel_id=1, source_target_pairs={{0,1},{1,0},{2,3},{3,2},{4,5},{5,4},{6,7},{7,6},{8,9},{9,8},{10,11... | collective-permute-start | bytes 614408 | tf_op jit(solution)/shard_map/ppermute | solution.py:26
  26.8 70.5 %copy-start.5 = (f32[4096]{0:T(1024)S(1)}, f32[4096]{0:T(1024)}, u32[]{:S(2)}) copy-start(f32[4096]{0:T(1024)} %param.11) | copy-start | bytes 49156
  84.4 2.0 %collective-permute-start.5 = (bf16[64,4096]{1,0:T(8,128)(2,1)S(1)}, bf16[64,4096]{1,0:T(8,128)(2,1)S(1)}, u32[]{:S(2)}, u32[]{:S(2)}) collective-permute-start(bf16[64,4096]{1,0:T(8,128)(2,1)S(1)} %get-tuple-element.19), channel_id=1, source_target_pairs={{0,1},{1,0},{2,3},{3,2},{4,5},{5,4},{6,7},{7,6},{8,9},{9,8},{10,11... | collective-permute-start | bytes 1572872 | tf_op jit(solution)/shard_map/ppermute | solution.py:26
  86.4 0.8 copy-start.4
  88.3 7.8 %collective-permute-start.6 = (bf16[1,32,4096]{2,1,0:T(8,128)(2,1)S(1)}, bf16[1,32,4096]{2,1,0:T(8,128)(2,1)S(1)}, u32[]{:S(2)}, u32[]{:S(2)}) collective-permute-start(bf16[1,32,4096]{2,1,0:T(8,128)(2,1)S(1)} %fusion.7), channel_id=1, source_target_pairs={{0,2},{1,3},{2,0},{3,1},{4,6},{5,7},{6,4},{7,5},{8,10},{9,11},{10,... | collective-permute-start | bytes 786440 | tf_op jit(solution)/shard_map/ppermute | solution.py:26
  97.3 11.9 %copy-start.3 = (bf16[32,4096]{1,0:T(8,128)(2,1)}, bf16[32,4096]{1,0:T(8,128)(2,1)S(1)}, u32[]{:S(2)}) copy-start(bf16[32,4096]{1,0:T(8,128)(2,1)S(1)} %get-tuple-element.21) | copy-start | bytes 786436
  97.5 6.9 %collective-permute-start.7 = (bf16[1,32,4096]{2,1,0:T(8,128)(2,1)S(1)}, bf16[1,32,4096]{2,1,0:T(8,128)(2,1)S(1)}, u32[]{:S(2)}, u32[]{:S(2)}) collective-permute-start(bf16[1,32,4096]{2,1,0:T(8,128)(2,1)S(1)} %get-tuple-element.27), channel_id=1, source_target_pairs={{0,2},{1,3},{2,0},{3,1},{4,6},{5,7},{6,4},{7,5},{8,10},{9,11},{10,... | collective-permute-start | bytes 786440 | tf_op jit(solution)/shard_map/ppermute | solution.py:26
  104.5 3.5 %collective-permute-start.8 = (bf16[2,32,4096]{2,1,0:T(8,128)(2,1)S(1)}, bf16[2,32,4096]{2,1,0:T(8,128)(2,1)S(1)}, u32[]{:S(2)}, u32[]{:S(2)}) collective-permute-start(bf16[2,32,4096]{2,1,0:T(8,128)(2,1)S(1)} %maximum_select_fusion.2), channel_id=1, source_target_pairs={{0,1},{1,0},{2,3},{3,2},{4,5},{5,4},{6,7},{7,6},{8,9},{9,8},{10,11... | collective-permute-start | bytes 1572872 | tf_op jit(solution)/shard_map/ppermute | solution.py:26

commit v6 on v5

--- a/solution.py
+++ b/solution.py
@@ -12,7 +12,7 @@
 W1 = 512
 W2 = 32
 GROUP = 2
-PIECES = 8
+PIECES = 4
 
 
 def from_behind(value, axis, steps):
@@ -108,6 +108,7 @@
     two_back, two_rim = two_back[:, :tokens], two_back[:, tokens:]
     sent = jnp.concatenate([four_back, two_back, first, jnp.where(odd == 0, rim, two_rim)], 1)
     other = swap(beside(sent), "ctx", 0)
+    other, done[-1] = lax.optimization_barrier((other, done[-1]))
     far, near, there = (other[:, step * tokens : (step + 1) * tokens] for step in range(3))
     value = jnp.concatenate(
         [
@@ -285,6 +286,44 @@
         sent = jnp.where(side == 0, odd, even)
         kept_ref[:, lane:lane + step] = kept.reshape(-1, step)
         sent_ref[:, lane:lane + step] = sent.reshape(-1, step).astype(sent_ref.dtype)
+
+
+def share_kernel(source_hbm, weight_hbm, source, out, weight, arrived):
+    size = weight.shape[0] // PIECES
+    rows = [slice(step * size, (step + 1) * size) for step in range(PIECES)]
+    copies = [
+        (
+            pltpu.make_async_copy(source_hbm.at[:, part], source.at[:, part], arrived.at[0, step]),
+            pltpu.make_async_copy(weight_hbm.at[part], weight.at[part], arrived.at[1, step]),
+        )
+        for step, part in enumerate(rows)
+    ]
+    for one, two in copies:
+        one.start()
+        two.start()
+    product = None
+    for (one, two), part in zip(copies, rows):
+        one.wait()
+        two.wait()
+        add = jnp.dot(source[:, part], weight[part, :], preferred_element_type=jnp.float32)
+        product = add if product is None else product + add
+    out[...] = product.astype(out.dtype)
+
+
+def share(source, weight):
+    vmem = pl.BlockSpec(memory_space=pltpu.VMEM)
+    return pl.pallas_call(
+        share_kernel,
+        out_shape=(
+            jax.ShapeDtypeStruct(source.shape, source.dtype),
+            jax.ShapeDtypeStruct((source.shape[0], weight.shape[1]), jnp.bfloat16),
+        ),
+        in_specs=[pl.BlockSpec(memory_space=pl.ANY)] * 2,
+        out_specs=(vmem, vmem),
+        scratch_shapes=[pltpu.VMEM(weight.shape, weight.dtype), pltpu.SemaphoreType.DMA((2, PIECES))],
+        compiler_params=pltpu.CompilerParams(vmem_limit_bytes=8 * 1024 * 1024),
+        name="share",
+    )(pltpu.with_memory_space_constraint(source, pltpu.HBM), pltpu.with_memory_space_constraint(weight, pltpu.HBM))
 
 
 def project_kernel(source, weight_hbm, out, weight, arrived, *, lane):
@@ -370,14 +409,12 @@
 
 
 def body(hidden_in, query_weight, shared_weight, out_weight, residual, norm_gain):
-    local_part = jnp.dot(hidden_in, shared_weight, preferred_element_type=jnp.float32).astype(
-        jnp.bfloat16
-    )
+    source, local_part = share(hidden_in, shared_weight)
     half = query_weight.shape[1] // 2
     query_weight = pltpu.with_memory_space_constraint(query_weight, pltpu.HBM)
     window, queries = window_of(
         local_part,
-        hidden_in,
+        source,
         [
             functools.partial(project, query_weight, lane, width)
             for lane, width in ((0, half // 2), (half // 2, half), (half // 2 + half, half // 2))

time: 110 us -> 103 us (0.936)
  waiting for transfers between devices: 20.8 us -> 16.7 us
  local copies, waits for them, and re-layouts: 4.41 us -> 1.17 us
  Pallas kernels: 66.2 us -> 68.5 us
  starting transfers between devices: 12.2 us -> 14.4 us
  other arithmetic: 3.02 us -> 1.02 us
  matrix products: 1.64 us -> 0 us
    ppermute x7, waiting for transfers between devices: 20.8 us -> 16.7 us  [swap(): lax.ppermute(value, axis, [(source, source ^ 1 << bit) for source in rang...]
    unnamed x16 -> x10, local copies, waits for them, and re-layouts: 3.29 us -> 0.05 us
    ppermute x7, starting transfers between devices: 6.65 us -> 8.93 us  [swap(): lax.ppermute(value, axis, [(source, source ^ 1 << bit) for source in rang...]
    pallas_call x0 -> x1, Pallas kernels: none -> 1.99 us  [share(): pl.pallas_call(share_kernel, out_shape=(jax.ShapeDtypeStruct(source.shape...]
    dot_general x1 -> x0, matrix products: 1.64 us -> none  [body(): jnp.dot(hidden_in, shared_weight, preferred_element_type=jnp.float32)]
  transfers between devices with their start and end apart: 9 -> 9, of which waited for: 5 -> 6; matrix products, arithmetic and copies ran while one was open for 0% -> 0% of each run, Pallas kernels for 8% -> 9%
where the time goes in v6:
time: 103 us
  Pallas kernels  68.5 us (67%)
  waiting for transfers between devices  16.7 us (16%)
  starting transfers between devices  14.4 us (14%)
  local copies, waits for them, and re-layouts  1.17 us (1%)
    pallas_call x1, Pallas kernels, attention_of(): pl.pallas_call(functools.partial(attention_kernel, count=count), out_shap...  57.4 us
    ppermute x7, waiting for transfers between devices, swap(): lax.ppermute(value, axis, [(source, source ^ 1 << bit) for source in rang...  16.7 us
    pallas_call x3, Pallas kernels, project(): pl.pallas_call(functools.partial(project_kernel, lane=lane), out_shape=ja...  9.09 us
    ppermute x7, starting transfers between devices, swap(): lax.ppermute(value, axis, [(source, source ^ 1 << bit) for source in rang...  8.93 us
    ppermute x2, starting transfers between devices, from_behind(): lax.ppermute(value, axis, [(source, source + steps) for source in range(i...  5.51 us
  transfers between devices with their start and end apart: 9, of which 6 were waited for; matrix products, arithmetic and copies ran while one was open for 0% of the time, Pallas kernels for 9%

profile of v6, /device:TPU:11, one launch (start us, length us, event | category | flops | bytes accessed | tf_op | source)
XLA Modules:
  0.0 102.6 jit_solution(12564514579551083344)
XLA Ops:
  0.6 2.0 %share.1 = (bf16[128,4096]{1,0:T(8,128)(2,1)S(1)}, bf16[128,128]{1,0:T(8,128)(2,1)S(1)}) custom-call(bf16[128,4096]{1,0:T(8,128)(2,1)} %source_hbm.1, bf16[4096,128]{1,0:T(8,128)(2,1)} %weight_hbm.5), custom_call_target="tpu_custom_call" | custom-call | tf_op jit(solution)/shard_map/share/pallas_call | solution.py:315
  2.6 1.3 %collective-permute-start = (bf16[1,128,128]{2,1,0:T(8,128)(2,1)S(1)}, bf16[1,128,128]{2,1,0:T(8,128)(2,1)S(1)}, u32[]{:S(2)}, u32[]{:S(2)}) collective-permute-start(bf16[1,128,128]{2,1,0:T(8,128)(2,1)S(1)} %bitcast.45), channel_id=1, source_target_pairs={{0,2},{1,3},{2,0},{3,1},{4,6},{5,7},{6,4},{7,5},{8,10},{9,11},{10,... | collective-permute-start | bytes 98312 | tf_op jit(solution)/shard_map/ppermute | solution.py:26
  3.9 2.5 %project.3.q_first = bf16[128,512]{1,0:T(8,128)(2,1)S(1)} custom-call(bf16[128,4096]{1,0:T(8,128)(2,1)S(1)} %get-tuple-element.23.source, bf16[4096,2048]{1,0:T(8,128)(2,1)} %weight_hbm.8), custom_call_target="tpu_custom_call" | custom-call | flops 536870912 | bytes 4194304 | tf_op jit(solution)/shard_map/project/pallas_call | solution.py:349
  6.5 0.0 collective-permute-done
  6.5 3.2 %collective-permute-start.2 = (bf16[1,160,128]{2,1,0:T(8,128)(2,1)S(1)}, bf16[1,160,128]{2,1,0:T(8,128)(2,1)S(1)}, u32[]{:S(2)}, u32[]{:S(2)}) collective-permute-start(bf16[1,160,128]{2,1,0:T(8,128)(2,1)S(1)} %pad_maximum_fusion.2), channel_id=1, source_target_pairs={{0,8},{4,12},{8,16},{12,20},{16,24},{20,28},{1,9},{5,13},{9,17},{1... | collective-permute-start | bytes 122888 | tf_op jit(solution)/shard_map/ppermute | solution.py:21
  9.8 2.3 %collective-permute-start.1 = (bf16[1,128,128]{2,1,0:T(8,128)(2,1)S(1)}, bf16[1,128,128]{2,1,0:T(8,128)(2,1)S(1)}, u32[]{:S(2)}, u32[]{:S(2)}) collective-permute-start(bf16[1,128,128]{2,1,0:T(8,128)(2,1)S(1)} %get-tuple-element.18), channel_id=1, source_target_pairs={{0,16},{4,20},{8,24},{12,28},{1,17},{5,21},{9,25},{13,29},{2,18},{... | collective-permute-start | bytes 98312 | tf_op jit(solution)/shard_map/ppermute | solution.py:21
  12.1 4.0 %project.4.q_middle = bf16[128,1024]{1,0:T(8,128)(2,1)S(1)} custom-call(bf16[128,4096]{1,0:T(8,128)(2,1)S(1)} %get-tuple-element.23.source, bf16[4096,2048]{1,0:T(8,128)(2,1)} %weight_hbm.8), custom_call_target="tpu_custom_call" | custom-call | flops 1073741824 | bytes 8388608 | tf_op jit(solution)/shard_map/project/pallas_call | solution.py:349
  16.0 0.0 collective-permute-done.2
  16.1 0.0 collective-permute-done.1
  16.1 0.3 collective-permute-start.3
  16.4 0.0 copy-start.1
  16.4 2.6 %project.5.q_last = bf16[128,512]{1,0:T(8,128)(2,1)S(1)} custom-call(bf16[128,4096]{1,0:T(8,128)(2,1)S(1)} %get-tuple-element.23.source, bf16[4096,2048]{1,0:T(8,128)(2,1)} %weight_hbm.8), custom_call_target="tpu_custom_call" | custom-call | flops 536870912 | bytes 4194304 | tf_op jit(solution)/shard_map/project/pallas_call | solution.py:349
  19.0 0.0 copy-start.2
  19.0 0.7 collective-permute-done.3
  19.8 2.4 %collective-permute-start.4 = (bf16[1,800,128]{2,1,0:T(8,128)(2,1)S(1)}, bf16[1,800,128]{2,1,0:T(8,128)(2,1)S(1)}, u32[]{:S(2)}, u32[]{:S(2)}) collective-permute-start(bf16[1,800,128]{2,1,0:T(8,128)(2,1)S(1)} %constant_dynamic-update-slice_fusion), channel_id=1, source_target_pairs={{0,1},{1,0},{2,3},{3,2},{4,5},{5,4},{6,7},{7,6},{8,9},{9,8},{10,11... | collective-permute-start | bytes 614408 | tf_op jit(solution)/shard_map/ppermute | solution.py:26
  22.3 0.1 pad_add_fusion.place
  22.3 1.0 collective-permute-done.4
  23.5 57.4 %attention.1 = (f32[64,4096]{1,0:T(8,128)S(1)}, bf16[64,4096]{1,0:T(8,128)(2,1)S(1)}) custom-call(s32[2]{0:T(128)S(1)} %pad_add_fusion.place, bf16[128,512]{1,0:T(8,128)(2,1)S(1)} %project.3.q_first, bf16[128,1024]{1,0:T(8,128)(2,1)S(1)} %project.4.q_middle, bf16[128,512]{1,0:T(8,128)(2,1)S(1)} %project.5.q_last, ...), custom_call_target="tpu_custom_call" | custom-call | tf_op jit(solution)/shard_map/attention/pallas_call | solution.py:375
  80.9 0.4 collective-permute-start.5
  81.3 1.5 %collective-permute-done.5 = bf16[64,4096]{1,0:T(8,128)(2,1)S(1)} collective-permute-done((bf16[64,4096]{1,0:T(8,128)(2,1)S(1)}, bf16[64,4096]{1,0:T(8,128)(2,1)S(1)}, u32[]{:S(2)}, u32[]{:S(2)}) %collective-permute-start.5) | collective-permute-done | bytes 524320 | tf_op jit(solution)/shard_map/ppermute | solution.py:26
  82.9 0.1 convert_add_fusion
  83.0 1.1 %collective-permute-start.6 = (bf16[1,32,4096]{2,1,0:T(8,128)(2,1)S(1)}, bf16[1,32,4096]{2,1,0:T(8,128)(2,1)S(1)}, u32[]{:S(2)}, u32[]{:S(2)}) collective-permute-start(bf16[1,32,4096]{2,1,0:T(8,128)(2,1)S(1)} %fusion.6), channel_id=1, source_target_pairs={{0,2},{1,3},{2,0},{3,1},{4,6},{5,7},{6,4},{7,5},{8,10},{9,11},{10,... | collective-permute-start | bytes 786440 | tf_op jit(solution)/shard_map/ppermute | solution.py:26
  84.1 6.4 %collective-permute-done.6 = bf16[1,32,4096]{2,1,0:T(8,128)(2,1)S(1)} collective-permute-done((bf16[1,32,4096]{2,1,0:T(8,128)(2,1)S(1)}, bf16[1,32,4096]{2,1,0:T(8,128)(2,1)S(1)}, u32[]{:S(2)}, u32[]{:S(2)}) %collective-permute-start.6) | collective-permute-done | bytes 262176 | tf_op jit(solution)/shard_map/ppermute | solution.py:26
  90.6 0.0 copy-done.1
  90.6 0.2 fusion
  90.8 0.0 copy-start
  90.8 0.0 copy-done.2
  90.8 0.1 fusion.9
  90.9 1.1 %collective-permute-start.7 = (bf16[1,32,4096]{2,1,0:T(8,128)(2,1)S(1)}, bf16[1,32,4096]{2,1,0:T(8,128)(2,1)S(1)}, u32[]{:S(2)}, u32[]{:S(2)}) collective-permute-start(bf16[1,32,4096]{2,1,0:T(8,128)(2,1)S(1)} %get-tuple-element.35), channel_id=1, source_target_pairs={{0,2},{1,3},{2,0},{3,1},{4,6},{5,7},{6,4},{7,5},{8,10},{9,11},{10,... | collective-permute-start | bytes 786440 | tf_op jit(solution)/shard_map/ppermute | solution.py:26
  92.1 5.6 %collective-permute-done.7 = bf16[1,32,4096]{2,1,0:T(8,128)(2,1)S(1)} collective-permute-done((bf16[1,32,4096]{2,1,0:T(8,128)(2,1)S(1)}, bf16[1,32,4096]{2,1,0:T(8,128)(2,1)S(1)}, u32[]{:S(2)}, u32[]{:S(2)}) %collective-permute-start.7) | collective-permute-done | bytes 262176 | tf_op jit(solution)/shard_map/ppermute | solution.py:26
  97.7 0.1 maximum_select_fusion.2
  97.7 2.1 %collective-permute-start.8 = (bf16[2,32,4096]{2,1,0:T(8,128)(2,1)S(1)}, bf16[2,32,4096]{2,1,0:T(8,128)(2,1)S(1)}, u32[]{:S(2)}, u32[]{:S(2)}) collective-permute-start(bf16[2,32,4096]{2,1,0:T(8,128)(2,1)S(1)} %maximum_select_fusion.2), channel_id=1, source_target_pairs={{0,1},{1,0},{2,3},{3,2},{4,5},{5,4},{6,7},{7,6},{8,9},{9,8},{10,11... | collective-permute-start | bytes 1572872 | tf_op jit(solution)/shard_map/ppermute | solution.py:26
  99.9 0.1 maximum_select_fusion.1
  100.0 1.5 %collective-permute-done.8 = bf16[2,32,4096]{2,1,0:T(8,128)(2,1)S(1)} collective-permute-done((bf16[2,32,4096]{2,1,0:T(8,128)(2,1)S(1)}, bf16[2,32,4096]{2,1,0:T(8,128)(2,1)S(1)}, u32[]{:S(2)}, u32[]{:S(2)}) %collective-permute-start.8) | collective-permute-done | bytes 524320 | tf_op jit(solution)/shard_map/ppermute | solution.py:26
  101.4 0.2 maximum_select_fusion
  101.6 1.0 %copy.10 = bf16[2,2,32,4096]{3,2,1,0:T(8,128)(2,1)} copy(bf16[2,2,32,4096]{3,2,0,1:T(8,128)(2,1)S(1)} %maximum_select_fusion) | data formatting | bytes 2097152 | tf_op jit(solution)/shard_map/jit(_where)/select_n | solution.py:55
  102.6 0.0 copy-done
  (20 shorter events, 0.3 us)
Async XLA Ops:
  2.6 3.9 %collective-permute-start = (bf16[1,128,128]{2,1,0:T(8,128)(2,1)S(1)}, bf16[1,128,128]{2,1,0:T(8,128)(2,1)S(1)}, u32[]{:S(2)}, u32[]{:S(2)}) collective-permute-start(bf16[1,128,128]{2,1,0:T(8,128)(2,1)S(1)} %bitcast.45), channel_id=1, source_target_pairs={{0,2},{1,3},{2,0},{3,1},{4,6},{5,7},{6,4},{7,5},{8,10},{9,11},{10,... | collective-permute-start | bytes 98312 | tf_op jit(solution)/shard_map/ppermute | solution.py:26
  6.5 9.5 %collective-permute-start.2 = (bf16[1,160,128]{2,1,0:T(8,128)(2,1)S(1)}, bf16[1,160,128]{2,1,0:T(8,128)(2,1)S(1)}, u32[]{:S(2)}, u32[]{:S(2)}) collective-permute-start(bf16[1,160,128]{2,1,0:T(8,128)(2,1)S(1)} %pad_maximum_fusion.2), channel_id=1, source_target_pairs={{0,8},{4,12},{8,16},{12,20},{16,24},{20,28},{1,9},{5,13},{9,17},{1... | collective-permute-start | bytes 122888 | tf_op jit(solution)/shard_map/ppermute | solution.py:21
  9.8 6.3 %collective-permute-start.1 = (bf16[1,128,128]{2,1,0:T(8,128)(2,1)S(1)}, bf16[1,128,128]{2,1,0:T(8,128)(2,1)S(1)}, u32[]{:S(2)}, u32[]{:S(2)}) collective-permute-start(bf16[1,128,128]{2,1,0:T(8,128)(2,1)S(1)} %get-tuple-element.18), channel_id=1, source_target_pairs={{0,16},{4,20},{8,24},{12,28},{1,17},{5,21},{9,25},{13,29},{2,18},{... | collective-permute-start | bytes 98312 | tf_op jit(solution)/shard_map/ppermute | solution.py:21
  16.1 3.6 %collective-permute-start.3 = (bf16[1,416,128]{2,1,0:T(8,128)(2,1)S(1)}, bf16[1,416,128]{2,1,0:T(8,128)(2,1)S(1)}, u32[]{:S(2)}, u32[]{:S(2)}) collective-permute-start(bf16[1,416,128]{2,1,0:T(8,128)(2,1)S(1)} %pad_maximum_fusion), channel_id=1, source_target_pairs={{0,4},{4,0},{8,12},{12,8},{16,20},{20,16},{24,28},{28,24},{1,5},{5... | collective-permute-start | bytes 319496 | tf_op jit(solution)/shard_map/ppermute | solution.py:26
  16.4 74.1 %copy-start.1 = (bf16[32,4096]{1,0:T(8,128)(2,1)S(1)}, bf16[32,4096]{1,0:T(8,128)(2,1)}, u32[]{:S(2)}) copy-start(bf16[32,4096]{1,0:T(8,128)(2,1)} %param.10) | copy-start | bytes 786436
  19.0 71.8 %copy-start.2 = (f32[4096]{0:T(1024)S(1)}, f32[4096]{0:T(1024)}, u32[]{:S(2)}) copy-start(f32[4096]{0:T(1024)} %param.11) | copy-start | bytes 49156
  19.8 3.5 %collective-permute-start.4 = (bf16[1,800,128]{2,1,0:T(8,128)(2,1)S(1)}, bf16[1,800,128]{2,1,0:T(8,128)(2,1)S(1)}, u32[]{:S(2)}, u32[]{:S(2)}) collective-permute-start(bf16[1,800,128]{2,1,0:T(8,128)(2,1)S(1)} %constant_dynamic-update-slice_fusion), channel_id=1, source_target_pairs={{0,1},{1,0},{2,3},{3,2},{4,5},{5,4},{6,7},{7,6},{8,9},{9,8},{10,11... | collective-permute-start | bytes 614408 | tf_op jit(solution)/shard_map/ppermute | solution.py:26
  80.9 2.0 %collective-permute-start.5 = (bf16[64,4096]{1,0:T(8,128)(2,1)S(1)}, bf16[64,4096]{1,0:T(8,128)(2,1)S(1)}, u32[]{:S(2)}, u32[]{:S(2)}) collective-permute-start(bf16[64,4096]{1,0:T(8,128)(2,1)S(1)} %get-tuple-element.27), channel_id=1, source_target_pairs={{0,1},{1,0},{2,3},{3,2},{4,5},{5,4},{6,7},{7,6},{8,9},{9,8},{10,11... | collective-permute-start | bytes 1572872 | tf_op jit(solution)/shard_map/ppermute | solution.py:26
  83.0 7.6 %collective-permute-start.6 = (bf16[1,32,4096]{2,1,0:T(8,128)(2,1)S(1)}, bf16[1,32,4096]{2,1,0:T(8,128)(2,1)S(1)}, u32[]{:S(2)}, u32[]{:S(2)}) collective-permute-start(bf16[1,32,4096]{2,1,0:T(8,128)(2,1)S(1)} %fusion.6), channel_id=1, source_target_pairs={{0,2},{1,3},{2,0},{3,1},{4,6},{5,7},{6,4},{7,5},{8,10},{9,11},{10,... | collective-permute-start | bytes 786440 | tf_op jit(solution)/shard_map/ppermute | solution.py:26
  90.8 11.9 %copy-start = (bf16[32,4096]{1,0:T(8,128)(2,1)}, bf16[32,4096]{1,0:T(8,128)(2,1)S(1)}, u32[]{:S(2)}) copy-start(bf16[32,4096]{1,0:T(8,128)(2,1)S(1)} %get-tuple-element.29) | copy-start | bytes 786436
  90.9 6.7 %collective-permute-start.7 = (bf16[1,32,4096]{2,1,0:T(8,128)(2,1)S(1)}, bf16[1,32,4096]{2,1,0:T(8,128)(2,1)S(1)}, u32[]{:S(2)}, u32[]{:S(2)}) collective-permute-start(bf16[1,32,4096]{2,1,0:T(8,128)(2,1)S(1)} %get-tuple-element.35), channel_id=1, source_target_pairs={{0,2},{1,3},{2,0},{3,1},{4,6},{5,7},{6,4},{7,5},{8,10},{9,11},{10,... | collective-permute-start | bytes 786440 | tf_op jit(solution)/shard_map/ppermute | solution.py:26
  97.7 3.7 %collective-permute-start.8 = (bf16[2,32,4096]{2,1,0:T(8,128)(2,1)S(1)}, bf16[2,32,4096]{2,1,0:T(8,128)(2,1)S(1)}, u32[]{:S(2)}, u32[]{:S(2)}) collective-permute-start(bf16[2,32,4096]{2,1,0:T(8,128)(2,1)S(1)} %maximum_select_fusion.2), channel_id=1, source_target_pairs={{0,1},{1,0},{2,3},{3,2},{4,5},{5,4},{6,7},{7,6},{8,9},{9,8},{10,11... | collective-permute-start | bytes 1572872 | tf_op jit(solution)/shard_map/ppermute | solution.py:26

commit v7 on v6

--- a/solution.py
+++ b/solution.py
@@ -11,7 +11,10 @@
 HD = 128
 W1 = 512
 W2 = 32
-GROUP = 2
+GROUP = 16
+SHORT_GROUP = 4
+HEADROOM = 60.0
+FLOOR = 2.0 ** -88
 PIECES = 4
 
 
@@ -132,7 +135,7 @@
 
 def attention_kernel(
     place, q_first, q_middle, q_last, k1_ref, v1_ref, k2_ref, v2_ref, weight_hbm, kept_ref, sent_ref,
-    weight, arrived, attention, query, last_key, first_key, key_diag, value_diag, column, order, result, scores, peaks,
+    weight, arrived, attention, query, last_key, first_key, key_diag, value_diag, column, order, result, scores, bound,
     *, count,
 ):
     tokens = q_first.shape[0]
@@ -186,10 +189,28 @@
     order[...] = lax.broadcasted_iota(jnp.int32, order.shape, 0).astype(jnp.float32).astype(order.dtype)
     column[...] = lax.broadcasted_iota(jnp.int32, column.shape, 1).astype(jnp.float32).astype(column.dtype)
 
+    key = k1_ref[...].astype(jnp.float32)
+    longest = jnp.max(jnp.sum(key * key, axis=1, keepdims=True), axis=0, keepdims=True)
+    key = k2_ref[...]
+    key = (key * key).astype(jnp.bfloat16)
+    row = lax.broadcasted_iota(jnp.int32, (tokens, key.shape[0]), 0)
+    col = lax.broadcasted_iota(jnp.int32, (tokens, key.shape[0]), 1)
+    seen = (col > row) & (col <= row + W2)
+    for pair in range(lines):
+        for half in (0, HD):
+            line = query[:, pair, half:half + HD]
+            size = lax.dot_general(
+                (line * line).astype(jnp.bfloat16), key, (((1,), (1,)), ((), ())),
+                preferred_element_type=jnp.float32,
+            )
+            size = jnp.max(jnp.where(seen, size, 0.0), axis=1, keepdims=True)
+            size = jnp.sqrt(size * longest) * (1.03 * rate) - HEADROOM
+            bound[:, pair, half:half + HD] = jnp.broadcast_to(size, (tokens, HD))
+
     def used(behind):
         return [0] + list(range(blocks - 1 - behind, blocks - 1))[-(blocks - 2):] if behind else [0]
 
-    def score(position, slot, behind):
+    def products(position, behind):
         line = query[position]
         line = jnp.concatenate([line] * (16 // lines), axis=0).astype(jnp.bfloat16)
         mixed = []
@@ -208,7 +229,7 @@
             if behind * tokens < W2 - 1:
                 shown = lax.broadcasted_iota(jnp.int32, (W2, 1, 1), 0) + (position + behind * tokens)
                 bias = bias + jnp.where(shown >= W2 - 1, 0.0, -jnp.inf)
-        peak = None
+        parts = []
         for j in used(behind):
             if j == 0:
                 weights = diag(jnp.where(late, last_key[...], first_key[...]))
@@ -217,27 +238,20 @@
             part = jnp.dot(mixed, weights, preferred_element_type=jnp.float32)
             if j == 0 and behind < blocks - 1:
                 part = (part.reshape(W2, lines, 2 * tokens) + bias).reshape(part.shape)
-            scores[slot, j] = part
-            high = jnp.max(part.reshape(W2, lines, 2 * tokens), axis=0)
-            peak = high if peak is None else jnp.maximum(peak, high)
-        left = jnp.max(peak[:, :tokens], axis=1, keepdims=True) * rate
-        right = jnp.max(peak[:, tokens:], axis=1, keepdims=True) * rate
-        peaks[slot] = jnp.concatenate(
-            [jnp.broadcast_to(left, (lines, tokens)), jnp.broadcast_to(right, (lines, tokens))], axis=1
-        )
-
-    def blend(position, slot, behind):
+            parts.append(part)
+        return parts
+
+    def attend(position, behind, parts, shift):
         base = pl.multiple_of(position // 16 * 16, 16)
         far = pl.multiple_of((blocks - 1) * tokens + base, 16)
         late = order[...] <= jnp.broadcast_to(position - base, (16, HD)).astype(jnp.float32).astype(jnp.bfloat16)
         value = jnp.where(late, v1_ref[pl.ds(far, 16), :], v1_ref[pl.ds(base, 16), :])
         value_diag[0, pl.ds(base, 16), :HD] = value
         value_diag[0, pl.ds(pl.multiple_of(tokens + base, 16), 16), HD:] = value
-        peak = peaks[slot][None]
         blended = total = None
-        for j in used(behind):
-            part = scores[slot, j].reshape(W2, lines, 2 * tokens)
-            part = jnp.exp2(part * rate - peak)
+        for j, part in zip(used(behind), parts):
+            part = part.reshape(W2, lines, 2 * tokens)
+            part = jnp.exp2(part * rate - shift[None])
             add = jnp.sum(part, axis=0)
             total = add if total is None else total + add
             part = jnp.dot(
@@ -253,21 +267,38 @@
         left = jnp.sum(total[:, :tokens], axis=1, keepdims=True)
         right = jnp.sum(total[:, tokens:], axis=1, keepdims=True)
         result[position] = jnp.concatenate([acc[:, :HD] / left, acc[:, HD:] / right], axis=1)
+        return jnp.broadcast_to(jnp.minimum(left, right), (lines, HD))
+
+    def exact(behind, position, _):
+        peak = None
+        for j, part in zip(used(behind), products(position, behind)):
+            scores[j] = part
+            high = jnp.max(part.reshape(W2, lines, 2 * tokens), axis=0)
+            peak = high if peak is None else jnp.maximum(peak, high)
+        left = jnp.max(peak[:, :tokens], axis=1, keepdims=True) * rate
+        right = jnp.max(peak[:, tokens:], axis=1, keepdims=True) * rate
+        shift = jnp.concatenate(
+            [jnp.broadcast_to(left, (lines, tokens)), jnp.broadcast_to(right, (lines, tokens))], axis=1
+        )
+        attend(position, behind, [scores[j] for j in used(behind)], shift)
+        return 0
 
     def run(behind):
-        for step in range(GROUP):
-            score(step, step, behind)
-
-        def trip(index, _):
-            for half in range(2):
-                first = (2 * index + half) * GROUP
-                for step in range(GROUP):
-                    ahead = jnp.minimum(first + GROUP + step, tokens - 1)
-                    score(ahead, (1 - half) * GROUP + step, behind)
-                    blend(first + step, half * GROUP + step, behind)
-            return 0
-
-        lax.fori_loop(0, tokens // (2 * GROUP), trip, 0)
+        group = GROUP if len(used(behind)) == blocks - 1 else SHORT_GROUP
+
+        def trip(index, low):
+            for step in range(group):
+                position = index * group + step
+                low = jnp.minimum(low, attend(position, behind, products(position, behind), bound[position]))
+            return low
+
+        low = lax.fori_loop(0, tokens // group, trip, jnp.full((lines, HD), jnp.inf, jnp.float32))
+        kept_all = jnp.min(low) >= FLOOR
+
+        @pl.when(jnp.logical_not(kept_all))
+        def _():
+            value_diag[0] = diag(v1_ref[:tokens, :])
+            lax.fori_loop(0, tokens, functools.partial(exact, behind), 0)
 
     for behind in range(blocks):
         pl.when(jnp.minimum(slab, blocks - 1) == behind)(functools.partial(run, behind))
@@ -392,8 +423,8 @@
             pltpu.VMEM((16, tokens), jnp.bfloat16),
             pltpu.VMEM((16, HD), jnp.bfloat16),
             pltpu.VMEM((tokens, lines, 2 * HD), jnp.float32),
-            pltpu.VMEM((2 * GROUP, blocks - 1, rows, 2 * tokens), jnp.float32),
-            pltpu.VMEM((2 * GROUP, lines, 2 * tokens), jnp.float32),
+            pltpu.VMEM((blocks - 1, rows, 2 * tokens), jnp.float32),
+            pltpu.VMEM((tokens, lines, 2 * HD), jnp.float32),
         ],
         compiler_params=pltpu.CompilerParams(vmem_limit_bytes=40 * 1024 * 1024),
         name="attention",

time: 103 us -> 221 us (2.15)
  Pallas kernels: 68.5 us -> 186 us
    pallas_call x1, Pallas kernels: 57.4 us -> 175 us  [attention_of(): pl.pallas_call(functools.partial(attention_kernel, count=count), out_shap...]
  transfers between devices with their start and end apart: 9 -> 9, of which waited for: 6 -> 6; matrix products, arithmetic and copies ran while one was open for 0% -> 0% of each run, Pallas kernels for 9% -> 4%
where the time goes in v7:
time: 221 us
  Pallas kernels  186 us (84%)
  waiting for transfers between devices  16.7 us (8%)
  starting transfers between devices  14.4 us (7%)
    pallas_call x1, Pallas kernels, attention_of(): pl.pallas_call(functools.partial(attention_kernel, count=count), out_shap...  175 us
    ppermute x7, waiting for transfers between devices, swap(): lax.ppermute(value, axis, [(source, source ^ 1 << bit) for source in rang...  16.7 us
    pallas_call x3, Pallas kernels, project(): pl.pallas_call(functools.partial(project_kernel, lane=lane), out_shape=ja...  9.09 us
    ppermute x7, starting transfers between devices, swap(): lax.ppermute(value, axis, [(source, source ^ 1 << bit) for source in rang...  8.91 us
    ppermute x2, starting transfers between devices, from_behind(): lax.ppermute(value, axis, [(source, source + steps) for source in range(i...  5.51 us
  transfers between devices with their start and end apart: 9, of which 6 were waited for; matrix products, arithmetic and copies ran while one was open for 0% of the time, Pallas kernels for 4%

profile of v7, /device:TPU:11, one launch (start us, length us, event | category | flops | bytes accessed | tf_op | source)
XLA Modules:
  0.0 220.6 jit_solution(641818487375623744)
XLA Ops:
  0.6 2.0 share.1
  2.6 1.3 collective-permute-start
  3.9 2.5 %project.3.q_first = bf16[128,512]{1,0:T(8,128)(2,1)S(1)} custom-call(bf16[128,4096]{1,0:T(8,128)(2,1)S(1)} %get-tuple-element.23.source, bf16[4096,2048]{1,0:T(8,128)(2,1)} %weight_hbm.8), custom_call_target="tpu_custom_call" | custom-call | flops 536870912 | bytes 4194304 | tf_op jit(solution)/shard_map/project/pallas_call | solution.py:380
  6.5 0.0 collective-permute-done
  6.5 3.2 %collective-permute-start.2 = (bf16[1,160,128]{2,1,0:T(8,128)(2,1)S(1)}, bf16[1,160,128]{2,1,0:T(8,128)(2,1)S(1)}, u32[]{:S(2)}, u32[]{:S(2)}) collective-permute-start(bf16[1,160,128]{2,1,0:T(8,128)(2,1)S(1)} %pad_maximum_fusion.2), channel_id=1, source_target_pairs={{0,8},{4,12},{8,16},{12,20},{16,24},{20,28},{1,9},{5,13},{9,17},{1... | collective-permute-start | bytes 122888 | tf_op jit(solution)/shard_map/ppermute | solution.py:24
  9.8 2.3 %collective-permute-start.1 = (bf16[1,128,128]{2,1,0:T(8,128)(2,1)S(1)}, bf16[1,128,128]{2,1,0:T(8,128)(2,1)S(1)}, u32[]{:S(2)}, u32[]{:S(2)}) collective-permute-start(bf16[1,128,128]{2,1,0:T(8,128)(2,1)S(1)} %get-tuple-element.18), channel_id=1, source_target_pairs={{0,16},{4,20},{8,24},{12,28},{1,17},{5,21},{9,25},{13,29},{2,18},{... | collective-permute-start | bytes 98312 | tf_op jit(solution)/shard_map/ppermute | solution.py:24
  12.1 4.0 %project.4.q_middle = bf16[128,1024]{1,0:T(8,128)(2,1)S(1)} custom-call(bf16[128,4096]{1,0:T(8,128)(2,1)S(1)} %get-tuple-element.23.source, bf16[4096,2048]{1,0:T(8,128)(2,1)} %weight_hbm.8), custom_call_target="tpu_custom_call" | custom-call | flops 1073741824 | bytes 8388608 | tf_op jit(solution)/shard_map/project/pallas_call | solution.py:380
  16.0 0.0 collective-permute-done.2
  16.1 0.0 collective-permute-done.1
  16.1 0.3 collective-permute-start.3
  16.4 0.0 copy-start.1
  16.4 2.6 %project.5.q_last = bf16[128,512]{1,0:T(8,128)(2,1)S(1)} custom-call(bf16[128,4096]{1,0:T(8,128)(2,1)S(1)} %get-tuple-element.23.source, bf16[4096,2048]{1,0:T(8,128)(2,1)} %weight_hbm.8), custom_call_target="tpu_custom_call" | custom-call | flops 536870912 | bytes 4194304 | tf_op jit(solution)/shard_map/project/pallas_call | solution.py:380
  19.0 0.0 copy-start.2
  19.0 0.7 collective-permute-done.3
  19.8 2.4 %collective-permute-start.4 = (bf16[1,800,128]{2,1,0:T(8,128)(2,1)S(1)}, bf16[1,800,128]{2,1,0:T(8,128)(2,1)S(1)}, u32[]{:S(2)}, u32[]{:S(2)}) collective-permute-start(bf16[1,800,128]{2,1,0:T(8,128)(2,1)S(1)} %constant_dynamic-update-slice_fusion), channel_id=1, source_target_pairs={{0,1},{1,0},{2,3},{3,2},{4,5},{5,4},{6,7},{7,6},{8,9},{9,8},{10,11... | collective-permute-start | bytes 614408 | tf_op jit(solution)/shard_map/ppermute | solution.py:29
  22.3 0.1 pad_add_fusion.place
  22.3 1.0 collective-permute-done.4
  23.5 175.3 %attention.1 = (f32[64,4096]{1,0:T(8,128)S(1)}, bf16[64,4096]{1,0:T(8,128)(2,1)S(1)}) custom-call(s32[2]{0:T(128)S(1)} %pad_add_fusion.place, bf16[128,512]{1,0:T(8,128)(2,1)S(1)} %project.3.q_first, bf16[128,1024]{1,0:T(8,128)(2,1)S(1)} %project.4.q_middle, bf16[128,512]{1,0:T(8,128)(2,1)S(1)} %project.5.q_last, ...), custom_call_target="tpu_custom_call" | custom-call | tf_op jit(solution)/shard_map/attention/pallas_call | solution.py:406
  198.8 0.4 collective-permute-start.5
  199.2 1.5 collective-permute-done.5
  200.8 0.1 convert_add_fusion
  200.9 1.1 collective-permute-start.6
  202.0 6.4 %collective-permute-done.6 = bf16[1,32,4096]{2,1,0:T(8,128)(2,1)S(1)} collective-permute-done((bf16[1,32,4096]{2,1,0:T(8,128)(2,1)S(1)}, bf16[1,32,4096]{2,1,0:T(8,128)(2,1)S(1)}, u32[]{:S(2)}, u32[]{:S(2)}) %collective-permute-start.6) | collective-permute-done | bytes 262176 | tf_op jit(solution)/shard_map/ppermute | solution.py:29
  208.5 0.0 copy-done.1
  208.5 0.2 fusion
  208.7 0.0 copy-start
  208.7 0.0 copy-done.2
  208.7 0.1 fusion.9
  208.9 1.1 collective-permute-start.7
  210.0 5.6 %collective-permute-done.7 = bf16[1,32,4096]{2,1,0:T(8,128)(2,1)S(1)} collective-permute-done((bf16[1,32,4096]{2,1,0:T(8,128)(2,1)S(1)}, bf16[1,32,4096]{2,1,0:T(8,128)(2,1)S(1)}, u32[]{:S(2)}, u32[]{:S(2)}) %collective-permute-start.7) | collective-permute-done | bytes 262176 | tf_op jit(solution)/shard_map/ppermute | solution.py:29
  215.6 0.1 maximum_select_fusion.2
  215.6 2.1 collective-permute-start.8
  217.8 0.1 maximum_select_fusion.1
  217.9 1.5 collective-permute-done.8
  219.3 0.2 maximum_select_fusion
  219.5 1.0 copy.10
  220.6 0.0 copy-done
  (20 shorter events, 0.3 us)
Async XLA Ops:
  2.6 3.9 %collective-permute-start = (bf16[1,128,128]{2,1,0:T(8,128)(2,1)S(1)}, bf16[1,128,128]{2,1,0:T(8,128)(2,1)S(1)}, u32[]{:S(2)}, u32[]{:S(2)}) collective-permute-start(bf16[1,128,128]{2,1,0:T(8,128)(2,1)S(1)} %bitcast.45), channel_id=1, source_target_pairs={{0,2},{1,3},{2,0},{3,1},{4,6},{5,7},{6,4},{7,5},{8,10},{9,11},{10,... | collective-permute-start | bytes 98312 | tf_op jit(solution)/shard_map/ppermute | solution.py:29
  6.5 9.5 %collective-permute-start.2 = (bf16[1,160,128]{2,1,0:T(8,128)(2,1)S(1)}, bf16[1,160,128]{2,1,0:T(8,128)(2,1)S(1)}, u32[]{:S(2)}, u32[]{:S(2)}) collective-permute-start(bf16[1,160,128]{2,1,0:T(8,128)(2,1)S(1)} %pad_maximum_fusion.2), channel_id=1, source_target_pairs={{0,8},{4,12},{8,16},{12,20},{16,24},{20,28},{1,9},{5,13},{9,17},{1... | collective-permute-start | bytes 122888 | tf_op jit(solution)/shard_map/ppermute | solution.py:24
  9.8 6.3 %collective-permute-start.1 = (bf16[1,128,128]{2,1,0:T(8,128)(2,1)S(1)}, bf16[1,128,128]{2,1,0:T(8,128)(2,1)S(1)}, u32[]{:S(2)}, u32[]{:S(2)}) collective-permute-start(bf16[1,128,128]{2,1,0:T(8,128)(2,1)S(1)} %get-tuple-element.18), channel_id=1, source_target_pairs={{0,16},{4,20},{8,24},{12,28},{1,17},{5,21},{9,25},{13,29},{2,18},{... | collective-permute-start | bytes 98312 | tf_op jit(solution)/shard_map/ppermute | solution.py:24
  16.1 3.6 %collective-permute-start.3 = (bf16[1,416,128]{2,1,0:T(8,128)(2,1)S(1)}, bf16[1,416,128]{2,1,0:T(8,128)(2,1)S(1)}, u32[]{:S(2)}, u32[]{:S(2)}) collective-permute-start(bf16[1,416,128]{2,1,0:T(8,128)(2,1)S(1)} %pad_maximum_fusion), channel_id=1, source_target_pairs={{0,4},{4,0},{8,12},{12,8},{16,20},{20,16},{24,28},{28,24},{1,5},{5... | collective-permute-start | bytes 319496 | tf_op jit(solution)/shard_map/ppermute | solution.py:29
  16.4 192.1 %copy-start.1 = (bf16[32,4096]{1,0:T(8,128)(2,1)S(1)}, bf16[32,4096]{1,0:T(8,128)(2,1)}, u32[]{:S(2)}) copy-start(bf16[32,4096]{1,0:T(8,128)(2,1)} %param.10) | copy-start | bytes 786436
  19.0 189.7 %copy-start.2 = (f32[4096]{0:T(1024)S(1)}, f32[4096]{0:T(1024)}, u32[]{:S(2)}) copy-start(f32[4096]{0:T(1024)} %param.11) | copy-start | bytes 49156
  19.8 3.5 %collective-permute-start.4 = (bf16[1,800,128]{2,1,0:T(8,128)(2,1)S(1)}, bf16[1,800,128]{2,1,0:T(8,128)(2,1)S(1)}, u32[]{:S(2)}, u32[]{:S(2)}) collective-permute-start(bf16[1,800,128]{2,1,0:T(8,128)(2,1)S(1)} %constant_dynamic-update-slice_fusion), channel_id=1, source_target_pairs={{0,1},{1,0},{2,3},{3,2},{4,5},{5,4},{6,7},{7,6},{8,9},{9,8},{10,11... | collective-permute-start | bytes 614408 | tf_op jit(solution)/shard_map/ppermute | solution.py:29
  198.8 2.0 collective-permute-start.5
  200.9 7.6 %collective-permute-start.6 = (bf16[1,32,4096]{2,1,0:T(8,128)(2,1)S(1)}, bf16[1,32,4096]{2,1,0:T(8,128)(2,1)S(1)}, u32[]{:S(2)}, u32[]{:S(2)}) collective-permute-start(bf16[1,32,4096]{2,1,0:T(8,128)(2,1)S(1)} %fusion.6), channel_id=1, source_target_pairs={{0,2},{1,3},{2,0},{3,1},{4,6},{5,7},{6,4},{7,5},{8,10},{9,11},{10,... | collective-permute-start | bytes 786440 | tf_op jit(solution)/shard_map/ppermute | solution.py:29
  208.7 11.9 %copy-start = (bf16[32,4096]{1,0:T(8,128)(2,1)}, bf16[32,4096]{1,0:T(8,128)(2,1)S(1)}, u32[]{:S(2)}) copy-start(bf16[32,4096]{1,0:T(8,128)(2,1)S(1)} %get-tuple-element.29) | copy-start | bytes 786436
  208.9 6.7 %collective-permute-start.7 = (bf16[1,32,4096]{2,1,0:T(8,128)(2,1)S(1)}, bf16[1,32,4096]{2,1,0:T(8,128)(2,1)S(1)}, u32[]{:S(2)}, u32[]{:S(2)}) collective-permute-start(bf16[1,32,4096]{2,1,0:T(8,128)(2,1)S(1)} %get-tuple-element.35), channel_id=1, source_target_pairs={{0,2},{1,3},{2,0},{3,1},{4,6},{5,7},{6,4},{7,5},{8,10},{9,11},{10,... | collective-permute-start | bytes 786440 | tf_op jit(solution)/shard_map/ppermute | solution.py:29
  215.6 3.7 %collective-permute-start.8 = (bf16[2,32,4096]{2,1,0:T(8,128)(2,1)S(1)}, bf16[2,32,4096]{2,1,0:T(8,128)(2,1)S(1)}, u32[]{:S(2)}, u32[]{:S(2)}) collective-permute-start(bf16[2,32,4096]{2,1,0:T(8,128)(2,1)S(1)} %maximum_select_fusion.2), channel_id=1, source_target_pairs={{0,1},{1,0},{2,3},{3,2},{4,5},{5,4},{6,7},{7,6},{8,9},{9,8},{10,11... | collective-permute-start | bytes 1572872 | tf_op jit(solution)/shard_map/ppermute | solution.py:29

commit v8 on v7

--- a/solution.py
+++ b/solution.py
@@ -11,7 +11,7 @@
 HD = 128
 W1 = 512
 W2 = 32
-GROUP = 16
+GROUP = 32
 SHORT_GROUP = 4
 HEADROOM = 60.0
 FLOOR = 2.0 ** -88
@@ -224,7 +224,8 @@
         here = jnp.broadcast_to(position, (16, tokens)).astype(jnp.float32).astype(jnp.bfloat16)
         late = jnp.concatenate([column[...] <= here] * (HD // 16), axis=0)
         if behind < blocks - 1:
-            bias = lax.broadcasted_iota(jnp.int32, (1, 2 * tokens), 1) % tokens <= position
+            open_from = jnp.where(slab >= blocks - 1, 2 * tokens, position)
+            bias = lax.broadcasted_iota(jnp.int32, (1, 2 * tokens), 1) % tokens <= open_from
             bias = jnp.where(bias, 0.0, -jnp.inf)[None]
             if behind * tokens < W2 - 1:
                 shown = lax.broadcasted_iota(jnp.int32, (W2, 1, 1), 0) + (position + behind * tokens)
@@ -300,8 +301,8 @@
             value_diag[0] = diag(v1_ref[:tokens, :])
             lax.fori_loop(0, tokens, functools.partial(exact, behind), 0)
 
-    for behind in range(blocks):
-        pl.when(jnp.minimum(slab, blocks - 1) == behind)(functools.partial(run, behind))
+    for behind in range(blocks - 1):
+        pl.when(jnp.minimum(slab, blocks - 2) == behind)(functools.partial(run, behind))
 
     for pair in range(pairs):
         attention[:, pair * 2 * HD:(pair + 1) * 2 * HD] = result[:, pair, :].astype(attention.dtype)

time: 221 us -> 219 us (level)
  no operation moved by 1% of the time
where the time goes in v8:
time: 219 us
  Pallas kernels  185 us (84%)
  waiting for transfers between devices  16.7 us (8%)
  starting transfers between devices  14.4 us (7%)
    pallas_call x1, Pallas kernels, attention_of(): pl.pallas_call(functools.partial(attention_kernel, count=count), out_shap...  174 us
    ppermute x7, waiting for transfers between devices, swap(): lax.ppermute(value, axis, [(source, source ^ 1 << bit) for source in rang...  16.7 us
    pallas_call x3, Pallas kernels, project(): pl.pallas_call(functools.partial(project_kernel, lane=lane), out_shape=ja...  9.09 us
    ppermute x7, starting transfers between devices, swap(): lax.ppermute(value, axis, [(source, source ^ 1 << bit) for source in rang...  8.91 us
    ppermute x2, starting transfers between devices, from_behind(): lax.ppermute(value, axis, [(source, source + steps) for source in range(i...  5.51 us
  transfers between devices with their start and end apart: 9, of which 6 were waited for; matrix products, arithmetic and copies ran while one was open for 0% of the time, Pallas kernels for 4%

profile of v8, /device:TPU:11, one launch (start us, length us, event | category | flops | bytes accessed | tf_op | source)
XLA Modules:
  0.0 218.9 jit_solution(16336844111326726817)
XLA Ops:
  0.6 2.0 share.1
  2.6 1.3 collective-permute-start
  3.9 2.5 %project.3.q_first = bf16[128,512]{1,0:T(8,128)(2,1)S(1)} custom-call(bf16[128,4096]{1,0:T(8,128)(2,1)S(1)} %get-tuple-element.23.source, bf16[4096,2048]{1,0:T(8,128)(2,1)} %weight_hbm.8), custom_call_target="tpu_custom_call" | custom-call | flops 536870912 | bytes 4194304 | tf_op jit(solution)/shard_map/project/pallas_call | solution.py:381
  6.5 0.0 collective-permute-done
  6.5 3.2 %collective-permute-start.2 = (bf16[1,160,128]{2,1,0:T(8,128)(2,1)S(1)}, bf16[1,160,128]{2,1,0:T(8,128)(2,1)S(1)}, u32[]{:S(2)}, u32[]{:S(2)}) collective-permute-start(bf16[1,160,128]{2,1,0:T(8,128)(2,1)S(1)} %pad_maximum_fusion.2), channel_id=1, source_target_pairs={{0,8},{4,12},{8,16},{12,20},{16,24},{20,28},{1,9},{5,13},{9,17},{1... | collective-permute-start | bytes 122888 | tf_op jit(solution)/shard_map/ppermute | solution.py:24
  9.8 2.3 %collective-permute-start.1 = (bf16[1,128,128]{2,1,0:T(8,128)(2,1)S(1)}, bf16[1,128,128]{2,1,0:T(8,128)(2,1)S(1)}, u32[]{:S(2)}, u32[]{:S(2)}) collective-permute-start(bf16[1,128,128]{2,1,0:T(8,128)(2,1)S(1)} %get-tuple-element.18), channel_id=1, source_target_pairs={{0,16},{4,20},{8,24},{12,28},{1,17},{5,21},{9,25},{13,29},{2,18},{... | collective-permute-start | bytes 98312 | tf_op jit(solution)/shard_map/ppermute | solution.py:24
  12.1 4.0 %project.4.q_middle = bf16[128,1024]{1,0:T(8,128)(2,1)S(1)} custom-call(bf16[128,4096]{1,0:T(8,128)(2,1)S(1)} %get-tuple-element.23.source, bf16[4096,2048]{1,0:T(8,128)(2,1)} %weight_hbm.8), custom_call_target="tpu_custom_call" | custom-call | flops 1073741824 | bytes 8388608 | tf_op jit(solution)/shard_map/project/pallas_call | solution.py:381
  16.0 0.0 collective-permute-done.2
  16.1 0.0 collective-permute-done.1
  16.1 0.3 collective-permute-start.3
  16.4 0.0 copy-start.1
  16.4 2.6 %project.5.q_last = bf16[128,512]{1,0:T(8,128)(2,1)S(1)} custom-call(bf16[128,4096]{1,0:T(8,128)(2,1)S(1)} %get-tuple-element.23.source, bf16[4096,2048]{1,0:T(8,128)(2,1)} %weight_hbm.8), custom_call_target="tpu_custom_call" | custom-call | flops 536870912 | bytes 4194304 | tf_op jit(solution)/shard_map/project/pallas_call | solution.py:381
  19.0 0.0 copy-start.2
  19.0 0.7 collective-permute-done.3
  19.8 2.4 %collective-permute-start.4 = (bf16[1,800,128]{2,1,0:T(8,128)(2,1)S(1)}, bf16[1,800,128]{2,1,0:T(8,128)(2,1)S(1)}, u32[]{:S(2)}, u32[]{:S(2)}) collective-permute-start(bf16[1,800,128]{2,1,0:T(8,128)(2,1)S(1)} %constant_dynamic-update-slice_fusion), channel_id=1, source_target_pairs={{0,1},{1,0},{2,3},{3,2},{4,5},{5,4},{6,7},{7,6},{8,9},{9,8},{10,11... | collective-permute-start | bytes 614408 | tf_op jit(solution)/shard_map/ppermute | solution.py:29
  22.3 0.1 pad_add_fusion.place
  22.3 1.0 collective-permute-done.4
  23.5 173.7 %attention.1 = (f32[64,4096]{1,0:T(8,128)S(1)}, bf16[64,4096]{1,0:T(8,128)(2,1)S(1)}) custom-call(s32[2]{0:T(128)S(1)} %pad_add_fusion.place, bf16[128,512]{1,0:T(8,128)(2,1)S(1)} %project.3.q_first, bf16[128,1024]{1,0:T(8,128)(2,1)S(1)} %project.4.q_middle, bf16[128,512]{1,0:T(8,128)(2,1)S(1)} %project.5.q_last, ...), custom_call_target="tpu_custom_call" | custom-call | tf_op jit(solution)/shard_map/attention/pallas_call | solution.py:407
  197.2 0.4 collective-permute-start.5
  197.6 1.5 collective-permute-done.5
  199.1 0.1 convert_add_fusion
  199.3 1.1 collective-permute-start.6
  200.4 6.4 %collective-permute-done.6 = bf16[1,32,4096]{2,1,0:T(8,128)(2,1)S(1)} collective-permute-done((bf16[1,32,4096]{2,1,0:T(8,128)(2,1)S(1)}, bf16[1,32,4096]{2,1,0:T(8,128)(2,1)S(1)}, u32[]{:S(2)}, u32[]{:S(2)}) %collective-permute-start.6) | collective-permute-done | bytes 262176 | tf_op jit(solution)/shard_map/ppermute | solution.py:29
  206.8 0.0 copy-done.1
  206.8 0.2 fusion
  207.1 0.0 copy-start
  207.1 0.0 copy-done.2
  207.1 0.1 fusion.9
  207.2 1.1 collective-permute-start.7
  208.4 5.6 %collective-permute-done.7 = bf16[1,32,4096]{2,1,0:T(8,128)(2,1)S(1)} collective-permute-done((bf16[1,32,4096]{2,1,0:T(8,128)(2,1)S(1)}, bf16[1,32,4096]{2,1,0:T(8,128)(2,1)S(1)}, u32[]{:S(2)}, u32[]{:S(2)}) %collective-permute-start.7) | collective-permute-done | bytes 262176 | tf_op jit(solution)/shard_map/ppermute | solution.py:29
  213.9 0.1 maximum_select_fusion.2
  214.0 2.1 collective-permute-start.8
  216.2 0.1 maximum_select_fusion.1
  216.2 1.5 collective-permute-done.8
  217.7 0.2 maximum_select_fusion
  217.9 1.0 copy.10
  218.9 0.0 copy-done
  (20 shorter events, 0.3 us)
Async XLA Ops:
  2.6 3.9 %collective-permute-start = (bf16[1,128,128]{2,1,0:T(8,128)(2,1)S(1)}, bf16[1,128,128]{2,1,0:T(8,128)(2,1)S(1)}, u32[]{:S(2)}, u32[]{:S(2)}) collective-permute-start(bf16[1,128,128]{2,1,0:T(8,128)(2,1)S(1)} %bitcast.45), channel_id=1, source_target_pairs={{0,2},{1,3},{2,0},{3,1},{4,6},{5,7},{6,4},{7,5},{8,10},{9,11},{10,... | collective-permute-start | bytes 98312 | tf_op jit(solution)/shard_map/ppermute | solution.py:29
  6.5 9.5 %collective-permute-start.2 = (bf16[1,160,128]{2,1,0:T(8,128)(2,1)S(1)}, bf16[1,160,128]{2,1,0:T(8,128)(2,1)S(1)}, u32[]{:S(2)}, u32[]{:S(2)}) collective-permute-start(bf16[1,160,128]{2,1,0:T(8,128)(2,1)S(1)} %pad_maximum_fusion.2), channel_id=1, source_target_pairs={{0,8},{4,12},{8,16},{12,20},{16,24},{20,28},{1,9},{5,13},{9,17},{1... | collective-permute-start | bytes 122888 | tf_op jit(solution)/shard_map/ppermute | solution.py:24
  9.8 6.3 %collective-permute-start.1 = (bf16[1,128,128]{2,1,0:T(8,128)(2,1)S(1)}, bf16[1,128,128]{2,1,0:T(8,128)(2,1)S(1)}, u32[]{:S(2)}, u32[]{:S(2)}) collective-permute-start(bf16[1,128,128]{2,1,0:T(8,128)(2,1)S(1)} %get-tuple-element.18), channel_id=1, source_target_pairs={{0,16},{4,20},{8,24},{12,28},{1,17},{5,21},{9,25},{13,29},{2,18},{... | collective-permute-start | bytes 98312 | tf_op jit(solution)/shard_map/ppermute | solution.py:24
  16.1 3.6 %collective-permute-start.3 = (bf16[1,416,128]{2,1,0:T(8,128)(2,1)S(1)}, bf16[1,416,128]{2,1,0:T(8,128)(2,1)S(1)}, u32[]{:S(2)}, u32[]{:S(2)}) collective-permute-start(bf16[1,416,128]{2,1,0:T(8,128)(2,1)S(1)} %pad_maximum_fusion), channel_id=1, source_target_pairs={{0,4},{4,0},{8,12},{12,8},{16,20},{20,16},{24,28},{28,24},{1,5},{5... | collective-permute-start | bytes 319496 | tf_op jit(solution)/shard_map/ppermute | solution.py:29
  16.4 190.4 %copy-start.1 = (bf16[32,4096]{1,0:T(8,128)(2,1)S(1)}, bf16[32,4096]{1,0:T(8,128)(2,1)}, u32[]{:S(2)}) copy-start(bf16[32,4096]{1,0:T(8,128)(2,1)} %param.10) | copy-start | bytes 786436
  19.0 188.1 %copy-start.2 = (f32[4096]{0:T(1024)S(1)}, f32[4096]{0:T(1024)}, u32[]{:S(2)}) copy-start(f32[4096]{0:T(1024)} %param.11) | copy-start | bytes 49156
  19.8 3.5 %collective-permute-start.4 = (bf16[1,800,128]{2,1,0:T(8,128)(2,1)S(1)}, bf16[1,800,128]{2,1,0:T(8,128)(2,1)S(1)}, u32[]{:S(2)}, u32[]{:S(2)}) collective-permute-start(bf16[1,800,128]{2,1,0:T(8,128)(2,1)S(1)} %constant_dynamic-update-slice_fusion), channel_id=1, source_target_pairs={{0,1},{1,0},{2,3},{3,2},{4,5},{5,4},{6,7},{7,6},{8,9},{9,8},{10,11... | collective-permute-start | bytes 614408 | tf_op jit(solution)/shard_map/ppermute | solution.py:29
  197.2 2.0 collective-permute-start.5
  199.3 7.6 %collective-permute-start.6 = (bf16[1,32,4096]{2,1,0:T(8,128)(2,1)S(1)}, bf16[1,32,4096]{2,1,0:T(8,128)(2,1)S(1)}, u32[]{:S(2)}, u32[]{:S(2)}) collective-permute-start(bf16[1,32,4096]{2,1,0:T(8,128)(2,1)S(1)} %fusion.6), channel_id=1, source_target_pairs={{0,2},{1,3},{2,0},{3,1},{4,6},{5,7},{6,4},{7,5},{8,10},{9,11},{10,... | collective-permute-start | bytes 786440 | tf_op jit(solution)/shard_map/ppermute | solution.py:29
  207.1 11.9 %copy-start = (bf16[32,4096]{1,0:T(8,128)(2,1)}, bf16[32,4096]{1,0:T(8,128)(2,1)S(1)}, u32[]{:S(2)}) copy-start(bf16[32,4096]{1,0:T(8,128)(2,1)S(1)} %get-tuple-element.29) | copy-start | bytes 786436
  207.2 6.7 %collective-permute-start.7 = (bf16[1,32,4096]{2,1,0:T(8,128)(2,1)S(1)}, bf16[1,32,4096]{2,1,0:T(8,128)(2,1)S(1)}, u32[]{:S(2)}, u32[]{:S(2)}) collective-permute-start(bf16[1,32,4096]{2,1,0:T(8,128)(2,1)S(1)} %get-tuple-element.35), channel_id=1, source_target_pairs={{0,2},{1,3},{2,0},{3,1},{4,6},{5,7},{6,4},{7,5},{8,10},{9,11},{10,... | collective-permute-start | bytes 786440 | tf_op jit(solution)/shard_map/ppermute | solution.py:29
  214.0 3.7 %collective-permute-start.8 = (bf16[2,32,4096]{2,1,0:T(8,128)(2,1)S(1)}, bf16[2,32,4096]{2,1,0:T(8,128)(2,1)S(1)}, u32[]{:S(2)}, u32[]{:S(2)}) collective-permute-start(bf16[2,32,4096]{2,1,0:T(8,128)(2,1)S(1)} %maximum_select_fusion.2), channel_id=1, source_target_pairs={{0,1},{1,0},{2,3},{3,2},{4,5},{5,4},{6,7},{7,6},{8,9},{9,8},{10,11... | collective-permute-start | bytes 1572872 | tf_op jit(solution)/shard_map/ppermute | solution.py:29

commit v9 on v8

--- a/solution.py
+++ b/solution.py
@@ -12,7 +12,7 @@
 W1 = 512
 W2 = 32
 GROUP = 32
-SHORT_GROUP = 4
+SHORT_GROUP = 8
 HEADROOM = 60.0
 FLOOR = 2.0 ** -88
 PIECES = 4

time: 219 us -> 219 us (level)
  the two profiles are of different devices: /device:TPU:11 before, /device:TPU:19 now
where the time goes in v9:
time: 219 us
  Pallas kernels  185 us (84%)
  waiting for transfers between devices  16.9 us (8%)
  starting transfers between devices  14.6 us (7%)
    pallas_call x1, Pallas kernels, attention_of(): pl.pallas_call(functools.partial(attention_kernel, count=count), out_shap...  174 us
    ppermute x7, waiting for transfers between devices, swap(): lax.ppermute(value, axis, [(source, source ^ 1 << bit) for source in rang...  16.7 us
    ppermute x7, starting transfers between devices, swap(): lax.ppermute(value, axis, [(source, source ^ 1 << bit) for source in rang...  10.1 us
    pallas_call x3, Pallas kernels, project(): pl.pallas_call(functools.partial(project_kernel, lane=lane), out_shape=ja...  9.09 us
    ppermute x2, starting transfers between devices, from_behind(): lax.ppermute(value, axis, [(source, source + steps) for source in range(i...  4.5 us
  transfers between devices with their start and end apart: 9, of which 7 were waited for; matrix products, arithmetic and copies ran while one was open for 0% of the time, Pallas kernels for 4%

profile of v9, /device:TPU:19, one launch (start us, length us, event | category | flops | bytes accessed | tf_op | source)
XLA Modules:
  0.0 219.3 jit_solution(9402504016625422759)
XLA Ops:
  0.6 2.0 share.1
  2.6 1.3 collective-permute-start
  3.9 2.5 %project.3.q_first = bf16[128,512]{1,0:T(8,128)(2,1)S(1)} custom-call(bf16[128,4096]{1,0:T(8,128)(2,1)S(1)} %get-tuple-element.23.source, bf16[4096,2048]{1,0:T(8,128)(2,1)} %weight_hbm.8), custom_call_target="tpu_custom_call" | custom-call | flops 536870912 | bytes 4194304 | tf_op jit(solution)/shard_map/project/pallas_call | solution.py:381
  6.5 0.0 collective-permute-done
  6.5 3.2 %collective-permute-start.2 = (bf16[1,160,128]{2,1,0:T(8,128)(2,1)S(1)}, bf16[1,160,128]{2,1,0:T(8,128)(2,1)S(1)}, u32[]{:S(2)}, u32[]{:S(2)}) collective-permute-start(bf16[1,160,128]{2,1,0:T(8,128)(2,1)S(1)} %pad_maximum_fusion.2), channel_id=1, source_target_pairs={{0,8},{4,12},{8,16},{12,20},{16,24},{20,28},{1,9},{5,13},{9,17},{1... | collective-permute-start | bytes 122888 | tf_op jit(solution)/shard_map/ppermute | solution.py:24
  9.8 1.3 collective-permute-start.1
  11.1 4.0 %project.4.q_middle = bf16[128,1024]{1,0:T(8,128)(2,1)S(1)} custom-call(bf16[128,4096]{1,0:T(8,128)(2,1)S(1)} %get-tuple-element.23.source, bf16[4096,2048]{1,0:T(8,128)(2,1)} %weight_hbm.8), custom_call_target="tpu_custom_call" | custom-call | flops 1073741824 | bytes 8388608 | tf_op jit(solution)/shard_map/project/pallas_call | solution.py:381
  15.0 0.0 collective-permute-done.2
  15.1 0.3 collective-permute-done.1
  15.3 0.3 collective-permute-start.3
  15.6 0.0 copy-start.1
  15.7 2.6 %project.5.q_last = bf16[128,512]{1,0:T(8,128)(2,1)S(1)} custom-call(bf16[128,4096]{1,0:T(8,128)(2,1)S(1)} %get-tuple-element.23.source, bf16[4096,2048]{1,0:T(8,128)(2,1)} %weight_hbm.8), custom_call_target="tpu_custom_call" | custom-call | flops 536870912 | bytes 4194304 | tf_op jit(solution)/shard_map/project/pallas_call | solution.py:381
  18.2 0.0 copy-start.2
  18.3 0.7 collective-permute-done.3
  19.1 3.6 %collective-permute-start.4 = (bf16[1,800,128]{2,1,0:T(8,128)(2,1)S(1)}, bf16[1,800,128]{2,1,0:T(8,128)(2,1)S(1)}, u32[]{:S(2)}, u32[]{:S(2)}) collective-permute-start(bf16[1,800,128]{2,1,0:T(8,128)(2,1)S(1)} %constant_dynamic-update-slice_fusion), channel_id=1, source_target_pairs={{0,1},{1,0},{2,3},{3,2},{4,5},{5,4},{6,7},{7,6},{8,9},{9,8},{10,11... | collective-permute-start | bytes 614408 | tf_op jit(solution)/shard_map/ppermute | solution.py:29
  22.6 0.1 pad_add_fusion.place
  22.7 1.0 collective-permute-done.4
  23.9 173.7 %attention.1 = (f32[64,4096]{1,0:T(8,128)S(1)}, bf16[64,4096]{1,0:T(8,128)(2,1)S(1)}) custom-call(s32[2]{0:T(128)S(1)} %pad_add_fusion.place, bf16[128,512]{1,0:T(8,128)(2,1)S(1)} %project.3.q_first, bf16[128,1024]{1,0:T(8,128)(2,1)S(1)} %project.4.q_middle, bf16[128,512]{1,0:T(8,128)(2,1)S(1)} %project.5.q_last, ...), custom_call_target="tpu_custom_call" | custom-call | tf_op jit(solution)/shard_map/attention/pallas_call | solution.py:407
  197.5 0.4 collective-permute-start.5
  198.0 1.5 collective-permute-done.5
  199.5 0.1 convert_add_fusion
  199.7 1.1 collective-permute-start.6
  200.8 6.4 %collective-permute-done.6 = bf16[1,32,4096]{2,1,0:T(8,128)(2,1)S(1)} collective-permute-done((bf16[1,32,4096]{2,1,0:T(8,128)(2,1)S(1)}, bf16[1,32,4096]{2,1,0:T(8,128)(2,1)S(1)}, u32[]{:S(2)}, u32[]{:S(2)}) %collective-permute-start.6) | collective-permute-done | bytes 262176 | tf_op jit(solution)/shard_map/ppermute | solution.py:29
  207.2 0.0 copy-done.1
  207.2 0.2 fusion
  207.4 0.0 copy-start
  207.5 0.0 copy-done.2
  207.5 0.1 fusion.9
  207.6 1.1 collective-permute-start.7
  208.7 5.6 %collective-permute-done.7 = bf16[1,32,4096]{2,1,0:T(8,128)(2,1)S(1)} collective-permute-done((bf16[1,32,4096]{2,1,0:T(8,128)(2,1)S(1)}, bf16[1,32,4096]{2,1,0:T(8,128)(2,1)S(1)}, u32[]{:S(2)}, u32[]{:S(2)}) %collective-permute-start.7) | collective-permute-done | bytes 262176 | tf_op jit(solution)/shard_map/ppermute | solution.py:29
  214.3 0.1 maximum_select_fusion.2
  214.4 2.1 collective-permute-start.8
  216.5 0.1 maximum_select_fusion.1
  216.6 1.5 collective-permute-done.8
  218.1 0.2 maximum_select_fusion
  218.3 1.0 copy.10
  219.3 0.0 copy-done
  (20 shorter events, 0.3 us)
Async XLA Ops:
  2.6 3.9 %collective-permute-start = (bf16[1,128,128]{2,1,0:T(8,128)(2,1)S(1)}, bf16[1,128,128]{2,1,0:T(8,128)(2,1)S(1)}, u32[]{:S(2)}, u32[]{:S(2)}) collective-permute-start(bf16[1,128,128]{2,1,0:T(8,128)(2,1)S(1)} %bitcast.45), channel_id=1, source_target_pairs={{0,2},{1,3},{2,0},{3,1},{4,6},{5,7},{6,4},{7,5},{8,10},{9,11},{10,... | collective-permute-start | bytes 98312 | tf_op jit(solution)/shard_map/ppermute | solution.py:29
  6.5 8.5 %collective-permute-start.2 = (bf16[1,160,128]{2,1,0:T(8,128)(2,1)S(1)}, bf16[1,160,128]{2,1,0:T(8,128)(2,1)S(1)}, u32[]{:S(2)}, u32[]{:S(2)}) collective-permute-start(bf16[1,160,128]{2,1,0:T(8,128)(2,1)S(1)} %pad_maximum_fusion.2), channel_id=1, source_target_pairs={{0,8},{4,12},{8,16},{12,20},{16,24},{20,28},{1,9},{5,13},{9,17},{1... | collective-permute-start | bytes 122888 | tf_op jit(solution)/shard_map/ppermute | solution.py:24
  9.8 5.6 %collective-permute-start.1 = (bf16[1,128,128]{2,1,0:T(8,128)(2,1)S(1)}, bf16[1,128,128]{2,1,0:T(8,128)(2,1)S(1)}, u32[]{:S(2)}, u32[]{:S(2)}) collective-permute-start(bf16[1,128,128]{2,1,0:T(8,128)(2,1)S(1)} %get-tuple-element.18), channel_id=1, source_target_pairs={{0,16},{4,20},{8,24},{12,28},{1,17},{5,21},{9,25},{13,29},{2,18},{... | collective-permute-start | bytes 98312 | tf_op jit(solution)/shard_map/ppermute | solution.py:24
  15.3 3.6 %collective-permute-start.3 = (bf16[1,416,128]{2,1,0:T(8,128)(2,1)S(1)}, bf16[1,416,128]{2,1,0:T(8,128)(2,1)S(1)}, u32[]{:S(2)}, u32[]{:S(2)}) collective-permute-start(bf16[1,416,128]{2,1,0:T(8,128)(2,1)S(1)} %pad_maximum_fusion), channel_id=1, source_target_pairs={{0,4},{4,0},{8,12},{12,8},{16,20},{20,16},{24,28},{28,24},{1,5},{5... | collective-permute-start | bytes 319496 | tf_op jit(solution)/shard_map/ppermute | solution.py:29
  15.6 191.6 %copy-start.1 = (bf16[32,4096]{1,0:T(8,128)(2,1)S(1)}, bf16[32,4096]{1,0:T(8,128)(2,1)}, u32[]{:S(2)}) copy-start(bf16[32,4096]{1,0:T(8,128)(2,1)} %param.10) | copy-start | bytes 786436
  18.2 189.2 %copy-start.2 = (f32[4096]{0:T(1024)S(1)}, f32[4096]{0:T(1024)}, u32[]{:S(2)}) copy-start(f32[4096]{0:T(1024)} %param.11) | copy-start | bytes 49156
  19.1 4.7 %collective-permute-start.4 = (bf16[1,800,128]{2,1,0:T(8,128)(2,1)S(1)}, bf16[1,800,128]{2,1,0:T(8,128)(2,1)S(1)}, u32[]{:S(2)}, u32[]{:S(2)}) collective-permute-start(bf16[1,800,128]{2,1,0:T(8,128)(2,1)S(1)} %constant_dynamic-update-slice_fusion), channel_id=1, source_target_pairs={{0,1},{1,0},{2,3},{3,2},{4,5},{5,4},{6,7},{7,6},{8,9},{9,8},{10,11... | collective-permute-start | bytes 614408 | tf_op jit(solution)/shard_map/ppermute | solution.py:29
  197.5 2.0 collective-permute-start.5
  199.7 7.6 %collective-permute-start.6 = (bf16[1,32,4096]{2,1,0:T(8,128)(2,1)S(1)}, bf16[1,32,4096]{2,1,0:T(8,128)(2,1)S(1)}, u32[]{:S(2)}, u32[]{:S(2)}) collective-permute-start(bf16[1,32,4096]{2,1,0:T(8,128)(2,1)S(1)} %fusion.6), channel_id=1, source_target_pairs={{0,2},{1,3},{2,0},{3,1},{4,6},{5,7},{6,4},{7,5},{8,10},{9,11},{10,... | collective-permute-start | bytes 786440 | tf_op jit(solution)/shard_map/ppermute | solution.py:29
  207.4 11.9 %copy-start = (bf16[32,4096]{1,0:T(8,128)(2,1)}, bf16[32,4096]{1,0:T(8,128)(2,1)S(1)}, u32[]{:S(2)}) copy-start(bf16[32,4096]{1,0:T(8,128)(2,1)S(1)} %get-tuple-element.29) | copy-start | bytes 786436
  207.6 6.7 %collective-permute-start.7 = (bf16[1,32,4096]{2,1,0:T(8,128)(2,1)S(1)}, bf16[1,32,4096]{2,1,0:T(8,128)(2,1)S(1)}, u32[]{:S(2)}, u32[]{:S(2)}) collective-permute-start(bf16[1,32,4096]{2,1,0:T(8,128)(2,1)S(1)} %get-tuple-element.35), channel_id=1, source_target_pairs={{0,2},{1,3},{2,0},{3,1},{4,6},{5,7},{6,4},{7,5},{8,10},{9,11},{10,... | collective-permute-start | bytes 786440 | tf_op jit(solution)/shard_map/ppermute | solution.py:29
  214.4 3.7 %collective-permute-start.8 = (bf16[2,32,4096]{2,1,0:T(8,128)(2,1)S(1)}, bf16[2,32,4096]{2,1,0:T(8,128)(2,1)S(1)}, u32[]{:S(2)}, u32[]{:S(2)}) collective-permute-start(bf16[2,32,4096]{2,1,0:T(8,128)(2,1)S(1)} %maximum_select_fusion.2), channel_id=1, source_target_pairs={{0,1},{1,0},{2,3},{3,2},{4,5},{5,4},{6,7},{7,6},{8,9},{9,8},{10,11... | collective-permute-start | bytes 1572872 | tf_op jit(solution)/shard_map/ppermute | solution.py:29
